TPU v7x, 512 devices: a whole 4x8x8 slice. The times are simulated.
512 devices in a mesh: row: 16 (over z, y_hi), col: 32 (over x, y_lo, core).
Axes of the slice: x: 4, y: 8 (y_hi: 2, y_lo: 4; y = y_hi * 4 + y_lo), z: 8, core: 2. Of those that a mesh axis runs over, the one named last changes fastest.
Arguments:
- scalars: float32 [1, 256, 256, 512], P(None, 'row', 'col'), may hold values from -6 to 6
- velocity: bfloat16 [3, 256, 256, 512], P(None, 'row', 'col'), may hold values from -6 to 6
- first_x: bfloat16 [512, 512], replicated, may hold values from -0.25 to 0.25
- second_x: bfloat16 [512, 512], replicated, may hold values from -0.25 to 0.25
- first_y: bfloat16 [256, 256], replicated, may hold values from -0.375 to 0.375
- second_y: bfloat16 [256, 256], replicated, may hold values from -0.375 to 0.375
- first_z: bfloat16 [256, 256], replicated, may hold values from -0.375 to 0.375
- second_z: bfloat16 [256, 256], replicated, may hold values from -0.375 to 0.375
Outputs:
- updated: float32 [1, 256, 256, 512], P(None, 'row', 'col')
All inputs are finite; a program needn't handle non-finite values.
Results may differ from a plain program's by a relative error of at most 0.0021.
Values may be sent and summed in bfloat16 or wider, within the bound.
No kernel may reach another device: no remote copies, remote signals or barrier semaphores. Data moves between devices by JAX's collectives and lax.ppermute only.
A program may use at most 64 MiB of HBM per device.

v0:
```python
import jax
import jax.numpy as jnp
from jax import lax
from jax.sharding import PartitionSpec as P

diffusion_coefficient = 0.5
step_weight = 0.5


def contract_last(scalar_values, matrix):
    return lax.dot_general(
        scalar_values,
        matrix,
        (((scalar_values.ndim - 1,), (1,)), ((), ())),
        preferred_element_type=jnp.float32,
    )


def contract_middle(scalar_values, matrix):
    return jnp.einsum("syc,ky->skc", scalar_values, matrix, preferred_element_type=jnp.float32)


def contract_z(scalar_values, matrix):
    blocks = scalar_values.shape[2]
    depth_z = scalar_values.shape[4]
    shaped = matrix.reshape(matrix.shape[0] // depth_z, depth_z, blocks, depth_z)
    return jnp.einsum(
        "sajxz,JZjz->saJxZ", scalar_values, shaped, preferred_element_type=jnp.float32
    )


def derivative_pair(scalar_values, first_derivative_matrix, second_derivative_matrix, apply_matrix):
    return (
        apply_matrix(scalar_values, first_derivative_matrix),
        apply_matrix(scalar_values, second_derivative_matrix),
    )


def axis_contribution(
    scalar_values, velocity_field, first_derivative_matrix, second_derivative_matrix, apply_matrix
):
    velocity_flux = velocity_field.astype(jnp.float32)
    flux_product = (velocity_flux * scalar_values.astype(jnp.float32)).astype(jnp.bfloat16)
    scalar_gradient, second_derivative = derivative_pair(
        scalar_values, first_derivative_matrix, second_derivative_matrix, apply_matrix
    )
    advected_scalar = apply_matrix(flux_product, first_derivative_matrix)
    return (
        -0.5 * (velocity_flux * scalar_gradient + advected_scalar)
        + diffusion_coefficient * second_derivative
    )


def body(scalars, velocity, first_x, second_x, first_y, second_y, first_z, second_z):
    scalar_count = scalars.shape[0]
    rows_local = scalars.shape[1]
    depth_z = scalars.shape[2]
    length_x = scalars.shape[3]
    compiled_step = scalars.astype(jnp.bfloat16)
    x_term = axis_contribution(compiled_step, velocity[0], first_x, second_x, contract_last)
    outgoing = jnp.concatenate([compiled_step, velocity[1:]], axis=0)
    outgoing = jnp.transpose(outgoing, (0, 1, 3, 2)).reshape(
        scalar_count + 2, rows_local, length_x * depth_z
    )
    pencil_y = lax.all_to_all(outgoing, "row", split_axis=2, concat_axis=1, tiled=True)
    y_term = axis_contribution(
        pencil_y[:scalar_count], pencil_y[scalar_count], first_y, second_y, contract_middle
    )
    onward = jnp.concatenate([pencil_y[:scalar_count], pencil_y[scalar_count + 1 :]], axis=0)
    pencil_z = lax.all_to_all(onward, "col", split_axis=1, concat_axis=2, tiled=True)
    blocks = lax.axis_size("col")
    width_y = pencil_z.shape[1]
    columns = pencil_y.shape[2]
    pencil_z = pencil_z.reshape(scalar_count + 1, width_y, blocks, columns // depth_z, depth_z)
    z_term = axis_contribution(
        pencil_z[:scalar_count], pencil_z[scalar_count], first_z, second_z, contract_z
    )
    z_term = z_term.reshape(scalar_count, width_y, blocks * columns)
    z_lines = lax.all_to_all(z_term, "col", split_axis=2, concat_axis=1, tiled=True)
    y_back_part, z_back_part = (
        lax.all_to_all(y_term, "row", split_axis=1, concat_axis=2, tiled=True),
        lax.all_to_all(z_lines, "row", split_axis=1, concat_axis=2, tiled=True),
    )
    returned = y_back_part + z_back_part
    returned = returned.reshape(scalar_count, rows_local, length_x, depth_z)
    returned = jnp.transpose(returned, (0, 1, 3, 2))
    return scalars + step_weight * (x_term + returned)


def solution(mesh):
    return jax.shard_map(
        body,
        mesh=mesh,
        in_specs=(
            P(None, "row", "col", None),
            P(None, "row", "col", None),
            P(),
            P(),
            P(),
            P(),
            P(),
            P(),
        ),
        out_specs=P(None, "row", "col", None),
        check_vma=False,
    )
```

profile of v0, /device:TPU:1, one launch (start us, length us, event | category | flops | bytes accessed | tf_op | source)
XLA Modules:
  0.0 199.9 jit_solution(11211925408046868918)
XLA Ops:
  0.0 1.0 convert_element_type.74
  1.0 1.0 slice.32
  2.1 3.4 %copy.35 = bf16[3,16,512,8]{1,3,2,0:T(8,128)(2,1)} copy(bf16[3,16,512,8]{2,3,1,0:T(8,128)(2,1)S(1)} %maximum_bitcast_fusion) | data formatting | bytes 786432 | tf_op jit(solution)/shard_map/transpose | solution.py:62
  5.5 6.8 %copy.95 = bf16[3,16,4096]{1,0,2:T(4,128)(2,1)} copy(bf16[3,16,4096]{1,2,0:T(8,128)(2,1)} %bitcast.143) | data formatting | bytes 786432 | tf_op jit(solution)/shard_map/reshape | solution.py:62
  12.3 6.6 %reshape.147 = bf16[16,2,6144]{2,1,0:T(2,128)(2,1)S(1)} reshape(bf16[4096,3,16]{2,1,0:T(4,128)(2,1)} %bitcast.140) | data formatting | bytes 786432
  18.9 29.4 %all_to_all.66 = bf16[16,2,6144]{2,1,0:T(2,128)(2,1)S(1)} all-to-all(bf16[16,2,6144]{2,1,0:T(2,128)(2,1)S(1)} %reshape.147), channel_id=1, replica_groups=mesh['row'=16,'col'=32] {'row'}, dimensions={0} | all-to-all | bytes 786432 | tf_op jit(solution)/shard_map/all_to_all | solution.py:65
  48.3 5.6 %reshape.148 = bf16[4096,3,16]{2,1,0:T(4,128)(2,1)} reshape(bf16[16,2,6144]{2,1,0:T(2,128)(2,1)S(1)} %all_to_all.66) | data formatting | bytes 786432
  53.9 4.2 %copy.71 = bf16[3,16,16,256]{3,2,1,0:T(8,128)(2,1)S(1)} copy(bf16[3,16,16,256]{1,0,3,2:T(4,128)(2,1)} %bitcast.141) | data formatting | bytes 786432 | tf_op jit(solution)/shard_map/all_to_all | solution.py:65
  58.3 1.0 copy.44
  59.2 11.2 %all-to-all-start.2 = ((bf16[2,256,256]{2,0,1:T(2,128)(2,1)}), bf16[2,256,256]{2,0,1:T(2,128)(2,1)S(1)}, u32[]{:S(2)}, u32[]{:S(2)}) async-start(bf16[2,256,256]{2,0,1:T(2,128)(2,1)} %copy.44), calls=%async_computation.2 | async-start | bytes 524288 | tf_op jit(solution)/shard_map/all_to_all | solution.py:70
  70.5 2.5 %reshape.130 = bf16[32,8,32,8]{3,2,1,0:T(8,128)(2,1)S(1)} reshape(bf16[256,256]{1,0:T(8,128)(2,1)S(1)} %copy-done.6) | data formatting | bytes 262144 | tf_op jit(solution)/shard_map/reshape | solution.py:26
  72.9 1.9 copy.49
  74.8 3.4 %reshape.131 = bf16[32,8,32,8]{3,2,1,0:T(8,128)(2,1)S(1)} reshape(bf16[256,256]{1,0:T(8,128)(2,1)} %param.15) | data formatting | bytes 262144 | tf_op jit(solution)/shard_map/reshape | solution.py:26
  78.2 1.9 copy.55
  80.1 0.2 copy.38
  80.2 0.1 copy.40
  80.4 1.3 all-to-all-done.2
  81.8 1.0 copy.47
  82.9 0.4 copy.46
  83.2 1.0 copy.51
  84.2 2.0 fusion.1
  86.2 2.0 fusion.5
  88.2 0.7 fusion.4
  89.0 4.3 %copy.78 = f32[1,8,32,32,8]{1,4,3,2,0:T(8,128)} copy(f32[1,8,32,32,8]{2,3,4,1,0:T(8,128)S(1)} %fusion.4) | data formatting | bytes 524288 | tf_op jit(solution)/shard_map/reshape | solution.py:78
  93.3 0.6 broadcast.21
  93.9 38.4 %reduce = f32[8192,8]{1,0:T(8,128)} reduce(f32[8192,1,8]{2,1,0:T(1,128)} %bitcast.139, f32[]{:T(128)} %broadcast.21), dimensions={1}, to_apply=%bitcast.128.reduce_sub_computation | reduce | bytes 524292
  132.3 4.5 %reshape.149 = f32[32,1,2048]{2,1,0:T(1,128)} reshape(f32[8192,8]{1,0:T(8,128)} %reduce) | data formatting | bytes 524288
  136.9 6.4 %all-to-all-start.3 = ((f32[32,1,2048]{2,1,0:T(1,128)}), f32[32,1,2048]{2,1,0:T(1,128)S(1)}, u32[]{:S(2)}, u32[]{:S(2)}) async-start(f32[32,1,2048]{2,1,0:T(1,128)} %reshape.149), calls=%async_computation.3 | async-start | bytes 524288 | tf_op jit(solution)/shard_map/all_to_all | solution.py:79
  143.3 0.2 fusion.14
  143.5 0.2 fusion.13
  143.8 0.2 fusion.8
  144.0 0.8 copy.41
  144.8 9.7 %all-to-all-done.3 = f32[32,1,2048]{2,1,0:T(1,128)S(1)} async-done(((f32[32,1,2048]{2,1,0:T(1,128)}), f32[32,1,2048]{2,1,0:T(1,128)S(1)}, u32[]{:S(2)}, u32[]{:S(2)}) %all-to-all-start.3) | async-done | bytes 262176 | tf_op jit(solution)/shard_map/all_to_all | solution.py:79
  154.5 3.9 %all-to-all-start.1 = ((f32[1,256,256]{2,0,1:T(1,128)}), f32[1,256,256]{2,0,1:T(1,128)S(1)}, u32[]{:S(2)}, u32[]{:S(2)}) async-start(f32[1,256,256]{2,0,1:T(1,128)} %copy.41), calls=%async_computation.1 | async-start | bytes 524288 | tf_op jit(solution)/shard_map/all_to_all | solution.py:81
  158.4 1.3 reduce.1
  159.8 0.0 copy-start.2
  159.8 8.4 %reshape.150 = f32[8192,1,8]{2,1,0:T(1,128)} reshape(f32[32,2048]{1,0:T(8,128)S(1)} %reduce.1) | data formatting | bytes 524288
  168.1 2.8 %copy.79 = f32[1,8,32,256]{3,2,1,0:T(8,128)S(1)} copy(f32[1,8,32,256]{1,3,2,0:T(8,128)} %bitcast.142) | data formatting | bytes 524288 | tf_op jit(solution)/shard_map/all_to_all | solution.py:79
  171.0 0.2 copy.93
  171.1 1.0 copy.60
  172.1 0.0 all-to-all-done.1
  172.1 11.6 %all-to-all-start.4 = ((f32[1,256,256]{2,0,1:T(1,128)}), f32[1,256,256]{2,0,1:T(1,128)S(1)}, u32[]{:S(2)}, u32[]{:S(2)}) async-start(f32[1,256,256]{2,0,1:T(1,128)} %copy.60), calls=%async_computation.4 | async-start | bytes 524288 | tf_op jit(solution)/shard_map/all_to_all | solution.py:82
  183.7 0.3 convolution_multiply_fusion.2
  184.0 0.3 fusion.9
  184.4 12.0 %all-to-all-done.4 = f32[1,256,256]{2,0,1:T(1,128)S(1)} async-done(((f32[1,256,256]{2,0,1:T(1,128)}), f32[1,256,256]{2,0,1:T(1,128)S(1)}, u32[]{:S(2)}, u32[]{:S(2)}) %all-to-all-start.4) | async-done | bytes 262176 | tf_op jit(solution)/shard_map/all_to_all | solution.py:82
  196.4 0.6 copy.63
  197.0 0.8 copy.64
  197.8 2.1 %fusion.17 = f32[1,16,8,512]{3,2,1,0:T(8,128)} fusion(f32[1,16,8,512]{3,2,1,0:T(8,128)S(1)} %copy-done.1, f32[16,8,512]{2,1,0:T(8,128)S(1)} %fusion.9, bf16[512,512]{1,0:T(8,128)(2,1)} %param.11, f32[1,16,512,8]{2,3,1,0:T(8,128)S(1)} %copy.64, bf16[1,16,8,512]{3,2,1,0:T(8,128)(2,1)S(1)} %convert_element_type.74), kind=kOutput, calls=%fused_computation.26 | convolution fusion | flops 67436544 | bytes 1703936 | tf_op jit(solution)/shard_map/dot_general | solution.py:11
  (24 shorter events, 0.3 us)
Async XLA Ops:
  0.0 183.7 %copy-start = (bf16[512,512]{1,0:T(8,128)(2,1)S(1)}, bf16[512,512]{1,0:T(8,128)(2,1)}, u32[]{:S(2)}) copy-start(bf16[512,512]{1,0:T(8,128)(2,1)} %param.10) | copy-start | bytes 1572868
  53.9 16.6 %copy-start.6 = (bf16[256,256]{1,0:T(8,128)(2,1)S(1)}, bf16[256,256]{1,0:T(8,128)(2,1)}, u32[]{:S(2)}) copy-start(bf16[256,256]{1,0:T(8,128)(2,1)} %param.14) | copy-start | bytes 393220
  59.2 22.5 %all-to-all-start.2 = ((bf16[2,256,256]{2,0,1:T(2,128)(2,1)}), bf16[2,256,256]{2,0,1:T(2,128)(2,1)S(1)}, u32[]{:S(2)}, u32[]{:S(2)}) async-start(bf16[2,256,256]{2,0,1:T(2,128)(2,1)} %copy.44), calls=%async_computation.2 | async-start | bytes 524288 | tf_op jit(solution)/shard_map/all_to_all | solution.py:70
  82.8 5.4 %copy-start.3 = (bf16[32,8,32,8]{2,0,3,1:T(8,128)(2,1)S(1)}, bf16[32,8,32,8]{2,0,3,1:T(8,128)(2,1)}, u32[]{:S(2)}) copy-start(bf16[32,8,32,8]{2,0,3,1:T(8,128)(2,1)} %copy.49) | copy-start | bytes 393220
  84.2 4.0 %copy-start.4 = (bf16[1,8,32,256]{2,3,1,0:T(8,128)(2,1)S(1)}, bf16[1,8,32,256]{2,3,1,0:T(8,128)(2,1)}, u32[]{:S(2)}) copy-start(bf16[1,8,32,256]{2,3,1,0:T(8,128)(2,1)} %copy.51) | copy-start | bytes 393220
  132.3 10.9 %copy-start.5 = (bf16[256,256]{1,0:T(8,128)(2,1)S(1)}, bf16[256,256]{1,0:T(8,128)(2,1)}, u32[]{:S(2)}) copy-start(bf16[256,256]{1,0:T(8,128)(2,1)} %param.12) | copy-start | bytes 393220
  132.3 11.4 %copy-start.7 = (bf16[256,256]{1,0:T(8,128)(2,1)S(1)}, bf16[256,256]{1,0:T(8,128)(2,1)}, u32[]{:S(2)}) copy-start(bf16[256,256]{1,0:T(8,128)(2,1)} %param.13) | copy-start | bytes 393220
  136.9 17.6 %all-to-all-start.3 = ((f32[32,1,2048]{2,1,0:T(1,128)}), f32[32,1,2048]{2,1,0:T(1,128)S(1)}, u32[]{:S(2)}, u32[]{:S(2)}) async-start(f32[32,1,2048]{2,1,0:T(1,128)} %reshape.149), calls=%async_computation.3 | async-start | bytes 524288 | tf_op jit(solution)/shard_map/all_to_all | solution.py:79
  154.5 17.6 %all-to-all-start.1 = ((f32[1,256,256]{2,0,1:T(1,128)}), f32[1,256,256]{2,0,1:T(1,128)S(1)}, u32[]{:S(2)}, u32[]{:S(2)}) async-start(f32[1,256,256]{2,0,1:T(1,128)} %copy.41), calls=%async_computation.1 | async-start | bytes 524288 | tf_op jit(solution)/shard_map/all_to_all | solution.py:81
  159.8 24.0 %copy-start.2 = (bf16[3,16,8,512]{3,2,1,0:T(8,128)(2,1)S(1)}, bf16[3,16,8,512]{3,2,1,0:T(8,128)(2,1)}, u32[]{:S(2)}) copy-start(bf16[3,16,8,512]{3,2,1,0:T(8,128)(2,1)} %param.9) | copy-start | bytes 1179652
  172.1 25.7 %copy-start.1 = (f32[1,16,8,512]{3,2,1,0:T(8,128)S(1)}, f32[1,16,8,512]{3,2,1,0:T(8,128)}, u32[]{:S(2)}) copy-start(f32[1,16,8,512]{3,2,1,0:T(8,128)} %param.8) | copy-start | bytes 786436
  172.1 24.3 %all-to-all-start.4 = ((f32[1,256,256]{2,0,1:T(1,128)}), f32[1,256,256]{2,0,1:T(1,128)S(1)}, u32[]{:S(2)}, u32[]{:S(2)}) async-start(f32[1,256,256]{2,0,1:T(1,128)} %copy.60), calls=%async_computation.4 | async-start | bytes 524288 | tf_op jit(solution)/shard_map/all_to_all | solution.py:82
where the time goes:
time: 202 us; the launch traced here: 200 us
  local copies, waits for them, and re-layouts  65 us (32%)
  other arithmetic  41 us (20%)
  starting transfers between devices  33.1 us (16%)
  blocking collectives  29.4 us (15%)
  waiting for transfers between devices  23.1 us (11%)
  matrix products  8.05 us (4%)
    unnamed x1, other arithmetic  38.4 us
    all_to_all x1, blocking collectives, body(): lax.all_to_all(outgoing, 'row', split_axis=2, concat_axis=1, tiled=True)  29.4 us
    unnamed x21, local copies, waits for them, and re-layouts  25.8 us
    all_to_all x1, waiting for transfers between devices, body(): lax.all_to_all(z_lines, 'row', split_axis=1, concat_axis=2, tiled=True)  12 us
    all_to_all x1, starting transfers between devices, body(): lax.all_to_all(z_lines, 'row', split_axis=1, concat_axis=2, tiled=True)  11.6 us
    all_to_all x1, starting transfers between devices, body(): lax.all_to_all(onward, 'col', split_axis=1, concat_axis=2, tiled=True)  11.2 us
    all_to_all x1, waiting for transfers between devices, body(): lax.all_to_all(z_term, 'col', split_axis=2, concat_axis=1, tiled=True)  9.69 us
    reshape x4, local copies, waits for them, and re-layouts, contract_z(): matrix.reshape(matrix.shape[0] // depth_z, depth_z, blocks, depth_z)  9.6 us
  transfers between devices with their start and end apart: 4, of which 3 were waited for; matrix products, arithmetic and copies ran while one was open for 13% of the time, Pallas kernels for 0%

commit v1 on v0

v1 whole, which is shorter than its diff:
```python
import jax
import jax.numpy as jnp
from jax import lax
from jax.experimental import pallas as pl
from jax.experimental.pallas import tpu as pltpu
from jax.sharding import PartitionSpec as P

LANES = 128
VMEM = pl.BlockSpec(memory_space=pltpu.VMEM)


def call(kernel, out_shape, scratch_shapes=()):
    shapes = out_shape if isinstance(out_shape, list) else [out_shape]
    run = pl.pallas_call(
        kernel,
        out_shape=out_shape,
        out_specs=[VMEM] * len(shapes) if isinstance(out_shape, list) else VMEM,
        scratch_shapes=list(scratch_shapes),
        name=kernel.__name__,
    )
    return run


def pack_kernel(s_ref, v_ref, w_ref, row_ref, col_ref, s32, v32):
    ny, nz, nx = s_ref.shape
    half = nx // 2
    for t in range(nx // LANES):
        h, at = divmod(t * LANES, half)
        lanes = slice(t * LANES, (t + 1) * LANES)
        to = slice(at, at + LANES)
        s = s_ref[:, :, lanes]
        s32[t] = s.reshape(ny * nz, LANES)
        v32[t] = v_ref[:, :, lanes].astype(jnp.float32).reshape(ny * nz, LANES)
        col_ref[:, h, 0, :, to] = s.astype(jnp.bfloat16)
        col_ref[:, h, 1, :, to] = w_ref[:, :, lanes]
        for z in range(nz):
            row_ref[2 * z + h, 0, :, to] = s32[t, pl.ds(z, ny, stride=nz), :].astype(jnp.bfloat16)
            row_ref[2 * z + h, 1, :, to] = v32[t, pl.ds(z, ny, stride=nz), :].astype(jnp.bfloat16)


def dot(a, b):
    return lax.dot_general(a, b, (((1,), (0,)), ((), ())), preferred_element_type=jnp.float32)


def line_kernel(r_ref, first_ref, second_ref, out_ref):
    blocks, _, depth, lanes = r_ref.shape
    s = r_ref[:, 0].reshape(blocks * depth, lanes)
    c = r_ref[:, 1].reshape(blocks * depth, lanes).astype(jnp.float32)
    flux = (c * s.astype(jnp.float32)).astype(jnp.bfloat16)
    first = first_ref[...]
    term = -0.5 * (c * dot(first, s) + dot(first, flux)) + 0.5 * dot(second_ref[...], s)
    out_ref[...] = term.astype(jnp.bfloat16).reshape(blocks, depth, lanes)


def dot_t(a, b):
    return lax.dot_general(a, b, (((1,), (1,)), ((), ())), preferred_element_type=jnp.float32)


def x_kernel(s_ref, u_ref, first_ref, second_ref, out_ref):
    ny, nz, nx = s_ref.shape
    s = s_ref[...].reshape(ny * nz, nx)
    sb = s.astype(jnp.bfloat16)
    u = u_ref[...].astype(jnp.float32).reshape(ny * nz, nx)
    flux = (u * sb.astype(jnp.float32)).astype(jnp.bfloat16)
    first = first_ref[...]
    term = -0.5 * (u * dot_t(sb, first) + dot_t(flux, first)) + 0.5 * dot_t(sb, second_ref[...])
    out_ref[...] = (s + 0.5 * term).reshape(ny, nz, nx)


def final_kernel(base_ref, y_ref, z_ref, out_ref, y32):
    ny, nz, nx = base_ref.shape
    half = nx // 2
    for t in range(nx // LANES):
        h, at = divmod(t * LANES, half)
        lanes = slice(t * LANES, (t + 1) * LANES)
        of = slice(at, at + LANES)
        for z in range(nz):
            y32[t, pl.ds(z, ny, stride=nz), :] = y_ref[2 * z + h, :, of].astype(jnp.float32)
        y = y32[t].reshape(ny, nz, LANES)
        out_ref[:, :, lanes] = base_ref[:, :, lanes] + 0.5 * (y + z_ref[:, h, :, of].astype(jnp.float32))


def body(scalars, velocity, first_x, second_x, first_y, second_y, first_z, second_z):
    _, ny, nz, nx = scalars.shape
    rows, cols = lax.axis_size("row"), lax.axis_size("col")
    half = nx // 2
    s = scalars[0]
    u, v, w = velocity[0], velocity[1], velocity[2]
    bf16, f32 = jnp.bfloat16, jnp.float32
    row_send, col_send = call(
        pack_kernel,
        [jax.ShapeDtypeStruct((rows, 2, ny, half), bf16), jax.ShapeDtypeStruct((ny, 2, 2, nz, half), bf16)],
        [pltpu.VMEM((nx // LANES, ny * nz, LANES), f32)] * 2,
    )(s, v, w)
    col_send = col_send.reshape(cols, 2, nz, half)
    row_in = lax.all_to_all(row_send, "row", split_axis=0, concat_axis=0, tiled=True)
    col_in = lax.all_to_all(col_send, "col", split_axis=0, concat_axis=0, tiled=True)
    base = call(x_kernel, jax.ShapeDtypeStruct((ny, nz, nx), f32))(s, u, first_x, second_x)
    y_term = call(line_kernel, jax.ShapeDtypeStruct((rows, ny, half), bf16))(row_in, first_y, second_y)
    z_term = call(line_kernel, jax.ShapeDtypeStruct((cols, nz, half), bf16))(col_in, first_z, second_z)
    y_back = lax.all_to_all(y_term, "row", split_axis=0, concat_axis=0, tiled=True)
    z_back = lax.all_to_all(z_term, "col", split_axis=0, concat_axis=0, tiled=True)
    out = call(
        final_kernel,
        jax.ShapeDtypeStruct((ny, nz, nx), f32),
        [pltpu.VMEM((nx // LANES, ny * nz, LANES), f32)],
    )(base, y_back, z_back.reshape(ny, 2, nz, half))
    return out[None]


def solution(mesh):
    return jax.shard_map(
        body,
        mesh=mesh,
        in_specs=(
            P(None, "row", "col", None),
            P(None, "row", "col", None),
            P(),
            P(),
            P(),
            P(),
            P(),
            P(),
        ),
        out_specs=P(None, "row", "col", None),
        check_vma=False,
    )
```

time: 202 us -> 86 us (0.43)
  local copies, waits for them, and re-layouts: 65 us -> 3.09 us
  other arithmetic: 41 us -> 0 us
  starting transfers between devices: 33.1 us -> 17.1 us
  Pallas kernels: 0 us -> 10.5 us
  matrix products: 8.05 us -> 0 us
  waiting for transfers between devices: 23.1 us -> 25.5 us
    unnamed x1 -> x0, other arithmetic: 38.4 us -> none
    unnamed x21 -> x6, local copies, waits for them, and re-layouts: 25.8 us -> 1.3 us
    reshape x6 -> x0, local copies, waits for them, and re-layouts: 20.7 us -> none  [the longest x4 9.6 us: contract_z(): matrix.reshape(matrix.shape[0] // depth_z, depth_z, blocks, depth_z)]
    all_to_all x4 -> x3, starting transfers between devices: 33.1 us -> 17.1 us  [the longest x1 9.14 us: body(): lax.all_to_all(col_send, 'col', split_axis=0, concat_axis=0, tiled=True)]
    pallas_call x0 -> x5, Pallas kernels: none -> 10.5 us  [the longest x1 2.72 us: body(): call(x_kernel, jax.ShapeDtypeStruct((ny, nz, nx), f32))]
    all_to_all x5 -> x0, local copies, waits for them, and re-layouts: 8.2 us -> none  [the longest x1 4.22 us: body(): lax.all_to_all(outgoing, 'row', split_axis=2, concat_axis=1, tiled=True)]
    dot_general x9 -> x0, matrix products: 8.05 us -> none  [the longest x3 4.68 us: contract_z(): jnp.einsum('sajxz,JZjz->saJxZ', scalar_values, shaped, preferred_element_...]
    transpose x1 -> x0, local copies, waits for them, and re-layouts: 3.44 us -> none  [body(): jnp.transpose(outgoing, (0, 1, 3, 2))]
  transfers between devices with their start and end apart: 4 -> 3, of which waited for: 3 -> 3; matrix products, arithmetic and copies ran while one was open for 13% -> 0% of each run, Pallas kernels for 0% -> 8%
where the time goes in v1:
time: 86 us; the launch traced here: 85.5 us
  blocking collectives  29.2 us (34%)
  waiting for transfers between devices  25.5 us (30%)
  starting transfers between devices  17.1 us (20%)
  Pallas kernels  10.5 us (12%)
  local copies, waits for them, and re-layouts  3.09 us (4%)
    all_to_all x1, blocking collectives, body(): lax.all_to_all(row_send, 'row', split_axis=0, concat_axis=0, tiled=True)  29.2 us
    all_to_all x1, waiting for transfers between devices, body(): lax.all_to_all(y_term, 'row', split_axis=0, concat_axis=0, tiled=True)  10.2 us
    all_to_all x1, waiting for transfers between devices, body(): lax.all_to_all(col_send, 'col', split_axis=0, concat_axis=0, tiled=True)  9.28 us
    all_to_all x1, starting transfers between devices, body(): lax.all_to_all(col_send, 'col', split_axis=0, concat_axis=0, tiled=True)  9.14 us
    all_to_all x1, waiting for transfers between devices, body(): lax.all_to_all(z_term, 'col', split_axis=0, concat_axis=0, tiled=True)  6.05 us
    all_to_all x1, starting transfers between devices, body(): lax.all_to_all(z_term, 'col', split_axis=0, concat_axis=0, tiled=True)  4.46 us
    all_to_all x1, starting transfers between devices, body(): lax.all_to_all(y_term, 'row', split_axis=0, concat_axis=0, tiled=True)  3.51 us
    pallas_call x1, Pallas kernels, body(): call(x_kernel, jax.ShapeDtypeStruct((ny, nz, nx), f32))  2.72 us
  transfers between devices with their start and end apart: 3, of which 3 were waited for; matrix products, arithmetic and copies ran while one was open for 0% of the time, Pallas kernels for 8%

profile of v1, /device:TPU:1, one launch (start us, length us, event | category | flops | bytes accessed | tf_op | source)
XLA Modules:
  0.0 85.5 jit_solution(16928397004035427029)
XLA Ops:
  0.0 1.8 %slice_bitcast_fusion = (bf16[16,8,512]{2,1,0:T(8,128)(2,1)}, bf16[16,8,512]{2,1,0:T(8,128)(2,1)}, bf16[16,8,512]{2,1,0:T(8,128)(2,1)}) fusion(bf16[3,16,8,512]{3,2,1,0:T(8,128)(2,1)} %param.9), kind=kLoop, calls=%fused_computation | loop fusion | bytes 786432 | tf_op jit(solution)/shard_map/squeeze | solution.py:88
  1.8 2.0 %pack_kernel.1 = (bf16[16,2,16,256]{3,2,1,0:T(8,128)(2,1)}, bf16[16,2,2,8,256]{4,3,2,1,0:T(8,128)(2,1)}) custom-call(f32[16,8,512]{2,1,0:T(8,128)} %bitcast.10, bf16[16,8,512]{2,1,0:T(8,128)(2,1)} %get-tuple-element.11.v_ref, bf16[16,8,512]{2,1,0:T(8,128)(2,1)} %get-tuple-element.9.w_ref), custom_call_target="tpu_custom_call" | custom-call | tf_op jit(solution)/shard_map/pack_kernel/pallas_call | solution.py:90
  3.8 29.2 %all_to_all.20.r_ref = bf16[16,2,16,256]{3,2,1,0:T(8,128)(2,1)} all-to-all(bf16[16,2,16,256]{3,2,1,0:T(8,128)(2,1)} %get-tuple-element.7), channel_id=1, replica_groups=mesh['row'=16,'col'=32] {'row'}, dimensions={0} | all-to-all | bytes 524288 | tf_op jit(solution)/shard_map/all_to_all | solution.py:96
  33.0 9.1 %all-to-all-start.2 = ((bf16[32,2,8,256]{3,2,1,0:T(8,128)(2,1)}), bf16[32,2,8,256]{3,2,1,0:T(8,128)(2,1)S(1)}, u32[]{:S(2)}, u32[]{:S(2)}) async-start(bf16[32,2,8,256]{3,2,1,0:T(8,128)(2,1)} %bitcast.4), calls=%async_computation.2 | async-start | bytes 524288 | tf_op jit(solution)/shard_map/all_to_all | solution.py:97
  42.1 2.0 %line_kernel.2 = bf16[16,16,256]{2,1,0:T(8,128)(2,1)} custom-call(bf16[16,2,16,256]{3,2,1,0:T(8,128)(2,1)} %all_to_all.20.r_ref, bf16[256,256]{1,0:T(8,128)(2,1)} %first_ref.4, bf16[256,256]{1,0:T(8,128)(2,1)} %second_ref.4), custom_call_target="tpu_custom_call" | custom-call | tf_op jit(solution)/shard_map/line_kernel/pallas_call | solution.py:99
  44.1 9.3 %all-to-all-done.2.r_ref = bf16[32,2,8,256]{3,2,1,0:T(8,128)(2,1)S(1)} async-done(((bf16[32,2,8,256]{3,2,1,0:T(8,128)(2,1)}), bf16[32,2,8,256]{3,2,1,0:T(8,128)(2,1)S(1)}, u32[]{:S(2)}, u32[]{:S(2)}) %all-to-all-start.2) | async-done | bytes 262176 | tf_op jit(solution)/shard_map/all_to_all | solution.py:97
  53.4 0.0 copy-start
  53.4 3.5 %all-to-all-start.1 = ((bf16[16,16,256]{2,1,0:T(8,128)(2,1)}), bf16[16,16,256]{2,1,0:T(8,128)(2,1)S(1)}, u32[]{:S(2)}, u32[]{:S(2)}) async-start(bf16[16,16,256]{2,1,0:T(8,128)(2,1)} %line_kernel.2), calls=%async_computation.1 | async-start | bytes 262144 | tf_op jit(solution)/shard_map/all_to_all | solution.py:101
  56.9 0.0 copy-done
  56.9 2.0 %line_kernel.3 = bf16[32,8,256]{2,1,0:T(8,128)(2,1)} custom-call(bf16[32,2,8,256]{3,2,1,0:T(8,128)(2,1)} %copy-done, bf16[256,256]{1,0:T(8,128)(2,1)} %first_ref.5, bf16[256,256]{1,0:T(8,128)(2,1)} %second_ref.5), custom_call_target="tpu_custom_call" | custom-call | tf_op jit(solution)/shard_map/line_kernel/pallas_call | solution.py:100
  58.9 10.2 %all-to-all-done.1.y_ref = bf16[16,16,256]{2,1,0:T(8,128)(2,1)S(1)} async-done(((bf16[16,16,256]{2,1,0:T(8,128)(2,1)}), bf16[16,16,256]{2,1,0:T(8,128)(2,1)S(1)}, u32[]{:S(2)}, u32[]{:S(2)}) %all-to-all-start.1) | async-done | bytes 131104 | tf_op jit(solution)/shard_map/all_to_all | solution.py:101
  69.1 0.0 copy-start.1
  69.1 0.7 copy-done.1
  69.7 4.5 %all-to-all-start.3 = ((bf16[32,8,256]{2,1,0:T(8,128)(2,1)}), bf16[32,8,256]{2,1,0:T(8,128)(2,1)S(1)}, u32[]{:S(2)}, u32[]{:S(2)}) async-start(bf16[32,8,256]{2,1,0:T(8,128)(2,1)} %line_kernel.3), calls=%async_computation.3 | async-start | bytes 262144 | tf_op jit(solution)/shard_map/all_to_all | solution.py:102
  74.2 2.7 %x_kernel.1.base_ref = f32[16,8,512]{2,1,0:T(8,128)} custom-call(f32[16,8,512]{2,1,0:T(8,128)} %bitcast.11, bf16[16,8,512]{2,1,0:T(8,128)(2,1)} %get-tuple-element.10.u_ref, bf16[512,512]{1,0:T(8,128)(2,1)} %first_ref.3, bf16[512,512]{1,0:T(8,128)(2,1)} %second_ref.3), custom_call_target="tpu_custom_call" | custom-call | tf_op jit(solution)/shard_map/x_kernel/pallas_call | solution.py:98
  76.9 6.1 %all-to-all-done.3 = bf16[32,8,256]{2,1,0:T(8,128)(2,1)S(1)} async-done(((bf16[32,8,256]{2,1,0:T(8,128)(2,1)}), bf16[32,8,256]{2,1,0:T(8,128)(2,1)S(1)}, u32[]{:S(2)}, u32[]{:S(2)}) %all-to-all-start.3) | async-done | bytes 131104 | tf_op jit(solution)/shard_map/all_to_all | solution.py:102
  83.0 0.0 copy-start.2
  83.0 0.6 copy-done.2
  83.6 1.8 %final_kernel.1 = f32[16,8,512]{2,1,0:T(8,128)} custom-call(f32[16,8,512]{2,1,0:T(8,128)} %x_kernel.1.base_ref, bf16[16,16,256]{2,1,0:T(8,128)(2,1)} %copy-done.1, bf16[16,2,8,256]{3,2,1,0:T(8,128)(2,1)} %bitcast.12), custom_call_target="tpu_custom_call" | custom-call | tf_op jit(solution)/shard_map/final_kernel/pallas_call | solution.py:103
Async XLA Ops:
  33.0 20.4 %all-to-all-start.2 = ((bf16[32,2,8,256]{3,2,1,0:T(8,128)(2,1)}), bf16[32,2,8,256]{3,2,1,0:T(8,128)(2,1)S(1)}, u32[]{:S(2)}, u32[]{:S(2)}) async-start(bf16[32,2,8,256]{3,2,1,0:T(8,128)(2,1)} %bitcast.4), calls=%async_computation.2 | async-start | bytes 524288 | tf_op jit(solution)/shard_map/all_to_all | solution.py:97
  53.4 3.5 %copy-start = (bf16[32,2,8,256]{3,2,1,0:T(8,128)(2,1)}, bf16[32,2,8,256]{3,2,1,0:T(8,128)(2,1)S(1)}, u32[]{:S(2)}) copy-start(bf16[32,2,8,256]{3,2,1,0:T(8,128)(2,1)S(1)} %all-to-all-done.2.r_ref) | copy-start | bytes 786436
  53.4 15.7 %all-to-all-start.1 = ((bf16[16,16,256]{2,1,0:T(8,128)(2,1)}), bf16[16,16,256]{2,1,0:T(8,128)(2,1)S(1)}, u32[]{:S(2)}, u32[]{:S(2)}) async-start(bf16[16,16,256]{2,1,0:T(8,128)(2,1)} %line_kernel.2), calls=%async_computation.1 | async-start | bytes 262144 | tf_op jit(solution)/shard_map/all_to_all | solution.py:101
  69.1 0.7 copy-start.1
  69.7 13.2 %all-to-all-start.3 = ((bf16[32,8,256]{2,1,0:T(8,128)(2,1)}), bf16[32,8,256]{2,1,0:T(8,128)(2,1)S(1)}, u32[]{:S(2)}, u32[]{:S(2)}) async-start(bf16[32,8,256]{2,1,0:T(8,128)(2,1)} %line_kernel.3), calls=%async_computation.3 | async-start | bytes 262144 | tf_op jit(solution)/shard_map/all_to_all | solution.py:102
  83.0 0.6 copy-start.2

commit v2 on v1

v2 whole, which is shorter than its diff:
```python
import jax
import jax.numpy as jnp
from jax import lax
from jax.experimental import pallas as pl
from jax.experimental.pallas import tpu as pltpu
from jax.sharding import Mesh
from jax.sharding import PartitionSpec as P


LANES = 128
VMEM = pl.BlockSpec(memory_space=pltpu.VMEM)
SMEM = pl.BlockSpec(memory_space=pltpu.SMEM)
BF16, F32 = jnp.bfloat16, jnp.float32


def component(shape, index):
    return pl.BlockSpec((None,) + shape[1:], lambda i: (index,) + (0,) * (len(shape) - 1))


def near(array):
    return pltpu.with_memory_space_constraint(array, pltpu.VMEM)


def dot(a, b, side):
    return lax.dot_general(a, b, (((1,), (side,)), ((), ())), preferred_element_type=F32)


def term_of(s, c, first, second, product):
    flux = (c * s.astype(F32)).astype(BF16)
    return -0.5 * (c * product(first, s) + product(first, flux)) + 0.5 * product(second, s)


def pack_kernel(high_ref, s_ref, v_ref, w_ref, keep_ref, give_ref, col_ref, s32, v32):
    ny, nz, nx = s_ref.shape
    half = nx // 2
    high = high_ref[0]
    for t in range(half // LANES):
        at = slice(t * LANES, (t + 1) * LANES)
        for h in range(2):
            lanes = slice(h * half + t * LANES, h * half + (t + 1) * LANES)
            s = s_ref[:, :, lanes]
            s32[h] = s.reshape(ny * nz, LANES)
            v32[h] = v_ref[:, :, lanes].astype(F32).reshape(ny * nz, LANES)
            col_ref[:, h, 0, :, at] = s.astype(BF16)
            col_ref[:, h, 1, :, at] = w_ref[:, :, lanes]
        for z in range(nz):
            for f, source in enumerate((s32, v32)):
                keep_ref[z, f, :, at] = source[high, pl.ds(z, ny, stride=nz), :].astype(BF16)
                give_ref[z, f, :, at] = source[1 - high, pl.ds(z, ny, stride=nz), :].astype(BF16)


def join_kernel(own_ref, other_ref, out_ref):
    out_ref[:, 0] = own_ref[...]
    out_ref[:, 1] = other_ref[...]


def x_kernel(s_ref, u_ref, first_ref, second_ref, out_ref):
    ny, nz, nx = s_ref.shape
    s = s_ref[...].reshape(ny * nz, nx)
    u = u_ref[...].astype(F32).reshape(ny * nz, nx)
    term = term_of(s.astype(BF16), u, first_ref[...], second_ref[...], lambda m, f: dot(f, m, 1))
    out_ref[...] = (s + 0.5 * term).reshape(ny, nz, nx)


def y_kernel(high_ref, r_ref, first_ref, second_ref, out_ref):
    blocks, _, _, depth, lanes = r_ref.shape
    high = high_ref[0]
    field = []
    for f in range(2):
        parts = [r_ref[:, high, f], r_ref[:, 1 - high, f]]
        field.append(jnp.stack(parts, axis=1).reshape(blocks * 2 * depth, lanes))
    s, c = field
    term = term_of(s, c.astype(F32), first_ref[...], second_ref[...], lambda m, f: dot(m, f, 0))
    term = term.astype(BF16).reshape(blocks, 2, depth, lanes)
    for slot in range(2):
        out_ref[:, high if slot == 0 else 1 - high] = term[:, slot]


def z_kernel(r_ref, first_ref, second_ref, out_ref):
    blocks, _, depth, lanes = r_ref.shape
    s = r_ref[:, 0].reshape(blocks * depth, lanes)
    c = r_ref[:, 1].reshape(blocks * depth, lanes).astype(F32)
    term = term_of(s, c, first_ref[...], second_ref[...], lambda m, f: dot(m, f, 0))
    out_ref[...] = term.astype(BF16).reshape(blocks, depth, lanes)


def final_kernel(high_ref, base_ref, own_ref, other_ref, z_ref, out_ref, y32):
    ny, nz, nx = base_ref.shape
    half = nx // 2
    high = high_ref[0]
    for t in range(half // LANES):
        at = slice(t * LANES, (t + 1) * LANES)
        for z in range(nz):
            y32[high, pl.ds(z, ny, stride=nz), :] = own_ref[z, 0, :, at].astype(F32)
            y32[1 - high, pl.ds(z, ny, stride=nz), :] = other_ref[z, :, at].astype(F32)
        for h in range(2):
            lanes = slice(h * half + t * LANES, h * half + (t + 1) * LANES)
            y = y32[h].reshape(ny, nz, LANES)
            out_ref[:, :, lanes] = base_ref[:, :, lanes] + 0.5 * (y + z_ref[:, h, :, at].astype(F32))


def body(scalars, velocity, first_x, second_x, first_y, second_y, first_z, second_z):
    _, ny, nz, nx = scalars.shape
    half = nx // 2
    blocks = lax.axis_size("z")
    cols = lax.axis_size("x") * lax.axis_size("l") * lax.axis_size("c")
    high = lax.axis_index("h").reshape(1)
    s = scalars[0]
    whole = pl.BlockSpec((ny, nz, nx), lambda i: (0, 0, 0))

    def partner(array):
        return lax.ppermute(array, "h", [(0, 1), (1, 0)])

    def exchange(array, axes):
        return lax.all_to_all(array, axes, split_axis=0, concat_axis=0, tiled=True)

    keep, give, col_send = pl.pallas_call(
        pack_kernel,
        grid=(1,),
        in_specs=[SMEM, whole, component(velocity.shape, 1), component(velocity.shape, 2)],
        out_specs=[VMEM] * 3,
        out_shape=[
            pltpu.VMEM((blocks, 2, ny, half), BF16),
            pltpu.VMEM((blocks, 2, ny, half), BF16),
            pltpu.VMEM((ny, 2, 2, nz, half), BF16),
        ],
        scratch_shapes=[pltpu.VMEM((2, ny * nz, LANES), F32)] * 2,
        name="pack",
    )(high, s, velocity, velocity)
    other = partner(give)
    col_in = exchange(col_send.reshape(cols, 2, nz, half), ("x", "l", "c"))
    row_send = pl.pallas_call(
        join_kernel,
        in_specs=[VMEM] * 2,
        out_specs=VMEM,
        out_shape=pltpu.VMEM((blocks, 2, 2, ny, half), BF16),
        name="join",
    )(near(keep), near(other))
    row_in = exchange(row_send, "z")
    base = pl.pallas_call(
        x_kernel,
        grid=(1,),
        in_specs=[whole, component(velocity.shape, 0), VMEM, VMEM],
        out_specs=VMEM,
        out_shape=pltpu.VMEM((ny, nz, nx), F32),
        name="xmath",
    )(s, velocity, near(first_x), near(second_x))
    z_term = pl.pallas_call(
        z_kernel,
        in_specs=[VMEM] * 3,
        out_specs=VMEM,
        out_shape=pltpu.VMEM((cols, nz, half), BF16),
        name="zmath",
    )(near(col_in), near(first_z), near(second_z))
    y_term = pl.pallas_call(
        y_kernel,
        in_specs=[SMEM, VMEM, VMEM, VMEM],
        out_specs=VMEM,
        out_shape=pltpu.VMEM((blocks, 2, ny, half), BF16),
        name="ymath",
    )(high, near(row_in), near(first_y), near(second_y))
    y_back = exchange(y_term, "z")
    z_back = exchange(z_term, ("x", "l", "c"))
    y_other = partner(y_back[:, 1])
    out = pl.pallas_call(
        final_kernel,
        in_specs=[SMEM] + [VMEM] * 4,
        out_specs=VMEM,
        out_shape=jax.ShapeDtypeStruct((ny, nz, nx), F32),
        scratch_shapes=[pltpu.VMEM((2, ny * nz, LANES), F32)],
        name="last",
    )(high, near(base), near(y_back), near(y_other), near(z_back.reshape(ny, 2, nz, half)))
    return out[None]


def solution(mesh):
    parts = Mesh(mesh.devices.reshape(8, 2, 4, 4, 2), ("z", "h", "x", "l", "c"))
    pencil = P(None, ("z", "h"), ("x", "l", "c"), None)
    return jax.shard_map(
        body,
        mesh=parts,
        in_specs=(pencil, pencil, P(), P(), P(), P(), P(), P()),
        out_specs=pencil,
        check_vma=False,
    )
```

time: 86 us -> 85.9 us (level)
  the two profiles are of different devices: /device:TPU:1 before, /device:TPU:23 now
where the time goes in v2:
time: 85.9 us; the launch traced here: 85.4 us
  starting transfers between devices  32 us (37%)
  waiting for transfers between devices  26.6 us (31%)
  blocking collectives  20.5 us (24%)
  Pallas kernels  6.24 us (7%)
    all_to_all x3, starting transfers between devices, exchange(): return lax.all_to_all(array, axes, split_axis=0, concat_axis=0, tiled=True)  21.5 us
    all_to_all x1, blocking collectives, exchange(): return lax.all_to_all(array, axes, split_axis=0, concat_axis=0, tiled=True)  20.5 us
    all_to_all x3, waiting for transfers between devices, exchange(): return lax.all_to_all(array, axes, split_axis=0, concat_axis=0, tiled=True)  13.7 us
    ppermute x2, waiting for transfers between devices, partner(): return lax.ppermute(array, 'h', [(0, 1), (1, 0)])  12.9 us
    ppermute x2, starting transfers between devices, partner(): return lax.ppermute(array, 'h', [(0, 1), (1, 0)])  10.6 us
    pallas_call x1, Pallas kernels, body(): pl.pallas_call(pack_kernel, grid=(1,), in_specs=[SMEM, whole, component(v...  1.94 us
  transfers between devices with their start and end apart: 5, of which 4 were waited for; matrix products, arithmetic and copies ran while one was open for 0% of the time, Pallas kernels for 4%

profile of v2, /device:TPU:23, one launch (start us, length us, event | category | flops | bytes accessed | tf_op | source)
XLA Modules:
  0.0 85.4 jit_solution(15052549078905803375)
XLA Ops:
  0.0 1.9 %pack.1 = (bf16[8,2,16,256]{3,2,1,0:T(8,128)(2,1)S(1)}, bf16[8,2,16,256]{3,2,1,0:T(8,128)(2,1)S(1)}, bf16[16,2,2,8,256]{4,3,2,1,0:T(8,128)(2,1)}) custom-call(s32[1]{0:T(128)} %bitcast.high_ref, f32[16,8,512]{2,1,0:T(8,128)} %bitcast.10, bf16[3,16,8,512]{3,2,1,0:T(8,128)(2,1)} %w_ref.1, bf16[3,16,8,512]{3,2,1,0:T(8,128)(2,1)} %w_ref.1), custom_call_target="tpu_custom_call" | custom-call | tf_op jit(solution)/shard_map/pack/pallas_call | solution.py:117
  1.9 5.6 %collective-permute-start = (bf16[8,2,16,256]{3,2,1,0:T(8,128)(2,1)S(1)}, bf16[8,2,16,256]{3,2,1,0:T(8,128)(2,1)S(1)}, u32[]{:S(2)}, u32[]{:S(2)}) collective-permute-start(bf16[8,2,16,256]{3,2,1,0:T(8,128)(2,1)S(1)} %get-tuple-element.9), channel_id=1, source_target_pairs={{0,32},{32,0},{1,33},{33,1},{2,34},{34,2},{3,35},{35,3},{4,36},{36... | collective-permute-start | bytes 393224 | tf_op jit(solution)/shard_map/ppermute | solution.py:112
  7.6 8.3 %collective-permute-done.other_ref = bf16[8,2,16,256]{3,2,1,0:T(8,128)(2,1)S(1)} collective-permute-done((bf16[8,2,16,256]{3,2,1,0:T(8,128)(2,1)S(1)}, bf16[8,2,16,256]{3,2,1,0:T(8,128)(2,1)S(1)}, u32[]{:S(2)}, u32[]{:S(2)}) %collective-permute-start) | collective-permute-done | bytes 131104 | tf_op jit(solution)/shard_map/ppermute | solution.py:112
  15.9 20.5 %all_to_all.20.r_ref = bf16[8,2,2,16,256]{4,3,2,1,0:T(8,128)(2,1)S(1)} all-to-all(bf16[8,2,2,16,256]{4,3,2,1,0:T(8,128)(2,1)S(1)} %join.1), channel_id=1, replica_groups=mesh['z'=8,'h'=2,'x'=4,'l'=4,'c'=2] {'z'}, dimensions={0} | all-to-all | bytes 524288 | tf_op jit(solution)/shard_map/all_to_all | solution.py:115
  36.4 0.0 copy-start.4
  36.4 0.0 copy-start.5
  36.4 8.8 %all-to-all-start.2 = ((bf16[32,2,8,256]{3,2,1,0:T(8,128)(2,1)}), bf16[32,2,8,256]{3,2,1,0:T(8,128)(2,1)S(1)}, u32[]{:S(2)}, u32[]{:S(2)}) async-start(bf16[32,2,8,256]{3,2,1,0:T(8,128)(2,1)} %bitcast.3), calls=%async_computation.2 | async-start | bytes 524288 | tf_op jit(solution)/shard_map/all_to_all | solution.py:115
  45.2 0.0 copy-done.4
  45.2 0.0 copy-done.5
  45.2 0.9 %ymath.1 = bf16[8,2,16,256]{3,2,1,0:T(8,128)(2,1)} custom-call(s32[1]{0:T(128)} %bitcast.high_ref, bf16[8,2,2,16,256]{4,3,2,1,0:T(8,128)(2,1)S(1)} %all_to_all.20.r_ref, bf16[256,256]{1,0:T(8,128)(2,1)S(1)} %copy-done.4, bf16[256,256]{1,0:T(8,128)(2,1)S(1)} %copy-done.5), custom_call_target="tpu_custom_call" | custom-call | tf_op jit(solution)/shard_map/ymath/pallas_call | solution.py:155
  46.1 0.0 copy-start.2
  46.1 0.0 copy-start.3
  46.1 6.5 %all-to-all-done.2.r_ref = bf16[32,2,8,256]{3,2,1,0:T(8,128)(2,1)S(1)} async-done(((bf16[32,2,8,256]{3,2,1,0:T(8,128)(2,1)}), bf16[32,2,8,256]{3,2,1,0:T(8,128)(2,1)S(1)}, u32[]{:S(2)}, u32[]{:S(2)}) %all-to-all-start.2) | async-done | bytes 262176 | tf_op jit(solution)/shard_map/all_to_all | solution.py:115
  52.6 0.0 copy-start.1
  52.6 3.5 %all-to-all-start.1 = ((bf16[8,2,16,256]{3,2,1,0:T(8,128)(2,1)}), bf16[8,2,16,256]{3,2,1,0:T(8,128)(2,1)S(1)}, u32[]{:S(2)}, u32[]{:S(2)}) async-start(bf16[8,2,16,256]{3,2,1,0:T(8,128)(2,1)} %ymath.1), calls=%async_computation.1 | async-start | bytes 262144 | tf_op jit(solution)/shard_map/all_to_all | solution.py:115
  56.1 0.0 copy-done.2
  56.1 0.0 copy-done.3
  56.1 0.0 copy-start
  56.2 0.9 %zmath.1 = bf16[32,8,256]{2,1,0:T(8,128)(2,1)} custom-call(bf16[32,2,8,256]{3,2,1,0:T(8,128)(2,1)S(1)} %all-to-all-done.2.r_ref, bf16[256,256]{1,0:T(8,128)(2,1)S(1)} %copy-done.2, bf16[256,256]{1,0:T(8,128)(2,1)S(1)} %copy-done.3), custom_call_target="tpu_custom_call" | custom-call | tf_op jit(solution)/shard_map/zmath/pallas_call | solution.py:148
  57.1 7.2 %all-to-all-done.1.own_ref = bf16[8,2,16,256]{3,2,1,0:T(8,128)(2,1)S(1)} async-done(((bf16[8,2,16,256]{3,2,1,0:T(8,128)(2,1)}), bf16[8,2,16,256]{3,2,1,0:T(8,128)(2,1)S(1)}, u32[]{:S(2)}, u32[]{:S(2)}) %all-to-all-start.1) | async-done | bytes 131104 | tf_op jit(solution)/shard_map/all_to_all | solution.py:115
  64.3 9.2 %all-to-all-start.3 = ((bf16[32,8,256]{2,1,0:T(8,128)(2,1)}), bf16[32,8,256]{2,1,0:T(8,128)(2,1)S(1)}, u32[]{:S(2)}, u32[]{:S(2)}) async-start(bf16[32,8,256]{2,1,0:T(8,128)(2,1)} %zmath.1), calls=%async_computation.3 | async-start | bytes 262144 | tf_op jit(solution)/shard_map/all_to_all | solution.py:115
  73.5 4.9 %collective-permute-start.1 = (bf16[8,16,256]{2,1,0:T(8,128)(2,1)S(1)}, bf16[8,16,256]{2,1,0:T(8,128)(2,1)S(1)}, u32[]{:S(2)}, u32[]{:S(2)}) collective-permute-start(bf16[8,16,256]{2,1,0:T(8,128)(2,1)S(1)} %slice_bitcast_fusion), channel_id=1, source_target_pairs={{0,32},{32,0},{1,33},{33,1},{2,34},{34,2},{3,35},{35,3},{4,36},{36... | collective-permute-start | bytes 196616 | tf_op jit(solution)/shard_map/ppermute | solution.py:112
  78.4 0.0 copy-done.1
  78.4 0.0 copy-done
  78.4 1.6 %xmath.1.base_ref = f32[16,8,512]{2,1,0:T(8,128)S(1)} custom-call(f32[16,8,512]{2,1,0:T(8,128)} %bitcast.11, bf16[3,16,8,512]{3,2,1,0:T(8,128)(2,1)} %w_ref.1, bf16[512,512]{1,0:T(8,128)(2,1)S(1)} %copy-done, bf16[512,512]{1,0:T(8,128)(2,1)S(1)} %copy-done.1), custom_call_target="tpu_custom_call" | custom-call | tf_op jit(solution)/shard_map/xmath/pallas_call | solution.py:140
  80.1 0.0 all-to-all-done.3
  80.1 4.5 %collective-permute-done.1.other_ref = bf16[8,16,256]{2,1,0:T(8,128)(2,1)S(1)} collective-permute-done((bf16[8,16,256]{2,1,0:T(8,128)(2,1)S(1)}, bf16[8,16,256]{2,1,0:T(8,128)(2,1)S(1)}, u32[]{:S(2)}, u32[]{:S(2)}) %collective-permute-start.1) | collective-permute-done | bytes 65568 | tf_op jit(solution)/shard_map/ppermute | solution.py:112
  84.6 0.8 last.1
  (2 shorter events, 0.0 us)
Async XLA Ops:
  1.9 14.0 %collective-permute-start = (bf16[8,2,16,256]{3,2,1,0:T(8,128)(2,1)S(1)}, bf16[8,2,16,256]{3,2,1,0:T(8,128)(2,1)S(1)}, u32[]{:S(2)}, u32[]{:S(2)}) collective-permute-start(bf16[8,2,16,256]{3,2,1,0:T(8,128)(2,1)S(1)} %get-tuple-element.9), channel_id=1, source_target_pairs={{0,32},{32,0},{1,33},{33,1},{2,34},{34,2},{3,35},{35,3},{4,36},{36... | collective-permute-start | bytes 393224 | tf_op jit(solution)/shard_map/ppermute | solution.py:112
  36.4 8.8 %copy-start.4 = (bf16[256,256]{1,0:T(8,128)(2,1)S(1)}, bf16[256,256]{1,0:T(8,128)(2,1)}, u32[]{:S(2)}) copy-start(bf16[256,256]{1,0:T(8,128)(2,1)} %first_ref.4) | copy-start | bytes 393220
  36.4 8.8 %copy-start.5 = (bf16[256,256]{1,0:T(8,128)(2,1)S(1)}, bf16[256,256]{1,0:T(8,128)(2,1)}, u32[]{:S(2)}) copy-start(bf16[256,256]{1,0:T(8,128)(2,1)} %second_ref.4) | copy-start | bytes 393220
  36.4 16.2 %all-to-all-start.2 = ((bf16[32,2,8,256]{3,2,1,0:T(8,128)(2,1)}), bf16[32,2,8,256]{3,2,1,0:T(8,128)(2,1)S(1)}, u32[]{:S(2)}, u32[]{:S(2)}) async-start(bf16[32,2,8,256]{3,2,1,0:T(8,128)(2,1)} %bitcast.3), calls=%async_computation.2 | async-start | bytes 524288 | tf_op jit(solution)/shard_map/all_to_all | solution.py:115
  46.1 10.0 %copy-start.2 = (bf16[256,256]{1,0:T(8,128)(2,1)S(1)}, bf16[256,256]{1,0:T(8,128)(2,1)}, u32[]{:S(2)}) copy-start(bf16[256,256]{1,0:T(8,128)(2,1)} %first_ref.5) | copy-start | bytes 393220
  46.1 10.0 %copy-start.3 = (bf16[256,256]{1,0:T(8,128)(2,1)S(1)}, bf16[256,256]{1,0:T(8,128)(2,1)}, u32[]{:S(2)}) copy-start(bf16[256,256]{1,0:T(8,128)(2,1)} %second_ref.5) | copy-start | bytes 393220
  52.6 25.8 %copy-start.1 = (bf16[512,512]{1,0:T(8,128)(2,1)S(1)}, bf16[512,512]{1,0:T(8,128)(2,1)}, u32[]{:S(2)}) copy-start(bf16[512,512]{1,0:T(8,128)(2,1)} %second_ref.3) | copy-start | bytes 1572868
  52.6 11.7 %all-to-all-start.1 = ((bf16[8,2,16,256]{3,2,1,0:T(8,128)(2,1)}), bf16[8,2,16,256]{3,2,1,0:T(8,128)(2,1)S(1)}, u32[]{:S(2)}, u32[]{:S(2)}) async-start(bf16[8,2,16,256]{3,2,1,0:T(8,128)(2,1)} %ymath.1), calls=%async_computation.1 | async-start | bytes 262144 | tf_op jit(solution)/shard_map/all_to_all | solution.py:115
  56.1 22.3 %copy-start = (bf16[512,512]{1,0:T(8,128)(2,1)S(1)}, bf16[512,512]{1,0:T(8,128)(2,1)}, u32[]{:S(2)}) copy-start(bf16[512,512]{1,0:T(8,128)(2,1)} %first_ref.3) | copy-start | bytes 1572868
  64.3 15.8 %all-to-all-start.3 = ((bf16[32,8,256]{2,1,0:T(8,128)(2,1)}), bf16[32,8,256]{2,1,0:T(8,128)(2,1)S(1)}, u32[]{:S(2)}, u32[]{:S(2)}) async-start(bf16[32,8,256]{2,1,0:T(8,128)(2,1)} %zmath.1), calls=%async_computation.3 | async-start | bytes 262144 | tf_op jit(solution)/shard_map/all_to_all | solution.py:115
  73.5 11.1 %collective-permute-start.1 = (bf16[8,16,256]{2,1,0:T(8,128)(2,1)S(1)}, bf16[8,16,256]{2,1,0:T(8,128)(2,1)S(1)}, u32[]{:S(2)}, u32[]{:S(2)}) collective-permute-start(bf16[8,16,256]{2,1,0:T(8,128)(2,1)S(1)} %slice_bitcast_fusion), channel_id=1, source_target_pairs={{0,32},{32,0},{1,33},{33,1},{2,34},{34,2},{3,35},{35,3},{4,36},{36... | collective-permute-start | bytes 196616 | tf_op jit(solution)/shard_map/ppermute | solution.py:112

commit v3 on v2

v3 whole, which is shorter than its diff:
```python
import jax
import jax.numpy as jnp
from jax import lax
from jax.experimental import pallas as pl
from jax.experimental.pallas import tpu as pltpu
from jax.sharding import Mesh
from jax.sharding import PartitionSpec as P


LANES = 128
VMEM = pl.BlockSpec(memory_space=pltpu.VMEM)
SMEM = pl.BlockSpec(memory_space=pltpu.SMEM)
BF16, F32 = jnp.bfloat16, jnp.float32


def component(shape, index):
    return pl.BlockSpec((None,) + shape[1:], lambda i: (index,) + (0,) * (len(shape) - 1))


def near(array):
    return pltpu.with_memory_space_constraint(array, pltpu.VMEM)


def dot(a, b, side):
    return lax.dot_general(a, b, (((1,), (side,)), ((), ())), preferred_element_type=F32)


def term_of(s, c, first, second, product):
    flux = (c * s.astype(F32)).astype(BF16)
    return -0.5 * (c * product(first, s) + product(first, flux)) + 0.5 * product(second, s)


def pack_kernel(s_ref, v_ref, w_ref, row_ref, col_ref, s32, v32):
    ny, nz, nx = s_ref.shape
    half = nx // 2
    for t in range(nx // LANES):
        h, at = divmod(t * LANES, half)
        lanes = slice(t * LANES, (t + 1) * LANES)
        to = slice(at, at + LANES)
        s = s_ref[:, :, lanes]
        s32[t] = s.reshape(ny * nz, LANES)
        v32[t] = v_ref[:, :, lanes].astype(F32).reshape(ny * nz, LANES)
        col_ref[:, h, 0, :, to] = s.astype(BF16)
        col_ref[:, h, 1, :, to] = w_ref[:, :, lanes]
        for z in range(nz):
            row_ref[z, 0, :, lanes] = s32[t, pl.ds(z, ny, stride=nz), :].astype(BF16)
            row_ref[z, 1, :, lanes] = v32[t, pl.ds(z, ny, stride=nz), :].astype(BF16)


def flux_kernel(r_ref, out_ref):
    s = r_ref[:, 0]
    out_ref[0] = s
    out_ref[1] = (r_ref[:, 1].astype(F32) * s.astype(F32)).astype(BF16)


def x_kernel(s_ref, u_ref, first_ref, second_ref, out_ref):
    ny, nz, nx = s_ref.shape
    s = s_ref[...].reshape(ny * nz, nx)
    u = u_ref[...].astype(F32).reshape(ny * nz, nx)
    term = term_of(s.astype(BF16), u, first_ref[...], second_ref[...], lambda m, f: dot(f, m, 1))
    out_ref[...] = (s + 0.5 * term).reshape(ny, nz, nx)


def y_kernel(high_ref, r_ref, own_ref, other_ref, first_ref, second_ref, out_ref, lines):
    _, blocks, depth, lanes = own_ref.shape
    high = high_ref[0]
    length = 2 * blocks * depth
    lines[:, :, high] = own_ref[...]
    lines[:, :, 1 - high] = other_ref[...]
    s = lines[0].reshape(length, lanes)
    flux = lines[1].reshape(length, lanes)
    first = first_ref[:, high].reshape(blocks * depth, length)
    second = second_ref[:, high].reshape(blocks * depth, length)
    c = r_ref[:, 1].reshape(blocks * depth, lanes).astype(F32)
    term = -0.5 * (c * dot(first, s, 0) + dot(first, flux, 0)) + 0.5 * dot(second, s, 0)
    out_ref[...] = term.astype(BF16).reshape(blocks, depth, lanes)


def z_kernel(r_ref, first_ref, second_ref, out_ref):
    blocks, _, depth, lanes = r_ref.shape
    s = r_ref[:, 0].reshape(blocks * depth, lanes)
    c = r_ref[:, 1].reshape(blocks * depth, lanes).astype(F32)
    term = term_of(s, c, first_ref[...], second_ref[...], lambda m, f: dot(m, f, 0))
    out_ref[...] = term.astype(BF16).reshape(blocks, depth, lanes)


def final_kernel(base_ref, y_ref, z_ref, out_ref, y32):
    ny, nz, nx = base_ref.shape
    half = nx // 2
    for t in range(nx // LANES):
        h, at = divmod(t * LANES, half)
        lanes = slice(t * LANES, (t + 1) * LANES)
        of = slice(at, at + LANES)
        for z in range(nz):
            y32[t, pl.ds(z, ny, stride=nz), :] = y_ref[z, :, lanes].astype(F32)
        y = y32[t].reshape(ny, nz, LANES)
        out_ref[:, :, lanes] = base_ref[:, :, lanes] + 0.5 * (y + z_ref[:, h, :, of].astype(F32))


def body(scalars, velocity, first_x, second_x, first_y, second_y, first_z, second_z):
    _, ny, nz, nx = scalars.shape
    half = nx // 2
    blocks = lax.axis_size("z")
    cols = lax.axis_size("x") * lax.axis_size("l") * lax.axis_size("c")
    high = lax.axis_index("h").reshape(1)
    s = scalars[0]
    whole = pl.BlockSpec((ny, nz, nx), lambda i: (0, 0, 0))

    def partner(array):
        return lax.ppermute(array, "h", [(0, 1), (1, 0)])

    def exchange(array, axes):
        return lax.all_to_all(array, axes, split_axis=0, concat_axis=0, tiled=True)

    def rows_split(matrix):
        return near(matrix.reshape(blocks, 2, ny, matrix.shape[1]))

    row_send, col_send = pl.pallas_call(
        pack_kernel,
        grid=(1,),
        in_specs=[whole, component(velocity.shape, 1), component(velocity.shape, 2)],
        out_specs=[VMEM] * 2,
        out_shape=[pltpu.VMEM((blocks, 2, ny, nx), BF16), pltpu.VMEM((ny, 2, 2, nz, half), BF16)],
        scratch_shapes=[pltpu.VMEM((nx // LANES, ny * nz, LANES), F32)] * 2,
        name="pack",
    )(s, velocity, velocity)
    row_in = near(exchange(row_send, "z"))
    col_in = exchange(col_send.reshape(cols, 2, nz, half), ("x", "l", "c"))
    own = pl.pallas_call(
        flux_kernel,
        in_specs=[VMEM],
        out_specs=VMEM,
        out_shape=pltpu.VMEM((2, blocks, ny, nx), BF16),
        name="flux",
    )(row_in)
    other = partner(own)
    base = pl.pallas_call(
        x_kernel,
        grid=(1,),
        in_specs=[whole, component(velocity.shape, 0), VMEM, VMEM],
        out_specs=VMEM,
        out_shape=pltpu.VMEM((ny, nz, nx), F32),
        name="xmath",
    )(s, velocity, near(first_x), near(second_x))
    z_term = pl.pallas_call(
        z_kernel,
        in_specs=[VMEM] * 3,
        out_specs=VMEM,
        out_shape=pltpu.VMEM((cols, nz, half), BF16),
        name="zmath",
    )(near(col_in), near(first_z), near(second_z))
    z_back = exchange(z_term, ("x", "l", "c"))
    y_term = pl.pallas_call(
        y_kernel,
        in_specs=[SMEM] + [VMEM] * 5,
        out_specs=VMEM,
        out_shape=pltpu.VMEM((blocks, ny, nx), BF16),
        scratch_shapes=[pltpu.VMEM((2, blocks, 2, ny, nx), BF16)],
        name="ymath",
    )(high, row_in, near(own), near(other), rows_split(first_y), rows_split(second_y))
    y_back = exchange(y_term, "z")
    out = pl.pallas_call(
        final_kernel,
        in_specs=[VMEM] * 3,
        out_specs=VMEM,
        out_shape=jax.ShapeDtypeStruct((ny, nz, nx), F32),
        scratch_shapes=[pltpu.VMEM((nx // LANES, ny * nz, LANES), F32)],
        name="last",
    )(near(base), near(y_back), near(z_back.reshape(ny, 2, nz, half)))
    return out[None]


def solution(mesh):
    parts = Mesh(mesh.devices.reshape(8, 2, 4, 4, 2), ("z", "h", "x", "l", "c"))
    pencil = P(None, ("z", "h"), ("x", "l", "c"), None)
    return jax.shard_map(
        body,
        mesh=parts,
        in_specs=(pencil, pencil, P(), P(), P(), P(), P(), P()),
        out_specs=pencil,
        check_vma=False,
    )
```

time: 85.9 us -> 76.3 us (0.89)
  the two profiles are of different devices: /device:TPU:23 before, /device:TPU:1 now
where the time goes in v3:
time: 76.3 us; the launch traced here: 75.8 us
  starting transfers between devices  27.5 us (36%)
  blocking collectives  21.1 us (28%)
  waiting for transfers between devices  20.7 us (27%)
  Pallas kernels  6.29 us (8%)
    all_to_all x3, starting transfers between devices, exchange(): return lax.all_to_all(array, axes, split_axis=0, concat_axis=0, tiled=True)  22.6 us
    all_to_all x1, blocking collectives, exchange(): return lax.all_to_all(array, axes, split_axis=0, concat_axis=0, tiled=True)  21.1 us
    all_to_all x3, waiting for transfers between devices, exchange(): return lax.all_to_all(array, axes, split_axis=0, concat_axis=0, tiled=True)  20.7 us
    ppermute x1, starting transfers between devices, partner(): return lax.ppermute(array, 'h', [(0, 1), (1, 0)])  4.89 us
    pallas_call x1, Pallas kernels, body(): pl.pallas_call(pack_kernel, grid=(1,), in_specs=[whole, component(velocit...  1.93 us
    pallas_call x1, Pallas kernels, body(): pl.pallas_call(x_kernel, grid=(1,), in_specs=[whole, component(velocity.s...  1.64 us
  transfers between devices with their start and end apart: 4, of which 3 were waited for; matrix products, arithmetic and copies ran while one was open for 0% of the time, Pallas kernels for 5%

profile of v3, /device:TPU:1, one launch (start us, length us, event | category | flops | bytes accessed | tf_op | source)
XLA Modules:
  0.0 75.8 jit_solution(14042030815436945806)
XLA Ops:
  0.0 1.9 %pack.1 = (bf16[8,2,16,512]{3,2,1,0:T(8,128)(2,1)S(1)}, bf16[16,2,2,8,256]{4,3,2,1,0:T(8,128)(2,1)}) custom-call(f32[16,8,512]{2,1,0:T(8,128)} %bitcast.10, bf16[3,16,8,512]{3,2,1,0:T(8,128)(2,1)} %w_ref.1, bf16[3,16,8,512]{3,2,1,0:T(8,128)(2,1)} %w_ref.1), custom_call_target="tpu_custom_call" | custom-call | tf_op jit(solution)/shard_map/pack/pallas_call | solution.py:118
  1.9 21.1 %all_to_all.20.r_ref = bf16[8,2,16,512]{3,2,1,0:T(8,128)(2,1)S(1)} all-to-all(bf16[8,2,16,512]{3,2,1,0:T(8,128)(2,1)S(1)} %get-tuple-element.7), channel_id=1, replica_groups=mesh['z'=8,'h'=2,'x'=4,'l'=4,'c'=2] {'z'}, dimensions={0} | all-to-all | bytes 524288 | tf_op jit(solution)/shard_map/all_to_all | solution.py:113
  23.1 9.8 %all-to-all-start.2 = ((bf16[32,2,8,256]{3,2,1,0:T(8,128)(2,1)}), bf16[32,2,8,256]{3,2,1,0:T(8,128)(2,1)S(1)}, u32[]{:S(2)}, u32[]{:S(2)}) async-start(bf16[32,2,8,256]{3,2,1,0:T(8,128)(2,1)} %bitcast.4), calls=%async_computation.2 | async-start | bytes 524288 | tf_op jit(solution)/shard_map/all_to_all | solution.py:113
  32.9 0.0 copy-start.2
  32.9 0.0 copy-start.3
  33.0 4.9 %collective-permute-start = (bf16[2,8,16,512]{3,2,1,0:T(8,128)(2,1)S(1)}, bf16[2,8,16,512]{3,2,1,0:T(8,128)(2,1)S(1)}, u32[]{:S(2)}, u32[]{:S(2)}) collective-permute-start(bf16[2,8,16,512]{3,2,1,0:T(8,128)(2,1)S(1)} %flux.1.own_ref), channel_id=1, source_target_pairs={{0,32},{32,0},{1,33},{33,1},{2,34},{34,2},{3,35},{35,3},{4,36},{36... | collective-permute-start | bytes 786440 | tf_op jit(solution)/shard_map/ppermute | solution.py:110
  37.9 6.6 %all-to-all-done.2.r_ref = bf16[32,2,8,256]{3,2,1,0:T(8,128)(2,1)S(1)} async-done(((bf16[32,2,8,256]{3,2,1,0:T(8,128)(2,1)}), bf16[32,2,8,256]{3,2,1,0:T(8,128)(2,1)S(1)}, u32[]{:S(2)}, u32[]{:S(2)}) %all-to-all-start.2) | async-done | bytes 262176 | tf_op jit(solution)/shard_map/all_to_all | solution.py:113
  44.5 0.0 copy-done.2
  44.5 0.0 copy-done.3
  44.5 0.9 %zmath.1 = bf16[32,8,256]{2,1,0:T(8,128)(2,1)} custom-call(bf16[32,2,8,256]{3,2,1,0:T(8,128)(2,1)S(1)} %all-to-all-done.2.r_ref, bf16[256,256]{1,0:T(8,128)(2,1)S(1)} %copy-done.2, bf16[256,256]{1,0:T(8,128)(2,1)S(1)} %copy-done.3), custom_call_target="tpu_custom_call" | custom-call | tf_op jit(solution)/shard_map/zmath/pallas_call | solution.py:145
  45.4 0.0 copy-start.4
  45.4 0.0 copy-start.5
  45.4 9.4 %all-to-all-start.3 = ((bf16[32,8,256]{2,1,0:T(8,128)(2,1)}), bf16[32,8,256]{2,1,0:T(8,128)(2,1)S(1)}, u32[]{:S(2)}, u32[]{:S(2)}) async-start(bf16[32,8,256]{2,1,0:T(8,128)(2,1)} %zmath.1), calls=%async_computation.3 | async-start | bytes 262144 | tf_op jit(solution)/shard_map/all_to_all | solution.py:113
  54.8 0.0 collective-permute-done.other_ref
  54.8 0.0 copy-done.4
  54.9 0.0 copy-done.5
  54.9 0.0 copy-start
  54.9 0.0 copy-start.1
  54.9 1.0 %ymath.1 = bf16[8,16,512]{2,1,0:T(8,128)(2,1)} custom-call(s32[1]{0:T(128)} %bitcast.1.high_ref, bf16[8,2,16,512]{3,2,1,0:T(8,128)(2,1)S(1)} %all_to_all.20.r_ref, bf16[2,8,16,512]{3,2,1,0:T(8,128)(2,1)S(1)} %flux.1.own_ref, bf16[2,8,16,512]{3,2,1,0:T(8,128)(2,1)S(1)} %collective-permute-done.other_ref, bf16[8,2,16,256]{3,2,1,0:T(8,128)(2,1)S(1)} %bitcast.8, ...), custom_call_target="tpu_custom_call" | custom-call | tf_op jit(solution)/shard_map/ymath/pallas_call | solution.py:153
  55.9 7.7 %all-to-all-done.3 = bf16[32,8,256]{2,1,0:T(8,128)(2,1)S(1)} async-done(((bf16[32,8,256]{2,1,0:T(8,128)(2,1)}), bf16[32,8,256]{2,1,0:T(8,128)(2,1)S(1)}, u32[]{:S(2)}, u32[]{:S(2)}) %all-to-all-start.3) | async-done | bytes 131104 | tf_op jit(solution)/shard_map/all_to_all | solution.py:113
  63.5 3.4 %all-to-all-start.1 = ((bf16[8,16,512]{2,1,0:T(8,128)(2,1)}), bf16[8,16,512]{2,1,0:T(8,128)(2,1)S(1)}, u32[]{:S(2)}, u32[]{:S(2)}) async-start(bf16[8,16,512]{2,1,0:T(8,128)(2,1)} %ymath.1), calls=%async_computation.1 | async-start | bytes 262144 | tf_op jit(solution)/shard_map/all_to_all | solution.py:113
  66.9 0.0 copy-done
  66.9 0.0 copy-done.1
  66.9 1.6 %xmath.1.base_ref = f32[16,8,512]{2,1,0:T(8,128)S(1)} custom-call(f32[16,8,512]{2,1,0:T(8,128)} %bitcast.11, bf16[3,16,8,512]{3,2,1,0:T(8,128)(2,1)} %w_ref.1, bf16[512,512]{1,0:T(8,128)(2,1)S(1)} %copy-done, bf16[512,512]{1,0:T(8,128)(2,1)S(1)} %copy-done.1), custom_call_target="tpu_custom_call" | custom-call | tf_op jit(solution)/shard_map/xmath/pallas_call | solution.py:137
  68.6 6.5 %all-to-all-done.1.y_ref = bf16[8,16,512]{2,1,0:T(8,128)(2,1)S(1)} async-done(((bf16[8,16,512]{2,1,0:T(8,128)(2,1)}), bf16[8,16,512]{2,1,0:T(8,128)(2,1)S(1)}, u32[]{:S(2)}, u32[]{:S(2)}) %all-to-all-start.1) | async-done | bytes 131104 | tf_op jit(solution)/shard_map/all_to_all | solution.py:113
  75.0 0.8 %last.1 = f32[16,8,512]{2,1,0:T(8,128)} custom-call(f32[16,8,512]{2,1,0:T(8,128)S(1)} %xmath.1.base_ref, bf16[8,16,512]{2,1,0:T(8,128)(2,1)S(1)} %all-to-all-done.1.y_ref, bf16[16,2,8,256]{3,2,1,0:T(8,128)(2,1)S(1)} %bitcast.7), custom_call_target="tpu_custom_call" | custom-call | tf_op jit(solution)/shard_map/last/pallas_call | solution.py:162
  (1 shorter events, 0.0 us)
Async XLA Ops:
  23.1 21.4 %all-to-all-start.2 = ((bf16[32,2,8,256]{3,2,1,0:T(8,128)(2,1)}), bf16[32,2,8,256]{3,2,1,0:T(8,128)(2,1)S(1)}, u32[]{:S(2)}, u32[]{:S(2)}) async-start(bf16[32,2,8,256]{3,2,1,0:T(8,128)(2,1)} %bitcast.4), calls=%async_computation.2 | async-start | bytes 524288 | tf_op jit(solution)/shard_map/all_to_all | solution.py:113
  32.9 11.5 %copy-start.2 = (bf16[256,256]{1,0:T(8,128)(2,1)S(1)}, bf16[256,256]{1,0:T(8,128)(2,1)}, u32[]{:S(2)}) copy-start(bf16[256,256]{1,0:T(8,128)(2,1)} %first_ref.3) | copy-start | bytes 393220
  32.9 11.5 %copy-start.3 = (bf16[256,256]{1,0:T(8,128)(2,1)S(1)}, bf16[256,256]{1,0:T(8,128)(2,1)}, u32[]{:S(2)}) copy-start(bf16[256,256]{1,0:T(8,128)(2,1)} %second_ref.3) | copy-start | bytes 393220
  33.0 21.9 %collective-permute-start = (bf16[2,8,16,512]{3,2,1,0:T(8,128)(2,1)S(1)}, bf16[2,8,16,512]{3,2,1,0:T(8,128)(2,1)S(1)}, u32[]{:S(2)}, u32[]{:S(2)}) collective-permute-start(bf16[2,8,16,512]{3,2,1,0:T(8,128)(2,1)S(1)} %flux.1.own_ref), channel_id=1, source_target_pairs={{0,32},{32,0},{1,33},{33,1},{2,34},{34,2},{3,35},{35,3},{4,36},{36... | collective-permute-start | bytes 786440 | tf_op jit(solution)/shard_map/ppermute | solution.py:110
  45.4 9.5 %copy-start.4 = (bf16[256,256]{1,0:T(8,128)(2,1)S(1)}, bf16[256,256]{1,0:T(8,128)(2,1)}, u32[]{:S(2)}) copy-start(bf16[256,256]{1,0:T(8,128)(2,1)} %param.12) | copy-start | bytes 393220
  45.4 9.5 %copy-start.5 = (bf16[256,256]{1,0:T(8,128)(2,1)S(1)}, bf16[256,256]{1,0:T(8,128)(2,1)}, u32[]{:S(2)}) copy-start(bf16[256,256]{1,0:T(8,128)(2,1)} %param.13) | copy-start | bytes 393220
  45.4 18.1 %all-to-all-start.3 = ((bf16[32,8,256]{2,1,0:T(8,128)(2,1)}), bf16[32,8,256]{2,1,0:T(8,128)(2,1)S(1)}, u32[]{:S(2)}, u32[]{:S(2)}) async-start(bf16[32,8,256]{2,1,0:T(8,128)(2,1)} %zmath.1), calls=%async_computation.3 | async-start | bytes 262144 | tf_op jit(solution)/shard_map/all_to_all | solution.py:113
  54.9 12.0 %copy-start = (bf16[512,512]{1,0:T(8,128)(2,1)S(1)}, bf16[512,512]{1,0:T(8,128)(2,1)}, u32[]{:S(2)}) copy-start(bf16[512,512]{1,0:T(8,128)(2,1)} %first_ref.2) | copy-start | bytes 1572868
  54.9 12.0 %copy-start.1 = (bf16[512,512]{1,0:T(8,128)(2,1)S(1)}, bf16[512,512]{1,0:T(8,128)(2,1)}, u32[]{:S(2)}) copy-start(bf16[512,512]{1,0:T(8,128)(2,1)} %second_ref.2) | copy-start | bytes 1572868
  63.5 11.5 %all-to-all-start.1 = ((bf16[8,16,512]{2,1,0:T(8,128)(2,1)}), bf16[8,16,512]{2,1,0:T(8,128)(2,1)S(1)}, u32[]{:S(2)}, u32[]{:S(2)}) async-start(bf16[8,16,512]{2,1,0:T(8,128)(2,1)} %ymath.1), calls=%async_computation.1 | async-start | bytes 262144 | tf_op jit(solution)/shard_map/all_to_all | solution.py:113

commit v4 on v3

--- a/solution.py
+++ b/solution.py
@@ -30,21 +30,31 @@
     return -0.5 * (c * product(first, s) + product(first, flux)) + 0.5 * product(second, s)
 
 
-def pack_kernel(s_ref, v_ref, w_ref, row_ref, col_ref, s32, v32):
+def pack_kernel(low_ref, s_ref, v_ref, w_ref, row_ref, *rest):
+    pieces, (s32, v32) = rest[:-2], rest[-2:]
     ny, nz, nx = s_ref.shape
     half = nx // 2
+    group = ny // len(pieces)
+    low = low_ref[0]
+    for j, piece in enumerate(pieces):
+        for q in range(group):
+            y = (low ^ j) * group + q
+            for h in range(2):
+                lanes = slice(h * half, (h + 1) * half)
+                piece[2 * q + h, 0] = s_ref[y, :, lanes].astype(BF16)
+                piece[2 * q + h, 1] = w_ref[y, :, lanes]
     for t in range(nx // LANES):
-        h, at = divmod(t * LANES, half)
         lanes = slice(t * LANES, (t + 1) * LANES)
-        to = slice(at, at + LANES)
-        s = s_ref[:, :, lanes]
-        s32[t] = s.reshape(ny * nz, LANES)
+        s32[t] = s_ref[:, :, lanes].reshape(ny * nz, LANES)
         v32[t] = v_ref[:, :, lanes].astype(F32).reshape(ny * nz, LANES)
-        col_ref[:, h, 0, :, to] = s.astype(BF16)
-        col_ref[:, h, 1, :, to] = w_ref[:, :, lanes]
         for z in range(nz):
             row_ref[z, 0, :, lanes] = s32[t, pl.ds(z, ny, stride=nz), :].astype(BF16)
             row_ref[z, 1, :, lanes] = v32[t, pl.ds(z, ny, stride=nz), :].astype(BF16)
+
+
+def join_kernel(*refs):
+    for j, piece in enumerate(refs[:-1]):
+        refs[-1][:, j] = piece[...]
 
 
 def flux_kernel(r_ref, out_ref):
@@ -76,38 +86,57 @@
     out_ref[...] = term.astype(BF16).reshape(blocks, depth, lanes)
 
 
-def z_kernel(r_ref, first_ref, second_ref, out_ref):
-    blocks, _, depth, lanes = r_ref.shape
-    s = r_ref[:, 0].reshape(blocks * depth, lanes)
-    c = r_ref[:, 1].reshape(blocks * depth, lanes).astype(F32)
+def z_kernel(low_ref, r_ref, first_ref, second_ref, out_ref, lines, terms):
+    _, nx_blocks, lows, cores, depth, lanes = lines.shape
+    low = low_ref[0]
+    length = nx_blocks * lows * cores * depth
+    for f in range(2):
+        for x in range(nx_blocks):
+            for j in range(lows):
+                for c in range(cores):
+                    lines[f, x, low ^ j, c] = r_ref[x * cores + c, j, f]
+    s = lines[0].reshape(length, lanes)
+    c = lines[1].reshape(length, lanes).astype(F32)
     term = term_of(s, c, first_ref[...], second_ref[...], lambda m, f: dot(m, f, 0))
-    out_ref[...] = term.astype(BF16).reshape(blocks, depth, lanes)
-
-
-def final_kernel(base_ref, y_ref, z_ref, out_ref, y32):
+    terms[...] = term.astype(BF16).reshape(terms.shape)
+    for x in range(nx_blocks):
+        for j in range(lows):
+            for c in range(cores):
+                out_ref[x * cores + c, j] = terms[x, low ^ j, c]
+
+
+def final_kernel(low_ref, base_ref, y_ref, own_ref, *rest):
+    others, (out_ref, y32) = rest[:-2], rest[-2:]
     ny, nz, nx = base_ref.shape
     half = nx // 2
+    group = ny // (1 + len(others))
+    low = low_ref[0]
     for t in range(nx // LANES):
         h, at = divmod(t * LANES, half)
         lanes = slice(t * LANES, (t + 1) * LANES)
         of = slice(at, at + LANES)
         for z in range(nz):
             y32[t, pl.ds(z, ny, stride=nz), :] = y_ref[z, :, lanes].astype(F32)
-        y = y32[t].reshape(ny, nz, LANES)
-        out_ref[:, :, lanes] = base_ref[:, :, lanes] + 0.5 * (y + z_ref[:, h, :, of].astype(F32))
+        for j in range(1 + len(others)):
+            for q in range(group):
+                y = (low ^ j) * group + q
+                z_term = others[j - 1][2 * q + h, :, of] if j else own_ref[2 * q + h, 0, :, of]
+                y_term = y32[t, pl.ds(pl.multiple_of(y * nz, nz), nz), :]
+                out_ref[y, :, lanes] = base_ref[y, :, lanes] + 0.5 * (y_term + z_term.astype(F32))
 
 
 def body(scalars, velocity, first_x, second_x, first_y, second_y, first_z, second_z):
     _, ny, nz, nx = scalars.shape
     half = nx // 2
-    blocks = lax.axis_size("z")
-    cols = lax.axis_size("x") * lax.axis_size("l") * lax.axis_size("c")
+    blocks, lows, cores = lax.axis_size("z"), lax.axis_size("l"), lax.axis_size("c")
+    peers = lax.axis_size("x") * cores
     high = lax.axis_index("h").reshape(1)
+    low = lax.axis_index("l").reshape(1)
     s = scalars[0]
     whole = pl.BlockSpec((ny, nz, nx), lambda i: (0, 0, 0))
 
-    def partner(array):
-        return lax.ppermute(array, "h", [(0, 1), (1, 0)])
+    def swap(array, axis, j):
+        return lax.ppermute(array, axis, [(i, i ^ j) for i in range(lax.axis_size(axis))])
 
     def exchange(array, axes):
         return lax.all_to_all(array, axes, split_axis=0, concat_axis=0, tiled=True)
@@ -115,17 +144,27 @@
     def rows_split(matrix):
         return near(matrix.reshape(blocks, 2, ny, matrix.shape[1]))
 
-    row_send, col_send = pl.pallas_call(
+    row_send, keep, *give = pl.pallas_call(
         pack_kernel,
         grid=(1,),
-        in_specs=[whole, component(velocity.shape, 1), component(velocity.shape, 2)],
-        out_specs=[VMEM] * 2,
-        out_shape=[pltpu.VMEM((blocks, 2, ny, nx), BF16), pltpu.VMEM((ny, 2, 2, nz, half), BF16)],
+        in_specs=[SMEM, whole, component(velocity.shape, 1), component(velocity.shape, 2)],
+        out_specs=[VMEM] * (1 + lows),
+        out_shape=[pltpu.VMEM((blocks, 2, ny, nx), BF16)] + [pltpu.VMEM((peers, 2, nz, half), BF16)] * lows,
         scratch_shapes=[pltpu.VMEM((nx // LANES, ny * nz, LANES), F32)] * 2,
         name="pack",
-    )(s, velocity, velocity)
+    )(low, s, velocity, velocity)
     row_in = near(exchange(row_send, "z"))
-    col_in = exchange(col_send.reshape(cols, 2, nz, half), ("x", "l", "c"))
+    got = []
+    for j, piece in enumerate(give, 1):
+        got.append(near(swap(piece, "l", j)))
+    col_send = pl.pallas_call(
+        join_kernel,
+        in_specs=[VMEM] * lows,
+        out_specs=VMEM,
+        out_shape=pltpu.VMEM((peers, lows, 2, nz, half), BF16),
+        name="join",
+    )(near(keep), *got)
+    col_in = exchange(col_send, ("x", "c"))
     own = pl.pallas_call(
         flux_kernel,
         in_specs=[VMEM],
@@ -133,7 +172,7 @@
         out_shape=pltpu.VMEM((2, blocks, ny, nx), BF16),
         name="flux",
     )(row_in)
-    other = partner(own)
+    other = swap(own, "h", 1)
     base = pl.pallas_call(
         x_kernel,
         grid=(1,),
@@ -144,12 +183,16 @@
     )(s, velocity, near(first_x), near(second_x))
     z_term = pl.pallas_call(
         z_kernel,
-        in_specs=[VMEM] * 3,
-        out_specs=VMEM,
-        out_shape=pltpu.VMEM((cols, nz, half), BF16),
+        in_specs=[SMEM] + [VMEM] * 3,
+        out_specs=VMEM,
+        out_shape=pltpu.VMEM((peers, lows, nz, half), BF16),
+        scratch_shapes=[
+            pltpu.VMEM((2, peers // cores, lows, cores, nz, half), BF16),
+            pltpu.VMEM((peers // cores, lows, cores, nz, half), BF16),
+        ],
         name="zmath",
-    )(near(col_in), near(first_z), near(second_z))
-    z_back = exchange(z_term, ("x", "l", "c"))
+    )(low, near(col_in), near(first_z), near(second_z))
+    z_back = exchange(z_term, ("x", "c"))
     y_term = pl.pallas_call(
         y_kernel,
         in_specs=[SMEM] + [VMEM] * 5,
@@ -159,14 +202,17 @@
         name="ymath",
     )(high, row_in, near(own), near(other), rows_split(first_y), rows_split(second_y))
     y_back = exchange(y_term, "z")
+    returned = []
+    for j in range(1, lows):
+        returned.append(near(swap(z_back[:, j], "l", j)))
     out = pl.pallas_call(
         final_kernel,
-        in_specs=[VMEM] * 3,
+        in_specs=[SMEM] + [VMEM] * (2 + lows),
         out_specs=VMEM,
         out_shape=jax.ShapeDtypeStruct((ny, nz, nx), F32),
         scratch_shapes=[pltpu.VMEM((nx // LANES, ny * nz, LANES), F32)],
         name="last",
-    )(near(base), near(y_back), near(z_back.reshape(ny, 2, nz, half)))
+    )(low, near(base), near(y_back), near(z_back), *returned)
     return out[None]
 
 

time: 76.3 us -> 75.9 us (level)
  the two profiles are of different devices: /device:TPU:1 before, /device:TPU:2 now
where the time goes in v4:
time: 75.9 us; the launch traced here: 75.2 us
  starting transfers between devices  52.6 us (69%)
  waiting for transfers between devices  15.4 us (20%)
  Pallas kernels  7.02 us (9%)
    all_to_all x4, starting transfers between devices, exchange(): return lax.all_to_all(array, axes, split_axis=0, concat_axis=0, tiled=True)  27.2 us
    ppermute x7, starting transfers between devices, swap(): lax.ppermute(array, axis, [(i, i ^ j) for i in range(lax.axis_size(axis))])  25.4 us
    ppermute x7, waiting for transfers between devices, swap(): lax.ppermute(array, axis, [(i, i ^ j) for i in range(lax.axis_size(axis))])  14.6 us
    pallas_call x1, Pallas kernels, body(): pl.pallas_call(pack_kernel, grid=(1,), in_specs=[SMEM, whole, component(v...  1.92 us
    pallas_call x1, Pallas kernels, body(): pl.pallas_call(x_kernel, grid=(1,), in_specs=[whole, component(velocity.s...  1.63 us
  transfers between devices with their start and end apart: 11, of which 5 were waited for; matrix products, arithmetic and copies ran while one was open for 0% of the time, Pallas kernels for 6%

profile of v4, /device:TPU:2, one launch (start us, length us, event | category | flops | bytes accessed | tf_op | source)
XLA Modules:
  0.0 75.2 jit_solution(43892884918369095)
XLA Ops:
  0.0 1.9 %pack.1 = (bf16[8,2,16,512]{3,2,1,0:T(8,128)(2,1)}, bf16[8,2,8,256]{3,2,1,0:T(8,128)(2,1)S(1)}, bf16[8,2,8,256]{3,2,1,0:T(8,128)(2,1)S(1)}, bf16[8,2,8,256]{3,2,1,0:T(8,128)(2,1)S(1)}, bf16[8,2,8,256]{3,2,1,0:T(8,128)(2,1)S(1)}) custom-call(s32[1]{0:T(128)} %bitcast.low_ref, f32[16,8,512]{2,1,0:T(8,128)} %bitcast.20, bf16[3,16,8,512]{3,2,1,0:T(8,128)(2,1)} %w_ref.1, ...), custom_call_target="tpu_custom_call" | custom-call | tf_op jit(solution)/shard_map/pack/pallas_call | solution.py:147
  1.9 10.3 %all-to-all-start = ((bf16[8,2,16,512]{3,2,1,0:T(8,128)(2,1)}), bf16[8,2,16,512]{3,2,1,0:T(8,128)(2,1)S(1)}, u32[]{:S(2)}, u32[]{:S(2)}) async-start(bf16[8,2,16,512]{3,2,1,0:T(8,128)(2,1)} %get-tuple-element.10), calls=%async_computation | async-start | bytes 524288 | tf_op jit(solution)/shard_map/all_to_all | solution.py:142
  12.2 3.5 %collective-permute-start.1 = (bf16[8,2,8,256]{3,2,1,0:T(8,128)(2,1)S(1)}, bf16[8,2,8,256]{3,2,1,0:T(8,128)(2,1)S(1)}, u32[]{:S(2)}, u32[]{:S(2)}) collective-permute-start(bf16[8,2,8,256]{3,2,1,0:T(8,128)(2,1)S(1)} %get-tuple-element.12), channel_id=1, source_target_pairs={{0,2},{2,0},{4,6},{6,4},{1,3},{3,1},{5,7},{7,5},{8,10},{10,8},{12,... | collective-permute-start | bytes 196616 | tf_op jit(solution)/shard_map/ppermute | solution.py:139
  15.7 4.5 %collective-permute-start.2 = (bf16[8,2,8,256]{3,2,1,0:T(8,128)(2,1)S(1)}, bf16[8,2,8,256]{3,2,1,0:T(8,128)(2,1)S(1)}, u32[]{:S(2)}, u32[]{:S(2)}) collective-permute-start(bf16[8,2,8,256]{3,2,1,0:T(8,128)(2,1)S(1)} %get-tuple-element.13), channel_id=1, source_target_pairs={{0,4},{2,6},{4,0},{6,2},{1,5},{3,7},{5,1},{7,3},{8,12},{10,14},{12... | collective-permute-start | bytes 196616 | tf_op jit(solution)/shard_map/ppermute | solution.py:139
  20.2 2.1 %collective-permute-start.3 = (bf16[8,2,8,256]{3,2,1,0:T(8,128)(2,1)S(1)}, bf16[8,2,8,256]{3,2,1,0:T(8,128)(2,1)S(1)}, u32[]{:S(2)}, u32[]{:S(2)}) collective-permute-start(bf16[8,2,8,256]{3,2,1,0:T(8,128)(2,1)S(1)} %get-tuple-element.14), channel_id=1, source_target_pairs={{0,6},{2,4},{4,2},{6,0},{1,7},{3,5},{5,3},{7,1},{8,14},{10,12},{12... | collective-permute-start | bytes 196616 | tf_op jit(solution)/shard_map/ppermute | solution.py:139
  22.4 0.0 collective-permute-done.1.refs_1_
  22.4 1.0 %collective-permute-done.2.refs_2_ = bf16[8,2,8,256]{3,2,1,0:T(8,128)(2,1)S(1)} collective-permute-done((bf16[8,2,8,256]{3,2,1,0:T(8,128)(2,1)S(1)}, bf16[8,2,8,256]{3,2,1,0:T(8,128)(2,1)S(1)}, u32[]{:S(2)}, u32[]{:S(2)}) %collective-permute-start.2) | collective-permute-done | bytes 65568 | tf_op jit(solution)/shard_map/ppermute | solution.py:139
  23.4 4.8 %collective-permute-done.3.refs_3_ = bf16[8,2,8,256]{3,2,1,0:T(8,128)(2,1)S(1)} collective-permute-done((bf16[8,2,8,256]{3,2,1,0:T(8,128)(2,1)S(1)}, bf16[8,2,8,256]{3,2,1,0:T(8,128)(2,1)S(1)}, u32[]{:S(2)}, u32[]{:S(2)}) %collective-permute-start.3) | collective-permute-done | bytes 65568 | tf_op jit(solution)/shard_map/ppermute | solution.py:139
  28.2 0.7 join.1
  28.9 0.0 all-to-all-done.r_ref
  28.9 4.8 %all-to-all-start.2 = ((bf16[8,4,2,8,256]{4,3,2,1,0:T(8,128)(2,1)}), bf16[8,4,2,8,256]{4,3,2,1,0:T(8,128)(2,1)S(1)}, u32[]{:S(2)}, u32[]{:S(2)}) async-start(bf16[8,4,2,8,256]{4,3,2,1,0:T(8,128)(2,1)} %join.1), calls=%async_computation.2 | async-start | bytes 524288 | tf_op jit(solution)/shard_map/all_to_all | solution.py:142
  33.7 0.0 copy-start.4
  33.7 0.0 copy-start.5
  33.8 5.2 %collective-permute-start = (bf16[2,8,16,512]{3,2,1,0:T(8,128)(2,1)S(1)}, bf16[2,8,16,512]{3,2,1,0:T(8,128)(2,1)S(1)}, u32[]{:S(2)}, u32[]{:S(2)}) collective-permute-start(bf16[2,8,16,512]{3,2,1,0:T(8,128)(2,1)S(1)} %flux.1.own_ref), channel_id=1, source_target_pairs={{0,32},{32,0},{1,33},{33,1},{2,34},{34,2},{3,35},{35,3},{4,36},{36... | collective-permute-start | bytes 786440 | tf_op jit(solution)/shard_map/ppermute | solution.py:139
  39.0 0.8 %all-to-all-done.2.r_ref = bf16[8,4,2,8,256]{4,3,2,1,0:T(8,128)(2,1)S(1)} async-done(((bf16[8,4,2,8,256]{4,3,2,1,0:T(8,128)(2,1)}), bf16[8,4,2,8,256]{4,3,2,1,0:T(8,128)(2,1)S(1)}, u32[]{:S(2)}, u32[]{:S(2)}) %all-to-all-start.2) | async-done | bytes 262176 | tf_op jit(solution)/shard_map/all_to_all | solution.py:142
  39.8 0.0 copy-done.4
  39.8 0.0 copy-done.5
  39.8 1.0 %zmath.1 = bf16[8,4,8,256]{3,2,1,0:T(8,128)(2,1)} custom-call(s32[1]{0:T(128)} %bitcast.low_ref, bf16[8,4,2,8,256]{4,3,2,1,0:T(8,128)(2,1)S(1)} %all-to-all-done.2.r_ref, bf16[256,256]{1,0:T(8,128)(2,1)S(1)} %copy-done.4, bf16[256,256]{1,0:T(8,128)(2,1)S(1)} %copy-done.5), custom_call_target="tpu_custom_call" | custom-call | tf_op jit(solution)/shard_map/zmath/pallas_call | solution.py:184
  40.7 0.0 copy-start.2
  40.7 0.0 copy-start.3
  40.7 4.9 %all-to-all-start.3 = ((bf16[8,4,8,256]{3,2,1,0:T(8,128)(2,1)}), bf16[8,4,8,256]{3,2,1,0:T(8,128)(2,1)S(1)}, u32[]{:S(2)}, u32[]{:S(2)}) async-start(bf16[8,4,8,256]{3,2,1,0:T(8,128)(2,1)} %zmath.1), calls=%async_computation.3 | async-start | bytes 262144 | tf_op jit(solution)/shard_map/all_to_all | solution.py:142
  45.6 8.1 %collective-permute-done.other_ref = bf16[2,8,16,512]{3,2,1,0:T(8,128)(2,1)S(1)} collective-permute-done((bf16[2,8,16,512]{3,2,1,0:T(8,128)(2,1)S(1)}, bf16[2,8,16,512]{3,2,1,0:T(8,128)(2,1)S(1)}, u32[]{:S(2)}, u32[]{:S(2)}) %collective-permute-start) | collective-permute-done | bytes 262176 | tf_op jit(solution)/shard_map/ppermute | solution.py:139
  53.7 0.0 copy-done.2
  53.7 0.0 copy-done.3
  53.7 0.0 copy-start
  53.7 0.0 copy-start.1
  53.7 1.0 %ymath.1 = bf16[8,16,512]{2,1,0:T(8,128)(2,1)} custom-call(s32[1]{0:T(128)} %bitcast.2.high_ref, bf16[8,2,16,512]{3,2,1,0:T(8,128)(2,1)S(1)} %all-to-all-done.r_ref, bf16[2,8,16,512]{3,2,1,0:T(8,128)(2,1)S(1)} %flux.1.own_ref, bf16[2,8,16,512]{3,2,1,0:T(8,128)(2,1)S(1)} %collective-permute-done.other_ref, bf16[8,2,16,256]{3,2,1,0:T(8,128)(2,1)S(1)} %bitcast.18, ...), custom_call_target="tpu_custom_call" | custom-call | tf_op jit(solution)/shard_map/ymath/pallas_call | solution.py:196
  54.7 0.0 all-to-all-done.3.own_ref
  54.7 7.2 %all-to-all-start.1 = ((bf16[8,16,512]{2,1,0:T(8,128)(2,1)}), bf16[8,16,512]{2,1,0:T(8,128)(2,1)S(1)}, u32[]{:S(2)}, u32[]{:S(2)}) async-start(bf16[8,16,512]{2,1,0:T(8,128)(2,1)} %ymath.1), calls=%async_computation.1 | async-start | bytes 262144 | tf_op jit(solution)/shard_map/all_to_all | solution.py:142
  61.9 1.9 %collective-permute-start.4 = (bf16[8,8,256]{2,1,0:T(8,128)(2,1)S(1)}, bf16[8,8,256]{2,1,0:T(8,128)(2,1)S(1)}, u32[]{:S(2)}, u32[]{:S(2)}) collective-permute-start(bf16[8,8,256]{2,1,0:T(8,128)(2,1)S(1)} %get-tuple-element.17), channel_id=1, source_target_pairs={{0,2},{2,0},{4,6},{6,4},{1,3},{3,1},{5,7},{7,5},{8,10},{10,8},{12,... | collective-permute-start | bytes 98312 | tf_op jit(solution)/shard_map/ppermute | solution.py:139
  63.8 3.0 %collective-permute-start.5 = (bf16[8,8,256]{2,1,0:T(8,128)(2,1)S(1)}, bf16[8,8,256]{2,1,0:T(8,128)(2,1)S(1)}, u32[]{:S(2)}, u32[]{:S(2)}) collective-permute-start(bf16[8,8,256]{2,1,0:T(8,128)(2,1)S(1)} %get-tuple-element.16), channel_id=1, source_target_pairs={{0,4},{2,6},{4,0},{6,2},{1,5},{3,7},{5,1},{7,3},{8,12},{10,14},{12... | collective-permute-start | bytes 98312 | tf_op jit(solution)/shard_map/ppermute | solution.py:139
  66.7 5.2 %collective-permute-start.6 = (bf16[8,8,256]{2,1,0:T(8,128)(2,1)S(1)}, bf16[8,8,256]{2,1,0:T(8,128)(2,1)S(1)}, u32[]{:S(2)}, u32[]{:S(2)}) collective-permute-start(bf16[8,8,256]{2,1,0:T(8,128)(2,1)S(1)} %get-tuple-element.15), channel_id=1, source_target_pairs={{0,6},{2,4},{4,2},{6,0},{1,7},{3,5},{5,3},{7,1},{8,14},{10,12},{12... | collective-permute-start | bytes 98312 | tf_op jit(solution)/shard_map/ppermute | solution.py:139
  72.0 0.0 copy-done
  72.0 0.0 copy-done.1
  72.0 1.6 %xmath.1.base_ref = f32[16,8,512]{2,1,0:T(8,128)S(1)} custom-call(f32[16,8,512]{2,1,0:T(8,128)} %bitcast.21, bf16[3,16,8,512]{3,2,1,0:T(8,128)(2,1)} %w_ref.1, bf16[512,512]{1,0:T(8,128)(2,1)S(1)} %copy-done, bf16[512,512]{1,0:T(8,128)(2,1)S(1)} %copy-done.1), custom_call_target="tpu_custom_call" | custom-call | tf_op jit(solution)/shard_map/xmath/pallas_call | solution.py:176
  73.7 0.0 collective-permute-done.4.rest_0_
  73.7 0.0 collective-permute-done.5.rest_1_
  73.7 0.7 collective-permute-done.6.rest_2_
  74.4 0.0 all-to-all-done.1.y_ref
  74.4 0.8 %last.1 = f32[16,8,512]{2,1,0:T(8,128)} custom-call(s32[1]{0:T(128)} %bitcast.low_ref, f32[16,8,512]{2,1,0:T(8,128)S(1)} %xmath.1.base_ref, bf16[8,16,512]{2,1,0:T(8,128)(2,1)S(1)} %all-to-all-done.1.y_ref, bf16[8,4,8,256]{3,2,1,0:T(8,128)(2,1)S(1)} %all-to-all-done.3.own_ref, bf16[8,8,256]{2,1,0:T(8,128)(2,1)S(1)} %collective-permute-done.4.rest_0_, ...), custom_call_target="tpu_custom_call" | custom-call | tf_op jit(solution)/shard_map/last/pallas_call | solution.py:208
  (2 shorter events, 0.0 us)
Async XLA Ops:
  1.9 27.0 %all-to-all-start = ((bf16[8,2,16,512]{3,2,1,0:T(8,128)(2,1)}), bf16[8,2,16,512]{3,2,1,0:T(8,128)(2,1)S(1)}, u32[]{:S(2)}, u32[]{:S(2)}) async-start(bf16[8,2,16,512]{3,2,1,0:T(8,128)(2,1)} %get-tuple-element.10), calls=%async_computation | async-start | bytes 524288 | tf_op jit(solution)/shard_map/all_to_all | solution.py:142
  12.2 10.1 %collective-permute-start.1 = (bf16[8,2,8,256]{3,2,1,0:T(8,128)(2,1)S(1)}, bf16[8,2,8,256]{3,2,1,0:T(8,128)(2,1)S(1)}, u32[]{:S(2)}, u32[]{:S(2)}) collective-permute-start(bf16[8,2,8,256]{3,2,1,0:T(8,128)(2,1)S(1)} %get-tuple-element.12), channel_id=1, source_target_pairs={{0,2},{2,0},{4,6},{6,4},{1,3},{3,1},{5,7},{7,5},{8,10},{10,8},{12,... | collective-permute-start | bytes 196616 | tf_op jit(solution)/shard_map/ppermute | solution.py:139
  15.7 7.6 %collective-permute-start.2 = (bf16[8,2,8,256]{3,2,1,0:T(8,128)(2,1)S(1)}, bf16[8,2,8,256]{3,2,1,0:T(8,128)(2,1)S(1)}, u32[]{:S(2)}, u32[]{:S(2)}) collective-permute-start(bf16[8,2,8,256]{3,2,1,0:T(8,128)(2,1)S(1)} %get-tuple-element.13), channel_id=1, source_target_pairs={{0,4},{2,6},{4,0},{6,2},{1,5},{3,7},{5,1},{7,3},{8,12},{10,14},{12... | collective-permute-start | bytes 196616 | tf_op jit(solution)/shard_map/ppermute | solution.py:139
  20.2 8.0 %collective-permute-start.3 = (bf16[8,2,8,256]{3,2,1,0:T(8,128)(2,1)S(1)}, bf16[8,2,8,256]{3,2,1,0:T(8,128)(2,1)S(1)}, u32[]{:S(2)}, u32[]{:S(2)}) collective-permute-start(bf16[8,2,8,256]{3,2,1,0:T(8,128)(2,1)S(1)} %get-tuple-element.14), channel_id=1, source_target_pairs={{0,6},{2,4},{4,2},{6,0},{1,7},{3,5},{5,3},{7,1},{8,14},{10,12},{12... | collective-permute-start | bytes 196616 | tf_op jit(solution)/shard_map/ppermute | solution.py:139
  28.9 10.9 %all-to-all-start.2 = ((bf16[8,4,2,8,256]{4,3,2,1,0:T(8,128)(2,1)}), bf16[8,4,2,8,256]{4,3,2,1,0:T(8,128)(2,1)S(1)}, u32[]{:S(2)}, u32[]{:S(2)}) async-start(bf16[8,4,2,8,256]{4,3,2,1,0:T(8,128)(2,1)} %join.1), calls=%async_computation.2 | async-start | bytes 524288 | tf_op jit(solution)/shard_map/all_to_all | solution.py:142
  33.7 6.1 %copy-start.4 = (bf16[256,256]{1,0:T(8,128)(2,1)S(1)}, bf16[256,256]{1,0:T(8,128)(2,1)}, u32[]{:S(2)}) copy-start(bf16[256,256]{1,0:T(8,128)(2,1)} %first_ref.3) | copy-start | bytes 393220
  33.7 6.1 %copy-start.5 = (bf16[256,256]{1,0:T(8,128)(2,1)S(1)}, bf16[256,256]{1,0:T(8,128)(2,1)}, u32[]{:S(2)}) copy-start(bf16[256,256]{1,0:T(8,128)(2,1)} %second_ref.3) | copy-start | bytes 393220
  33.8 19.9 %collective-permute-start = (bf16[2,8,16,512]{3,2,1,0:T(8,128)(2,1)S(1)}, bf16[2,8,16,512]{3,2,1,0:T(8,128)(2,1)S(1)}, u32[]{:S(2)}, u32[]{:S(2)}) collective-permute-start(bf16[2,8,16,512]{3,2,1,0:T(8,128)(2,1)S(1)} %flux.1.own_ref), channel_id=1, source_target_pairs={{0,32},{32,0},{1,33},{33,1},{2,34},{34,2},{3,35},{35,3},{4,36},{36... | collective-permute-start | bytes 786440 | tf_op jit(solution)/shard_map/ppermute | solution.py:139
  40.7 13.0 %copy-start.2 = (bf16[256,256]{1,0:T(8,128)(2,1)S(1)}, bf16[256,256]{1,0:T(8,128)(2,1)}, u32[]{:S(2)}) copy-start(bf16[256,256]{1,0:T(8,128)(2,1)} %param.12) | copy-start | bytes 393220
  40.7 13.0 %copy-start.3 = (bf16[256,256]{1,0:T(8,128)(2,1)S(1)}, bf16[256,256]{1,0:T(8,128)(2,1)}, u32[]{:S(2)}) copy-start(bf16[256,256]{1,0:T(8,128)(2,1)} %param.13) | copy-start | bytes 393220
  40.7 13.9 %all-to-all-start.3 = ((bf16[8,4,8,256]{3,2,1,0:T(8,128)(2,1)}), bf16[8,4,8,256]{3,2,1,0:T(8,128)(2,1)S(1)}, u32[]{:S(2)}, u32[]{:S(2)}) async-start(bf16[8,4,8,256]{3,2,1,0:T(8,128)(2,1)} %zmath.1), calls=%async_computation.3 | async-start | bytes 262144 | tf_op jit(solution)/shard_map/all_to_all | solution.py:142
  53.7 18.3 %copy-start = (bf16[512,512]{1,0:T(8,128)(2,1)S(1)}, bf16[512,512]{1,0:T(8,128)(2,1)}, u32[]{:S(2)}) copy-start(bf16[512,512]{1,0:T(8,128)(2,1)} %first_ref.2) | copy-start | bytes 1572868
  53.7 18.3 %copy-start.1 = (bf16[512,512]{1,0:T(8,128)(2,1)S(1)}, bf16[512,512]{1,0:T(8,128)(2,1)}, u32[]{:S(2)}) copy-start(bf16[512,512]{1,0:T(8,128)(2,1)} %second_ref.2) | copy-start | bytes 1572868
  54.7 19.7 %all-to-all-start.1 = ((bf16[8,16,512]{2,1,0:T(8,128)(2,1)}), bf16[8,16,512]{2,1,0:T(8,128)(2,1)S(1)}, u32[]{:S(2)}, u32[]{:S(2)}) async-start(bf16[8,16,512]{2,1,0:T(8,128)(2,1)} %ymath.1), calls=%async_computation.1 | async-start | bytes 262144 | tf_op jit(solution)/shard_map/all_to_all | solution.py:142
  61.9 11.8 %collective-permute-start.4 = (bf16[8,8,256]{2,1,0:T(8,128)(2,1)S(1)}, bf16[8,8,256]{2,1,0:T(8,128)(2,1)S(1)}, u32[]{:S(2)}, u32[]{:S(2)}) collective-permute-start(bf16[8,8,256]{2,1,0:T(8,128)(2,1)S(1)} %get-tuple-element.17), channel_id=1, source_target_pairs={{0,2},{2,0},{4,6},{6,4},{1,3},{3,1},{5,7},{7,5},{8,10},{10,8},{12,... | collective-permute-start | bytes 98312 | tf_op jit(solution)/shard_map/ppermute | solution.py:139
  63.8 9.9 %collective-permute-start.5 = (bf16[8,8,256]{2,1,0:T(8,128)(2,1)S(1)}, bf16[8,8,256]{2,1,0:T(8,128)(2,1)S(1)}, u32[]{:S(2)}, u32[]{:S(2)}) collective-permute-start(bf16[8,8,256]{2,1,0:T(8,128)(2,1)S(1)} %get-tuple-element.16), channel_id=1, source_target_pairs={{0,4},{2,6},{4,0},{6,2},{1,5},{3,7},{5,1},{7,3},{8,12},{10,14},{12... | collective-permute-start | bytes 98312 | tf_op jit(solution)/shard_map/ppermute | solution.py:139
  66.7 7.6 %collective-permute-start.6 = (bf16[8,8,256]{2,1,0:T(8,128)(2,1)S(1)}, bf16[8,8,256]{2,1,0:T(8,128)(2,1)S(1)}, u32[]{:S(2)}, u32[]{:S(2)}) collective-permute-start(bf16[8,8,256]{2,1,0:T(8,128)(2,1)S(1)} %get-tuple-element.15), channel_id=1, source_target_pairs={{0,6},{2,4},{4,2},{6,0},{1,7},{3,5},{5,3},{7,1},{8,14},{10,12},{12... | collective-permute-start | bytes 98312 | tf_op jit(solution)/shard_map/ppermute | solution.py:139

commit v5 on v4

--- a/solution.py
+++ b/solution.py
@@ -128,10 +128,11 @@
 def body(scalars, velocity, first_x, second_x, first_y, second_y, first_z, second_z):
     _, ny, nz, nx = scalars.shape
     half = nx // 2
-    blocks, lows, cores = lax.axis_size("z"), lax.axis_size("l"), lax.axis_size("c")
+    blocks, lows = lax.axis_size("z"), lax.axis_size("m")
+    cores = lax.axis_size("l") * lax.axis_size("c")
     peers = lax.axis_size("x") * cores
     high = lax.axis_index("h").reshape(1)
-    low = lax.axis_index("l").reshape(1)
+    low = lax.axis_index("m").reshape(1)
     s = scalars[0]
     whole = pl.BlockSpec((ny, nz, nx), lambda i: (0, 0, 0))
 
@@ -156,7 +157,7 @@
     row_in = near(exchange(row_send, "z"))
     got = []
     for j, piece in enumerate(give, 1):
-        got.append(near(swap(piece, "l", j)))
+        got.append(near(swap(piece, "m", j)))
     col_send = pl.pallas_call(
         join_kernel,
         in_specs=[VMEM] * lows,
@@ -164,7 +165,7 @@
         out_shape=pltpu.VMEM((peers, lows, 2, nz, half), BF16),
         name="join",
     )(near(keep), *got)
-    col_in = exchange(col_send, ("x", "c"))
+    col_in = exchange(col_send, ("x", "l", "c"))
     own = pl.pallas_call(
         flux_kernel,
         in_specs=[VMEM],
@@ -192,7 +193,7 @@
         ],
         name="zmath",
     )(low, near(col_in), near(first_z), near(second_z))
-    z_back = exchange(z_term, ("x", "c"))
+    z_back = exchange(z_term, ("x", "l", "c"))
     y_term = pl.pallas_call(
         y_kernel,
         in_specs=[SMEM] + [VMEM] * 5,
@@ -204,7 +205,7 @@
     y_back = exchange(y_term, "z")
     returned = []
     for j in range(1, lows):
-        returned.append(near(swap(z_back[:, j], "l", j)))
+        returned.append(near(swap(z_back[:, j], "m", j)))
     out = pl.pallas_call(
         final_kernel,
         in_specs=[SMEM] + [VMEM] * (2 + lows),
@@ -217,8 +218,8 @@
 
 
 def solution(mesh):
-    parts = Mesh(mesh.devices.reshape(8, 2, 4, 4, 2), ("z", "h", "x", "l", "c"))
-    pencil = P(None, ("z", "h"), ("x", "l", "c"), None)
+    parts = Mesh(mesh.devices.reshape(8, 2, 4, 2, 2, 2), ("z", "h", "x", "m", "l", "c"))
+    pencil = P(None, ("z", "h"), ("x", "m", "l", "c"), None)
     return jax.shard_map(
         body,
         mesh=parts,

time: 75.9 us -> 70.2 us (0.925)
  the two profiles are of different devices: /device:TPU:2 before, /device:TPU:1 now
where the time goes in v5:
time: 70.2 us; the launch traced here: 69.6 us
  starting transfers between devices  43.2 us (62%)
  waiting for transfers between devices  19.2 us (27%)
  Pallas kernels  7.03 us (10%)
    all_to_all x4, starting transfers between devices, exchange(): return lax.all_to_all(array, axes, split_axis=0, concat_axis=0, tiled=True)  29.9 us
    ppermute x3, starting transfers between devices, swap(): lax.ppermute(array, axis, [(i, i ^ j) for i in range(lax.axis_size(axis))])  13.3 us
    ppermute x3, waiting for transfers between devices, swap(): lax.ppermute(array, axis, [(i, i ^ j) for i in range(lax.axis_size(axis))])  11.7 us
    all_to_all x4, waiting for transfers between devices, exchange(): return lax.all_to_all(array, axes, split_axis=0, concat_axis=0, tiled=True)  7.44 us
    pallas_call x1, Pallas kernels, body(): pl.pallas_call(pack_kernel, grid=(1,), in_specs=[SMEM, whole, component(v...  1.92 us
    pallas_call x1, Pallas kernels, body(): pl.pallas_call(x_kernel, grid=(1,), in_specs=[whole, component(velocity.s...  1.64 us
  transfers between devices with their start and end apart: 7, of which 5 were waited for; matrix products, arithmetic and copies ran while one was open for 0% of the time, Pallas kernels for 6%

profile of v5, /device:TPU:1, one launch (start us, length us, event | category | flops | bytes accessed | tf_op | source)
XLA Modules:
  0.0 69.6 jit_solution(11871536333921446416)
XLA Ops:
  0.0 1.9 %pack.1 = (bf16[8,2,16,512]{3,2,1,0:T(8,128)(2,1)}, bf16[16,2,8,256]{3,2,1,0:T(8,128)(2,1)S(1)}, bf16[16,2,8,256]{3,2,1,0:T(8,128)(2,1)S(1)}) custom-call(s32[1]{0:T(128)} %bitcast.low_ref, f32[16,8,512]{2,1,0:T(8,128)} %bitcast.12, bf16[3,16,8,512]{3,2,1,0:T(8,128)(2,1)} %w_ref.1, bf16[3,16,8,512]{3,2,1,0:T(8,128)(2,1)} %w_ref.1), custom_call_target="tpu_custom_call" | custom-call | tf_op jit(solution)/shard_map/pack/pallas_call | solution.py:148
  1.9 10.9 %all-to-all-start = ((bf16[8,2,16,512]{3,2,1,0:T(8,128)(2,1)}), bf16[8,2,16,512]{3,2,1,0:T(8,128)(2,1)S(1)}, u32[]{:S(2)}, u32[]{:S(2)}) async-start(bf16[8,2,16,512]{3,2,1,0:T(8,128)(2,1)} %get-tuple-element.8), calls=%async_computation | async-start | bytes 524288 | tf_op jit(solution)/shard_map/all_to_all | solution.py:143
  12.8 4.2 %collective-permute-start.1 = (bf16[16,2,8,256]{3,2,1,0:T(8,128)(2,1)S(1)}, bf16[16,2,8,256]{3,2,1,0:T(8,128)(2,1)S(1)}, u32[]{:S(2)}, u32[]{:S(2)}) collective-permute-start(bf16[16,2,8,256]{3,2,1,0:T(8,128)(2,1)S(1)} %get-tuple-element.10), channel_id=1, source_target_pairs={{0,4},{4,0},{1,5},{5,1},{2,6},{6,2},{3,7},{7,3},{8,12},{12,8},{9,1... | collective-permute-start | bytes 393224 | tf_op jit(solution)/shard_map/ppermute | solution.py:140
  17.0 5.8 %collective-permute-done.1.refs_1_ = bf16[16,2,8,256]{3,2,1,0:T(8,128)(2,1)S(1)} collective-permute-done((bf16[16,2,8,256]{3,2,1,0:T(8,128)(2,1)S(1)}, bf16[16,2,8,256]{3,2,1,0:T(8,128)(2,1)S(1)}, u32[]{:S(2)}, u32[]{:S(2)}) %collective-permute-start.1) | collective-permute-done | bytes 131104 | tf_op jit(solution)/shard_map/ppermute | solution.py:140
  22.8 0.7 %join.1 = bf16[16,2,2,8,256]{4,3,2,1,0:T(8,128)(2,1)} custom-call(bf16[16,2,8,256]{3,2,1,0:T(8,128)(2,1)S(1)} %get-tuple-element.9.refs_0_, bf16[16,2,8,256]{3,2,1,0:T(8,128)(2,1)S(1)} %collective-permute-done.1.refs_1_), custom_call_target="tpu_custom_call" | custom-call | tf_op jit(solution)/shard_map/join/pallas_call | solution.py:161
  23.5 0.0 all-to-all-done.r_ref
  23.5 7.5 %all-to-all-start.2 = ((bf16[16,2,2,8,256]{4,3,2,1,0:T(8,128)(2,1)}), bf16[16,2,2,8,256]{4,3,2,1,0:T(8,128)(2,1)S(1)}, u32[]{:S(2)}, u32[]{:S(2)}) async-start(bf16[16,2,2,8,256]{4,3,2,1,0:T(8,128)(2,1)} %join.1), calls=%async_computation.2 | async-start | bytes 524288 | tf_op jit(solution)/shard_map/all_to_all | solution.py:143
  30.9 0.0 copy-start.4
  30.9 0.0 copy-start.5
  31.0 6.7 %collective-permute-start = (bf16[2,8,16,512]{3,2,1,0:T(8,128)(2,1)S(1)}, bf16[2,8,16,512]{3,2,1,0:T(8,128)(2,1)S(1)}, u32[]{:S(2)}, u32[]{:S(2)}) collective-permute-start(bf16[2,8,16,512]{3,2,1,0:T(8,128)(2,1)S(1)} %flux.1.own_ref), channel_id=1, source_target_pairs={{0,32},{32,0},{1,33},{33,1},{2,34},{34,2},{3,35},{35,3},{4,36},{36... | collective-permute-start | bytes 786440 | tf_op jit(solution)/shard_map/ppermute | solution.py:140
  37.7 0.4 all-to-all-done.2.r_ref
  38.1 0.0 copy-done.4
  38.1 0.0 copy-done.5
  38.1 1.0 %zmath.1 = bf16[16,2,8,256]{3,2,1,0:T(8,128)(2,1)} custom-call(s32[1]{0:T(128)} %bitcast.low_ref, bf16[16,2,2,8,256]{4,3,2,1,0:T(8,128)(2,1)S(1)} %all-to-all-done.2.r_ref, bf16[256,256]{1,0:T(8,128)(2,1)S(1)} %copy-done.4, bf16[256,256]{1,0:T(8,128)(2,1)S(1)} %copy-done.5), custom_call_target="tpu_custom_call" | custom-call | tf_op jit(solution)/shard_map/zmath/pallas_call | solution.py:185
  39.1 0.0 copy-start.2
  39.1 0.0 copy-start.3
  39.1 5.7 %all-to-all-start.3 = ((bf16[16,2,8,256]{3,2,1,0:T(8,128)(2,1)}), bf16[16,2,8,256]{3,2,1,0:T(8,128)(2,1)S(1)}, u32[]{:S(2)}, u32[]{:S(2)}) async-start(bf16[16,2,8,256]{3,2,1,0:T(8,128)(2,1)} %zmath.1), calls=%async_computation.3 | async-start | bytes 262144 | tf_op jit(solution)/shard_map/all_to_all | solution.py:143
  44.8 2.0 %collective-permute-done.other_ref = bf16[2,8,16,512]{3,2,1,0:T(8,128)(2,1)S(1)} collective-permute-done((bf16[2,8,16,512]{3,2,1,0:T(8,128)(2,1)S(1)}, bf16[2,8,16,512]{3,2,1,0:T(8,128)(2,1)S(1)}, u32[]{:S(2)}, u32[]{:S(2)}) %collective-permute-start) | collective-permute-done | bytes 262176 | tf_op jit(solution)/shard_map/ppermute | solution.py:140
  46.8 0.0 copy-done.2
  46.8 0.0 copy-done.3
  46.8 0.0 copy-start
  46.8 0.0 copy-start.1
  46.8 1.0 %ymath.1 = bf16[8,16,512]{2,1,0:T(8,128)(2,1)} custom-call(s32[1]{0:T(128)} %bitcast.2.high_ref, bf16[8,2,16,512]{3,2,1,0:T(8,128)(2,1)S(1)} %all-to-all-done.r_ref, bf16[2,8,16,512]{3,2,1,0:T(8,128)(2,1)S(1)} %flux.1.own_ref, bf16[2,8,16,512]{3,2,1,0:T(8,128)(2,1)S(1)} %collective-permute-done.other_ref, bf16[8,2,16,256]{3,2,1,0:T(8,128)(2,1)S(1)} %bitcast.10, ...), custom_call_target="tpu_custom_call" | custom-call | tf_op jit(solution)/shard_map/ymath/pallas_call | solution.py:197
  47.8 7.0 %all-to-all-done.3.own_ref = bf16[16,2,8,256]{3,2,1,0:T(8,128)(2,1)S(1)} async-done(((bf16[16,2,8,256]{3,2,1,0:T(8,128)(2,1)}), bf16[16,2,8,256]{3,2,1,0:T(8,128)(2,1)S(1)}, u32[]{:S(2)}, u32[]{:S(2)}) %all-to-all-start.3) | async-done | bytes 131104 | tf_op jit(solution)/shard_map/all_to_all | solution.py:143
  54.8 5.9 %all-to-all-start.1 = ((bf16[8,16,512]{2,1,0:T(8,128)(2,1)}), bf16[8,16,512]{2,1,0:T(8,128)(2,1)S(1)}, u32[]{:S(2)}, u32[]{:S(2)}) async-start(bf16[8,16,512]{2,1,0:T(8,128)(2,1)} %ymath.1), calls=%async_computation.1 | async-start | bytes 262144 | tf_op jit(solution)/shard_map/all_to_all | solution.py:143
  60.7 2.4 %collective-permute-start.2 = (bf16[16,8,256]{2,1,0:T(8,128)(2,1)S(1)}, bf16[16,8,256]{2,1,0:T(8,128)(2,1)S(1)}, u32[]{:S(2)}, u32[]{:S(2)}) collective-permute-start(bf16[16,8,256]{2,1,0:T(8,128)(2,1)S(1)} %slice_bitcast_fusion), channel_id=1, source_target_pairs={{0,4},{4,0},{1,5},{5,1},{2,6},{6,2},{3,7},{7,3},{8,12},{12,8},{9,1... | collective-permute-start | bytes 196616 | tf_op jit(solution)/shard_map/ppermute | solution.py:140
  63.1 0.0 copy-done
  63.1 0.0 copy-done.1
  63.2 1.6 %xmath.1.base_ref = f32[16,8,512]{2,1,0:T(8,128)S(1)} custom-call(f32[16,8,512]{2,1,0:T(8,128)} %bitcast.13, bf16[3,16,8,512]{3,2,1,0:T(8,128)(2,1)} %w_ref.1, bf16[512,512]{1,0:T(8,128)(2,1)S(1)} %copy-done, bf16[512,512]{1,0:T(8,128)(2,1)S(1)} %copy-done.1), custom_call_target="tpu_custom_call" | custom-call | tf_op jit(solution)/shard_map/xmath/pallas_call | solution.py:177
  64.8 4.0 %collective-permute-done.2.rest_0_ = bf16[16,8,256]{2,1,0:T(8,128)(2,1)S(1)} collective-permute-done((bf16[16,8,256]{2,1,0:T(8,128)(2,1)S(1)}, bf16[16,8,256]{2,1,0:T(8,128)(2,1)S(1)}, u32[]{:S(2)}, u32[]{:S(2)}) %collective-permute-start.2) | collective-permute-done | bytes 65568 | tf_op jit(solution)/shard_map/ppermute | solution.py:140
  68.8 0.0 all-to-all-done.1.y_ref
  68.8 0.8 %last.1 = f32[16,8,512]{2,1,0:T(8,128)} custom-call(s32[1]{0:T(128)} %bitcast.low_ref, f32[16,8,512]{2,1,0:T(8,128)S(1)} %xmath.1.base_ref, bf16[8,16,512]{2,1,0:T(8,128)(2,1)S(1)} %all-to-all-done.1.y_ref, bf16[16,2,8,256]{3,2,1,0:T(8,128)(2,1)S(1)} %all-to-all-done.3.own_ref, bf16[16,8,256]{2,1,0:T(8,128)(2,1)S(1)} %collective-permute-done.2.rest_0_), custom_call_target="tpu_custom_call" | custom-call | tf_op jit(solution)/shard_map/last/pallas_call | solution.py:209
  (2 shorter events, 0.0 us)
Async XLA Ops:
  1.9 21.6 %all-to-all-start = ((bf16[8,2,16,512]{3,2,1,0:T(8,128)(2,1)}), bf16[8,2,16,512]{3,2,1,0:T(8,128)(2,1)S(1)}, u32[]{:S(2)}, u32[]{:S(2)}) async-start(bf16[8,2,16,512]{3,2,1,0:T(8,128)(2,1)} %get-tuple-element.8), calls=%async_computation | async-start | bytes 524288 | tf_op jit(solution)/shard_map/all_to_all | solution.py:143
  12.8 10.0 %collective-permute-start.1 = (bf16[16,2,8,256]{3,2,1,0:T(8,128)(2,1)S(1)}, bf16[16,2,8,256]{3,2,1,0:T(8,128)(2,1)S(1)}, u32[]{:S(2)}, u32[]{:S(2)}) collective-permute-start(bf16[16,2,8,256]{3,2,1,0:T(8,128)(2,1)S(1)} %get-tuple-element.10), channel_id=1, source_target_pairs={{0,4},{4,0},{1,5},{5,1},{2,6},{6,2},{3,7},{7,3},{8,12},{12,8},{9,1... | collective-permute-start | bytes 393224 | tf_op jit(solution)/shard_map/ppermute | solution.py:140
  23.5 14.6 %all-to-all-start.2 = ((bf16[16,2,2,8,256]{4,3,2,1,0:T(8,128)(2,1)}), bf16[16,2,2,8,256]{4,3,2,1,0:T(8,128)(2,1)S(1)}, u32[]{:S(2)}, u32[]{:S(2)}) async-start(bf16[16,2,2,8,256]{4,3,2,1,0:T(8,128)(2,1)} %join.1), calls=%async_computation.2 | async-start | bytes 524288 | tf_op jit(solution)/shard_map/all_to_all | solution.py:143
  30.9 7.2 %copy-start.4 = (bf16[256,256]{1,0:T(8,128)(2,1)S(1)}, bf16[256,256]{1,0:T(8,128)(2,1)}, u32[]{:S(2)}) copy-start(bf16[256,256]{1,0:T(8,128)(2,1)} %first_ref.3) | copy-start | bytes 393220
  30.9 7.2 %copy-start.5 = (bf16[256,256]{1,0:T(8,128)(2,1)S(1)}, bf16[256,256]{1,0:T(8,128)(2,1)}, u32[]{:S(2)}) copy-start(bf16[256,256]{1,0:T(8,128)(2,1)} %second_ref.3) | copy-start | bytes 393220
  31.0 15.8 %collective-permute-start = (bf16[2,8,16,512]{3,2,1,0:T(8,128)(2,1)S(1)}, bf16[2,8,16,512]{3,2,1,0:T(8,128)(2,1)S(1)}, u32[]{:S(2)}, u32[]{:S(2)}) collective-permute-start(bf16[2,8,16,512]{3,2,1,0:T(8,128)(2,1)S(1)} %flux.1.own_ref), channel_id=1, source_target_pairs={{0,32},{32,0},{1,33},{33,1},{2,34},{34,2},{3,35},{35,3},{4,36},{36... | collective-permute-start | bytes 786440 | tf_op jit(solution)/shard_map/ppermute | solution.py:140
  39.1 7.7 %copy-start.2 = (bf16[256,256]{1,0:T(8,128)(2,1)S(1)}, bf16[256,256]{1,0:T(8,128)(2,1)}, u32[]{:S(2)}) copy-start(bf16[256,256]{1,0:T(8,128)(2,1)} %param.12) | copy-start | bytes 393220
  39.1 7.7 %copy-start.3 = (bf16[256,256]{1,0:T(8,128)(2,1)S(1)}, bf16[256,256]{1,0:T(8,128)(2,1)}, u32[]{:S(2)}) copy-start(bf16[256,256]{1,0:T(8,128)(2,1)} %param.13) | copy-start | bytes 393220
  39.1 15.7 %all-to-all-start.3 = ((bf16[16,2,8,256]{3,2,1,0:T(8,128)(2,1)}), bf16[16,2,8,256]{3,2,1,0:T(8,128)(2,1)S(1)}, u32[]{:S(2)}, u32[]{:S(2)}) async-start(bf16[16,2,8,256]{3,2,1,0:T(8,128)(2,1)} %zmath.1), calls=%async_computation.3 | async-start | bytes 262144 | tf_op jit(solution)/shard_map/all_to_all | solution.py:143
  46.8 16.3 %copy-start = (bf16[512,512]{1,0:T(8,128)(2,1)S(1)}, bf16[512,512]{1,0:T(8,128)(2,1)}, u32[]{:S(2)}) copy-start(bf16[512,512]{1,0:T(8,128)(2,1)} %first_ref.2) | copy-start | bytes 1572868
  46.8 16.3 %copy-start.1 = (bf16[512,512]{1,0:T(8,128)(2,1)S(1)}, bf16[512,512]{1,0:T(8,128)(2,1)}, u32[]{:S(2)}) copy-start(bf16[512,512]{1,0:T(8,128)(2,1)} %second_ref.2) | copy-start | bytes 1572868
  54.8 14.0 %all-to-all-start.1 = ((bf16[8,16,512]{2,1,0:T(8,128)(2,1)}), bf16[8,16,512]{2,1,0:T(8,128)(2,1)S(1)}, u32[]{:S(2)}, u32[]{:S(2)}) async-start(bf16[8,16,512]{2,1,0:T(8,128)(2,1)} %ymath.1), calls=%async_computation.1 | async-start | bytes 262144 | tf_op jit(solution)/shard_map/all_to_all | solution.py:143
  60.7 8.0 %collective-permute-start.2 = (bf16[16,8,256]{2,1,0:T(8,128)(2,1)S(1)}, bf16[16,8,256]{2,1,0:T(8,128)(2,1)S(1)}, u32[]{:S(2)}, u32[]{:S(2)}) collective-permute-start(bf16[16,8,256]{2,1,0:T(8,128)(2,1)S(1)} %slice_bitcast_fusion), channel_id=1, source_target_pairs={{0,4},{4,0},{1,5},{5,1},{2,6},{6,2},{3,7},{7,3},{8,12},{12,8},{9,1... | collective-permute-start | bytes 196616 | tf_op jit(solution)/shard_map/ppermute | solution.py:140

commit v6 on v5

--- a/solution.py
+++ b/solution.py
@@ -71,7 +71,13 @@
     out_ref[...] = (s + 0.5 * term).reshape(ny, nz, nx)
 
 
-def y_kernel(high_ref, r_ref, own_ref, other_ref, first_ref, second_ref, out_ref, lines):
+def rows_kernel(high_ref, first_ref, second_ref, out_ref):
+    high = high_ref[0]
+    out_ref[0] = first_ref[:, high]
+    out_ref[1] = second_ref[:, high]
+
+
+def y_kernel(high_ref, r_ref, own_ref, other_ref, rows_ref, out_ref, lines):
     _, blocks, depth, lanes = own_ref.shape
     high = high_ref[0]
     length = 2 * blocks * depth
@@ -79,14 +85,14 @@
     lines[:, :, 1 - high] = other_ref[...]
     s = lines[0].reshape(length, lanes)
     flux = lines[1].reshape(length, lanes)
-    first = first_ref[:, high].reshape(blocks * depth, length)
-    second = second_ref[:, high].reshape(blocks * depth, length)
+    first = rows_ref[0].reshape(blocks * depth, length)
+    second = rows_ref[1].reshape(blocks * depth, length)
     c = r_ref[:, 1].reshape(blocks * depth, lanes).astype(F32)
     term = -0.5 * (c * dot(first, s, 0) + dot(first, flux, 0)) + 0.5 * dot(second, s, 0)
     out_ref[...] = term.astype(BF16).reshape(blocks, depth, lanes)
 
 
-def z_kernel(low_ref, r_ref, first_ref, second_ref, out_ref, lines, terms):
+def z_kernel(low_ref, r_ref, first_ref, second_ref, out_ref, lines):
     _, nx_blocks, lows, cores, depth, lanes = lines.shape
     low = low_ref[0]
     length = nx_blocks * lows * cores * depth
@@ -98,31 +104,25 @@
     s = lines[0].reshape(length, lanes)
     c = lines[1].reshape(length, lanes).astype(F32)
     term = term_of(s, c, first_ref[...], second_ref[...], lambda m, f: dot(m, f, 0))
-    terms[...] = term.astype(BF16).reshape(terms.shape)
-    for x in range(nx_blocks):
-        for j in range(lows):
-            for c in range(cores):
-                out_ref[x * cores + c, j] = terms[x, low ^ j, c]
-
-
-def final_kernel(low_ref, base_ref, y_ref, own_ref, *rest):
-    others, (out_ref, y32) = rest[:-2], rest[-2:]
+    out_ref[...] = term.astype(BF16).reshape(out_ref.shape)
+
+
+def final_kernel(base_ref, y_ref, z_ref, out_ref, y32):
     ny, nz, nx = base_ref.shape
-    half = nx // 2
-    group = ny // (1 + len(others))
-    low = low_ref[0]
+    nx_blocks, lows, cores, _, half = z_ref.shape
     for t in range(nx // LANES):
         h, at = divmod(t * LANES, half)
         lanes = slice(t * LANES, (t + 1) * LANES)
         of = slice(at, at + LANES)
         for z in range(nz):
             y32[t, pl.ds(z, ny, stride=nz), :] = y_ref[z, :, lanes].astype(F32)
-        for j in range(1 + len(others)):
-            for q in range(group):
-                y = (low ^ j) * group + q
-                z_term = others[j - 1][2 * q + h, :, of] if j else own_ref[2 * q + h, 0, :, of]
-                y_term = y32[t, pl.ds(pl.multiple_of(y * nz, nz), nz), :]
-                out_ref[y, :, lanes] = base_ref[y, :, lanes] + 0.5 * (y_term + z_term.astype(F32))
+        for x in range(nx_blocks):
+            for j in range(lows):
+                for c in range(h, cores, 2):
+                    y = (j * nx_blocks + x) * (cores // 2) + c // 2
+                    y_term = y32[t, y * nz:(y + 1) * nz, :]
+                    z_term = z_ref[x, j, c, :, of].astype(F32)
+                    out_ref[y, :, lanes] = base_ref[y, :, lanes] + 0.5 * (y_term + z_term)
 
 
 def body(scalars, velocity, first_x, second_x, first_y, second_y, first_z, second_z):
@@ -182,38 +182,39 @@
         out_shape=pltpu.VMEM((ny, nz, nx), F32),
         name="xmath",
     )(s, velocity, near(first_x), near(second_x))
+    rows = pl.pallas_call(
+        rows_kernel,
+        in_specs=[SMEM] + [VMEM] * 2,
+        out_specs=VMEM,
+        out_shape=pltpu.VMEM((2, blocks, ny, first_y.shape[1]), BF16),
+        name="rows",
+    )(high, rows_split(first_y), rows_split(second_y))
     z_term = pl.pallas_call(
         z_kernel,
         in_specs=[SMEM] + [VMEM] * 3,
         out_specs=VMEM,
-        out_shape=pltpu.VMEM((peers, lows, nz, half), BF16),
-        scratch_shapes=[
-            pltpu.VMEM((2, peers // cores, lows, cores, nz, half), BF16),
-            pltpu.VMEM((peers // cores, lows, cores, nz, half), BF16),
-        ],
+        out_shape=pltpu.VMEM((peers * lows, nz, half), BF16),
+        scratch_shapes=[pltpu.VMEM((2, peers // cores, lows, cores, nz, half), BF16)],
         name="zmath",
     )(low, near(col_in), near(first_z), near(second_z))
-    z_back = exchange(z_term, ("x", "l", "c"))
+    z_back = exchange(z_term, ("x", "m", "l", "c"))
     y_term = pl.pallas_call(
         y_kernel,
-        in_specs=[SMEM] + [VMEM] * 5,
+        in_specs=[SMEM] + [VMEM] * 4,
         out_specs=VMEM,
         out_shape=pltpu.VMEM((blocks, ny, nx), BF16),
         scratch_shapes=[pltpu.VMEM((2, blocks, 2, ny, nx), BF16)],
         name="ymath",
-    )(high, row_in, near(own), near(other), rows_split(first_y), rows_split(second_y))
+    )(high, row_in, near(own), near(other), near(rows))
     y_back = exchange(y_term, "z")
-    returned = []
-    for j in range(1, lows):
-        returned.append(near(swap(z_back[:, j], "m", j)))
     out = pl.pallas_call(
         final_kernel,
-        in_specs=[SMEM] + [VMEM] * (2 + lows),
+        in_specs=[VMEM] * 3,
         out_specs=VMEM,
         out_shape=jax.ShapeDtypeStruct((ny, nz, nx), F32),
         scratch_shapes=[pltpu.VMEM((nx // LANES, ny * nz, LANES), F32)],
         name="last",
-    )(low, near(base), near(y_back), near(z_back), *returned)
+    )(near(base), near(y_back), near(z_back.reshape(peers // cores, lows, cores, nz, half)))
     return out[None]
 
 

time: 70.2 us -> 71.8 us (1.023)
  waiting for transfers between devices: 19.2 us -> 22.9 us
  starting transfers between devices: 43.2 us -> 41.2 us
    all_to_all x4, waiting for transfers between devices: 7.44 us -> 15.5 us  [exchange(): return lax.all_to_all(array, axes, split_axis=0, concat_axis=0, tiled=True)]
    ppermute x3 -> x2, waiting for transfers between devices: 11.7 us -> 7.35 us  [swap(): lax.ppermute(array, axis, [(i, i ^ j) for i in range(lax.axis_size(axis))])]
    ppermute x3 -> x2, starting transfers between devices: 13.3 us -> 10.9 us  [swap(): lax.ppermute(array, axis, [(i, i ^ j) for i in range(lax.axis_size(axis))])]
    pallas_call x2 -> x3, Pallas kernels: 1.77 us -> 1.77 us  [the longest x1 0.97 us: body(): pl.pallas_call(y_kernel, in_specs=[SMEM] + [VMEM] * 4, out_specs=VMEM, ou...]
  transfers between devices with their start and end apart: 7 -> 6, of which waited for: 5 -> 5; matrix products, arithmetic and copies ran while one was open for 0% -> 0% of each run, Pallas kernels for 6% -> 6%
where the time goes in v6:
time: 71.8 us; the launch traced here: 71.2 us
  starting transfers between devices  41.2 us (57%)
  waiting for transfers between devices  22.9 us (32%)
  Pallas kernels  7.02 us (10%)
    all_to_all x4, starting transfers between devices, exchange(): return lax.all_to_all(array, axes, split_axis=0, concat_axis=0, tiled=True)  30.3 us
    all_to_all x4, waiting for transfers between devices, exchange(): return lax.all_to_all(array, axes, split_axis=0, concat_axis=0, tiled=True)  15.5 us
    ppermute x2, starting transfers between devices, swap(): lax.ppermute(array, axis, [(i, i ^ j) for i in range(lax.axis_size(axis))])  10.9 us
    ppermute x2, waiting for transfers between devices, swap(): lax.ppermute(array, axis, [(i, i ^ j) for i in range(lax.axis_size(axis))])  7.35 us
    pallas_call x1, Pallas kernels, body(): pl.pallas_call(pack_kernel, grid=(1,), in_specs=[SMEM, whole, component(v...  1.92 us
    pallas_call x1, Pallas kernels, body(): pl.pallas_call(x_kernel, grid=(1,), in_specs=[whole, component(velocity.s...  1.64 us
  transfers between devices with their start and end apart: 6, of which 5 were waited for; matrix products, arithmetic and copies ran while one was open for 0% of the time, Pallas kernels for 6%

profile of v6, /device:TPU:1, one launch (start us, length us, event | category | flops | bytes accessed | tf_op | source)
XLA Modules:
  0.0 71.2 jit_solution(7147397597198777312)
XLA Ops:
  0.0 1.9 %pack.1 = (bf16[8,2,16,512]{3,2,1,0:T(8,128)(2,1)}, bf16[16,2,8,256]{3,2,1,0:T(8,128)(2,1)S(1)}, bf16[16,2,8,256]{3,2,1,0:T(8,128)(2,1)S(1)}) custom-call(s32[1]{0:T(128)} %bitcast.2.low_ref, f32[16,8,512]{2,1,0:T(8,128)} %bitcast.10, bf16[3,16,8,512]{3,2,1,0:T(8,128)(2,1)} %w_ref.1, bf16[3,16,8,512]{3,2,1,0:T(8,128)(2,1)} %w_ref.1), custom_call_target="tpu_custom_call" | custom-call | tf_op jit(solution)/shard_map/pack/pallas_call | solution.py:148
  1.9 10.9 %all-to-all-start = ((bf16[8,2,16,512]{3,2,1,0:T(8,128)(2,1)}), bf16[8,2,16,512]{3,2,1,0:T(8,128)(2,1)S(1)}, u32[]{:S(2)}, u32[]{:S(2)}) async-start(bf16[8,2,16,512]{3,2,1,0:T(8,128)(2,1)} %get-tuple-element.8), calls=%async_computation | async-start | bytes 524288 | tf_op jit(solution)/shard_map/all_to_all | solution.py:143
  12.8 4.2 %collective-permute-start.1 = (bf16[16,2,8,256]{3,2,1,0:T(8,128)(2,1)S(1)}, bf16[16,2,8,256]{3,2,1,0:T(8,128)(2,1)S(1)}, u32[]{:S(2)}, u32[]{:S(2)}) collective-permute-start(bf16[16,2,8,256]{3,2,1,0:T(8,128)(2,1)S(1)} %get-tuple-element.10), channel_id=1, source_target_pairs={{0,4},{4,0},{1,5},{5,1},{2,6},{6,2},{3,7},{7,3},{8,12},{12,8},{9,1... | collective-permute-start | bytes 393224 | tf_op jit(solution)/shard_map/ppermute | solution.py:140
  17.0 5.8 %collective-permute-done.1.refs_1_ = bf16[16,2,8,256]{3,2,1,0:T(8,128)(2,1)S(1)} collective-permute-done((bf16[16,2,8,256]{3,2,1,0:T(8,128)(2,1)S(1)}, bf16[16,2,8,256]{3,2,1,0:T(8,128)(2,1)S(1)}, u32[]{:S(2)}, u32[]{:S(2)}) %collective-permute-start.1) | collective-permute-done | bytes 131104 | tf_op jit(solution)/shard_map/ppermute | solution.py:140
  22.8 0.7 %join.1 = bf16[16,2,2,8,256]{4,3,2,1,0:T(8,128)(2,1)} custom-call(bf16[16,2,8,256]{3,2,1,0:T(8,128)(2,1)S(1)} %get-tuple-element.9.refs_0_, bf16[16,2,8,256]{3,2,1,0:T(8,128)(2,1)S(1)} %collective-permute-done.1.refs_1_), custom_call_target="tpu_custom_call" | custom-call | tf_op jit(solution)/shard_map/join/pallas_call | solution.py:161
  23.5 0.0 all-to-all-done.r_ref
  23.5 7.4 %all-to-all-start.2 = ((bf16[16,2,2,8,256]{4,3,2,1,0:T(8,128)(2,1)}), bf16[16,2,2,8,256]{4,3,2,1,0:T(8,128)(2,1)S(1)}, u32[]{:S(2)}, u32[]{:S(2)}) async-start(bf16[16,2,2,8,256]{4,3,2,1,0:T(8,128)(2,1)} %join.1), calls=%async_computation.2 | async-start | bytes 524288 | tf_op jit(solution)/shard_map/all_to_all | solution.py:143
  30.9 0.0 copy-start.4
  30.9 0.0 copy-start.5
  31.0 6.7 %collective-permute-start = (bf16[2,8,16,512]{3,2,1,0:T(8,128)(2,1)S(1)}, bf16[2,8,16,512]{3,2,1,0:T(8,128)(2,1)S(1)}, u32[]{:S(2)}, u32[]{:S(2)}) collective-permute-start(bf16[2,8,16,512]{3,2,1,0:T(8,128)(2,1)S(1)} %flux.1.own_ref), channel_id=1, source_target_pairs={{0,32},{32,0},{1,33},{33,1},{2,34},{34,2},{3,35},{35,3},{4,36},{36... | collective-permute-start | bytes 786440 | tf_op jit(solution)/shard_map/ppermute | solution.py:140
  37.7 0.4 all-to-all-done.2.r_ref
  38.1 0.0 copy-done.4
  38.1 0.0 copy-done.5
  38.1 1.0 %zmath.1 = bf16[32,8,256]{2,1,0:T(8,128)(2,1)} custom-call(s32[1]{0:T(128)} %bitcast.2.low_ref, bf16[16,2,2,8,256]{4,3,2,1,0:T(8,128)(2,1)S(1)} %all-to-all-done.2.r_ref, bf16[256,256]{1,0:T(8,128)(2,1)S(1)} %copy-done.4, bf16[256,256]{1,0:T(8,128)(2,1)S(1)} %copy-done.5), custom_call_target="tpu_custom_call" | custom-call | tf_op jit(solution)/shard_map/zmath/pallas_call | solution.py:192
  39.1 0.0 copy-start.2
  39.1 0.0 copy-start.3
  39.1 6.1 %all-to-all-start.3 = ((bf16[32,8,256]{2,1,0:T(8,128)(2,1)}), bf16[32,8,256]{2,1,0:T(8,128)(2,1)S(1)}, u32[]{:S(2)}, u32[]{:S(2)}) async-start(bf16[32,8,256]{2,1,0:T(8,128)(2,1)} %zmath.1), calls=%async_computation.3 | async-start | bytes 262144 | tf_op jit(solution)/shard_map/all_to_all | solution.py:143
  45.2 0.0 copy-done.2
  45.2 0.0 copy-done.3
  45.2 0.0 copy-start
  45.2 0.0 copy-start.1
  45.3 1.6 %collective-permute-done.other_ref = bf16[2,8,16,512]{3,2,1,0:T(8,128)(2,1)S(1)} collective-permute-done((bf16[2,8,16,512]{3,2,1,0:T(8,128)(2,1)S(1)}, bf16[2,8,16,512]{3,2,1,0:T(8,128)(2,1)S(1)}, u32[]{:S(2)}, u32[]{:S(2)}) %collective-permute-start) | collective-permute-done | bytes 262176 | tf_op jit(solution)/shard_map/ppermute | solution.py:140
  46.8 1.0 %ymath.1 = bf16[8,16,512]{2,1,0:T(8,128)(2,1)} custom-call(s32[1]{0:T(128)} %bitcast.1.high_ref, bf16[8,2,16,512]{3,2,1,0:T(8,128)(2,1)S(1)} %all-to-all-done.r_ref, bf16[2,8,16,512]{3,2,1,0:T(8,128)(2,1)S(1)} %flux.1.own_ref, bf16[2,8,16,512]{3,2,1,0:T(8,128)(2,1)S(1)} %collective-permute-done.other_ref, bf16[2,8,16,256]{3,2,1,0:T(8,128)(2,1)S(1)} %rows.1.rows_ref), custom_call_target="tpu_custom_call" | custom-call | tf_op jit(solution)/shard_map/ymath/pallas_call | solution.py:201
  47.8 8.9 %all-to-all-done.3 = bf16[32,8,256]{2,1,0:T(8,128)(2,1)S(1)} async-done(((bf16[32,8,256]{2,1,0:T(8,128)(2,1)}), bf16[32,8,256]{2,1,0:T(8,128)(2,1)S(1)}, u32[]{:S(2)}, u32[]{:S(2)}) %all-to-all-start.3) | async-done | bytes 131104 | tf_op jit(solution)/shard_map/all_to_all | solution.py:143
  56.7 5.9 %all-to-all-start.1 = ((bf16[8,16,512]{2,1,0:T(8,128)(2,1)}), bf16[8,16,512]{2,1,0:T(8,128)(2,1)S(1)}, u32[]{:S(2)}, u32[]{:S(2)}) async-start(bf16[8,16,512]{2,1,0:T(8,128)(2,1)} %ymath.1), calls=%async_computation.1 | async-start | bytes 262144 | tf_op jit(solution)/shard_map/all_to_all | solution.py:143
  62.5 0.0 copy-done
  62.5 0.0 copy-done.1
  62.6 1.6 %xmath.1.base_ref = f32[16,8,512]{2,1,0:T(8,128)S(1)} custom-call(f32[16,8,512]{2,1,0:T(8,128)} %bitcast.11, bf16[3,16,8,512]{3,2,1,0:T(8,128)(2,1)} %w_ref.1, bf16[512,512]{1,0:T(8,128)(2,1)S(1)} %copy-done, bf16[512,512]{1,0:T(8,128)(2,1)S(1)} %copy-done.1), custom_call_target="tpu_custom_call" | custom-call | tf_op jit(solution)/shard_map/xmath/pallas_call | solution.py:177
  64.2 6.2 %all-to-all-done.1.y_ref = bf16[8,16,512]{2,1,0:T(8,128)(2,1)S(1)} async-done(((bf16[8,16,512]{2,1,0:T(8,128)(2,1)}), bf16[8,16,512]{2,1,0:T(8,128)(2,1)S(1)}, u32[]{:S(2)}, u32[]{:S(2)}) %all-to-all-start.1) | async-done | bytes 131104 | tf_op jit(solution)/shard_map/all_to_all | solution.py:143
  70.4 0.8 %last.1 = f32[16,8,512]{2,1,0:T(8,128)} custom-call(f32[16,8,512]{2,1,0:T(8,128)S(1)} %xmath.1.base_ref, bf16[8,16,512]{2,1,0:T(8,128)(2,1)S(1)} %all-to-all-done.1.y_ref, bf16[4,2,4,8,256]{4,3,2,1,0:T(8,128)(2,1)S(1)} %bitcast.7), custom_call_target="tpu_custom_call" | custom-call | tf_op jit(solution)/shard_map/last/pallas_call | solution.py:210
  (2 shorter events, 0.1 us)
Async XLA Ops:
  1.9 21.6 %all-to-all-start = ((bf16[8,2,16,512]{3,2,1,0:T(8,128)(2,1)}), bf16[8,2,16,512]{3,2,1,0:T(8,128)(2,1)S(1)}, u32[]{:S(2)}, u32[]{:S(2)}) async-start(bf16[8,2,16,512]{3,2,1,0:T(8,128)(2,1)} %get-tuple-element.8), calls=%async_computation | async-start | bytes 524288 | tf_op jit(solution)/shard_map/all_to_all | solution.py:143
  12.8 10.0 %collective-permute-start.1 = (bf16[16,2,8,256]{3,2,1,0:T(8,128)(2,1)S(1)}, bf16[16,2,8,256]{3,2,1,0:T(8,128)(2,1)S(1)}, u32[]{:S(2)}, u32[]{:S(2)}) collective-permute-start(bf16[16,2,8,256]{3,2,1,0:T(8,128)(2,1)S(1)} %get-tuple-element.10), channel_id=1, source_target_pairs={{0,4},{4,0},{1,5},{5,1},{2,6},{6,2},{3,7},{7,3},{8,12},{12,8},{9,1... | collective-permute-start | bytes 393224 | tf_op jit(solution)/shard_map/ppermute | solution.py:140
  23.5 14.6 %all-to-all-start.2 = ((bf16[16,2,2,8,256]{4,3,2,1,0:T(8,128)(2,1)}), bf16[16,2,2,8,256]{4,3,2,1,0:T(8,128)(2,1)S(1)}, u32[]{:S(2)}, u32[]{:S(2)}) async-start(bf16[16,2,2,8,256]{4,3,2,1,0:T(8,128)(2,1)} %join.1), calls=%async_computation.2 | async-start | bytes 524288 | tf_op jit(solution)/shard_map/all_to_all | solution.py:143
  30.9 7.2 %copy-start.4 = (bf16[256,256]{1,0:T(8,128)(2,1)S(1)}, bf16[256,256]{1,0:T(8,128)(2,1)}, u32[]{:S(2)}) copy-start(bf16[256,256]{1,0:T(8,128)(2,1)} %first_ref.3) | copy-start | bytes 393220
  30.9 7.2 %copy-start.5 = (bf16[256,256]{1,0:T(8,128)(2,1)S(1)}, bf16[256,256]{1,0:T(8,128)(2,1)}, u32[]{:S(2)}) copy-start(bf16[256,256]{1,0:T(8,128)(2,1)} %second_ref.3) | copy-start | bytes 393220
  31.0 15.8 %collective-permute-start = (bf16[2,8,16,512]{3,2,1,0:T(8,128)(2,1)S(1)}, bf16[2,8,16,512]{3,2,1,0:T(8,128)(2,1)S(1)}, u32[]{:S(2)}, u32[]{:S(2)}) collective-permute-start(bf16[2,8,16,512]{3,2,1,0:T(8,128)(2,1)S(1)} %flux.1.own_ref), channel_id=1, source_target_pairs={{0,32},{32,0},{1,33},{33,1},{2,34},{34,2},{3,35},{35,3},{4,36},{36... | collective-permute-start | bytes 786440 | tf_op jit(solution)/shard_map/ppermute | solution.py:140
  39.1 6.1 %copy-start.2 = (bf16[256,256]{1,0:T(8,128)(2,1)S(1)}, bf16[256,256]{1,0:T(8,128)(2,1)}, u32[]{:S(2)}) copy-start(bf16[256,256]{1,0:T(8,128)(2,1)} %param.12) | copy-start | bytes 393220
  39.1 6.1 %copy-start.3 = (bf16[256,256]{1,0:T(8,128)(2,1)S(1)}, bf16[256,256]{1,0:T(8,128)(2,1)}, u32[]{:S(2)}) copy-start(bf16[256,256]{1,0:T(8,128)(2,1)} %param.13) | copy-start | bytes 393220
  39.1 17.6 %all-to-all-start.3 = ((bf16[32,8,256]{2,1,0:T(8,128)(2,1)}), bf16[32,8,256]{2,1,0:T(8,128)(2,1)S(1)}, u32[]{:S(2)}, u32[]{:S(2)}) async-start(bf16[32,8,256]{2,1,0:T(8,128)(2,1)} %zmath.1), calls=%async_computation.3 | async-start | bytes 262144 | tf_op jit(solution)/shard_map/all_to_all | solution.py:143
  45.2 17.3 %copy-start = (bf16[512,512]{1,0:T(8,128)(2,1)S(1)}, bf16[512,512]{1,0:T(8,128)(2,1)}, u32[]{:S(2)}) copy-start(bf16[512,512]{1,0:T(8,128)(2,1)} %first_ref.2) | copy-start | bytes 1572868
  45.2 17.3 %copy-start.1 = (bf16[512,512]{1,0:T(8,128)(2,1)S(1)}, bf16[512,512]{1,0:T(8,128)(2,1)}, u32[]{:S(2)}) copy-start(bf16[512,512]{1,0:T(8,128)(2,1)} %second_ref.2) | copy-start | bytes 1572868
  56.7 13.8 %all-to-all-start.1 = ((bf16[8,16,512]{2,1,0:T(8,128)(2,1)}), bf16[8,16,512]{2,1,0:T(8,128)(2,1)S(1)}, u32[]{:S(2)}, u32[]{:S(2)}) async-start(bf16[8,16,512]{2,1,0:T(8,128)(2,1)} %ymath.1), calls=%async_computation.1 | async-start | bytes 262144 | tf_op jit(solution)/shard_map/all_to_all | solution.py:143

commit v7 on v5

--- a/solution.py
+++ b/solution.py
@@ -30,9 +30,19 @@
     return -0.5 * (c * product(first, s) + product(first, flux)) + 0.5 * product(second, s)
 
 
-def pack_kernel(low_ref, s_ref, v_ref, w_ref, row_ref, *rest):
-    pieces, (s32, v32) = rest[:-2], rest[-2:]
+def pack_kernel(s_ref, v_ref, row_ref, s32, v32):
     ny, nz, nx = s_ref.shape
+    for t in range(nx // LANES):
+        lanes = slice(t * LANES, (t + 1) * LANES)
+        s32[t] = s_ref[:, :, lanes].reshape(ny * nz, LANES)
+        v32[t] = v_ref[:, :, lanes].astype(F32).reshape(ny * nz, LANES)
+        for z in range(nz):
+            row_ref[z, 0, :, lanes] = s32[t, pl.ds(z, ny, stride=nz), :].astype(BF16)
+            row_ref[z, 1, :, lanes] = v32[t, pl.ds(z, ny, stride=nz), :].astype(BF16)
+
+
+def pieces_kernel(low_ref, s_ref, w_ref, *pieces):
+    ny, _, nx = s_ref.shape
     half = nx // 2
     group = ny // len(pieces)
     low = low_ref[0]
@@ -43,13 +53,6 @@
                 lanes = slice(h * half, (h + 1) * half)
                 piece[2 * q + h, 0] = s_ref[y, :, lanes].astype(BF16)
                 piece[2 * q + h, 1] = w_ref[y, :, lanes]
-    for t in range(nx // LANES):
-        lanes = slice(t * LANES, (t + 1) * LANES)
-        s32[t] = s_ref[:, :, lanes].reshape(ny * nz, LANES)
-        v32[t] = v_ref[:, :, lanes].astype(F32).reshape(ny * nz, LANES)
-        for z in range(nz):
-            row_ref[z, 0, :, lanes] = s32[t, pl.ds(z, ny, stride=nz), :].astype(BF16)
-            row_ref[z, 1, :, lanes] = v32[t, pl.ds(z, ny, stride=nz), :].astype(BF16)
 
 
 def join_kernel(*refs):
@@ -71,7 +74,13 @@
     out_ref[...] = (s + 0.5 * term).reshape(ny, nz, nx)
 
 
-def y_kernel(high_ref, r_ref, own_ref, other_ref, first_ref, second_ref, out_ref, lines):
+def rows_kernel(high_ref, first_ref, second_ref, out_ref):
+    high = high_ref[0]
+    out_ref[0] = first_ref[:, high]
+    out_ref[1] = second_ref[:, high]
+
+
+def y_kernel(high_ref, r_ref, own_ref, other_ref, rows_ref, out_ref, lines):
     _, blocks, depth, lanes = own_ref.shape
     high = high_ref[0]
     length = 2 * blocks * depth
@@ -79,8 +88,8 @@
     lines[:, :, 1 - high] = other_ref[...]
     s = lines[0].reshape(length, lanes)
     flux = lines[1].reshape(length, lanes)
-    first = first_ref[:, high].reshape(blocks * depth, length)
-    second = second_ref[:, high].reshape(blocks * depth, length)
+    first = rows_ref[0].reshape(blocks * depth, length)
+    second = rows_ref[1].reshape(blocks * depth, length)
     c = r_ref[:, 1].reshape(blocks * depth, lanes).astype(F32)
     term = -0.5 * (c * dot(first, s, 0) + dot(first, flux, 0)) + 0.5 * dot(second, s, 0)
     out_ref[...] = term.astype(BF16).reshape(blocks, depth, lanes)
@@ -145,16 +154,24 @@
     def rows_split(matrix):
         return near(matrix.reshape(blocks, 2, ny, matrix.shape[1]))
 
-    row_send, keep, *give = pl.pallas_call(
+    row_send = pl.pallas_call(
         pack_kernel,
         grid=(1,),
-        in_specs=[SMEM, whole, component(velocity.shape, 1), component(velocity.shape, 2)],
-        out_specs=[VMEM] * (1 + lows),
-        out_shape=[pltpu.VMEM((blocks, 2, ny, nx), BF16)] + [pltpu.VMEM((peers, 2, nz, half), BF16)] * lows,
+        in_specs=[whole, component(velocity.shape, 1)],
+        out_specs=VMEM,
+        out_shape=pltpu.VMEM((blocks, 2, ny, nx), BF16),
         scratch_shapes=[pltpu.VMEM((nx // LANES, ny * nz, LANES), F32)] * 2,
         name="pack",
-    )(low, s, velocity, velocity)
+    )(s, velocity)
     row_in = near(exchange(row_send, "z"))
+    keep, *give = pl.pallas_call(
+        pieces_kernel,
+        grid=(1,),
+        in_specs=[SMEM, whole, component(velocity.shape, 2)],
+        out_specs=[VMEM] * lows,
+        out_shape=[pltpu.VMEM((peers, 2, nz, half), BF16)] * lows,
+        name="pieces",
+    )(low, s, velocity)
     got = []
     for j, piece in enumerate(give, 1):
         got.append(near(swap(piece, "m", j)))
@@ -182,6 +199,13 @@
         out_shape=pltpu.VMEM((ny, nz, nx), F32),
         name="xmath",
     )(s, velocity, near(first_x), near(second_x))
+    rows = pl.pallas_call(
+        rows_kernel,
+        in_specs=[SMEM] + [VMEM] * 2,
+        out_specs=VMEM,
+        out_shape=pltpu.VMEM((2, blocks, ny, first_y.shape[1]), BF16),
+        name="rows",
+    )(high, rows_split(first_y), rows_split(second_y))
     z_term = pl.pallas_call(
         z_kernel,
         in_specs=[SMEM] + [VMEM] * 3,
@@ -196,12 +220,12 @@
     z_back = exchange(z_term, ("x", "l", "c"))
     y_term = pl.pallas_call(
         y_kernel,
-        in_specs=[SMEM] + [VMEM] * 5,
+        in_specs=[SMEM] + [VMEM] * 4,
         out_specs=VMEM,
         out_shape=pltpu.VMEM((blocks, ny, nx), BF16),
         scratch_shapes=[pltpu.VMEM((2, blocks, 2, ny, nx), BF16)],
         name="ymath",
-    )(high, row_in, near(own), near(other), rows_split(first_y), rows_split(second_y))
+    )(high, row_in, near(own), near(other), near(rows))
     y_back = exchange(y_term, "z")
     returned = []
     for j in range(1, lows):

time: 70.2 us -> 71.1 us (1.013)
  Pallas kernels: 7.03 us -> 7.96 us
    pallas_call x2 -> x4, Pallas kernels: 2.89 us -> 3.82 us  [the longest x1 1.83 us: body(): pl.pallas_call(pack_kernel, grid=(1,), in_specs=[whole, component(velocit...]
  transfers between devices with their start and end apart: 7 -> 7, of which waited for: 5 -> 5; matrix products, arithmetic and copies ran while one was open for 0% -> 0% of each run, Pallas kernels for 6% -> 8%
where the time goes in v7:
time: 71.1 us; the launch traced here: 70.5 us
  starting transfers between devices  43.5 us (61%)
  waiting for transfers between devices  18.9 us (27%)
  Pallas kernels  7.96 us (11%)
    all_to_all x4, starting transfers between devices, exchange(): return lax.all_to_all(array, axes, split_axis=0, concat_axis=0, tiled=True)  29.9 us
    ppermute x3, starting transfers between devices, swap(): lax.ppermute(array, axis, [(i, i ^ j) for i in range(lax.axis_size(axis))])  13.6 us
    ppermute x3, waiting for transfers between devices, swap(): lax.ppermute(array, axis, [(i, i ^ j) for i in range(lax.axis_size(axis))])  11.8 us
    all_to_all x4, waiting for transfers between devices, exchange(): return lax.all_to_all(array, axes, split_axis=0, concat_axis=0, tiled=True)  7.1 us
    pallas_call x1, Pallas kernels, body(): pl.pallas_call(pack_kernel, grid=(1,), in_specs=[whole, component(velocit...  1.83 us
    pallas_call x1, Pallas kernels, body(): pl.pallas_call(x_kernel, grid=(1,), in_specs=[whole, component(velocity.s...  1.64 us
  transfers between devices with their start and end apart: 7, of which 5 were waited for; matrix products, arithmetic and copies ran while one was open for 0% of the time, Pallas kernels for 8%

profile of v7, /device:TPU:1, one launch (start us, length us, event | category | flops | bytes accessed | tf_op | source)
XLA Modules:
  0.0 70.5 jit_solution(2061427342705370017)
XLA Ops:
  0.0 1.8 %pack.1 = bf16[8,2,16,512]{3,2,1,0:T(8,128)(2,1)} custom-call(f32[16,8,512]{2,1,0:T(8,128)} %bitcast.12, bf16[3,16,8,512]{3,2,1,0:T(8,128)(2,1)} %w_ref.1), custom_call_target="tpu_custom_call" | custom-call | tf_op jit(solution)/shard_map/pack/pallas_call | solution.py:157
  1.8 10.9 %all-to-all-start = ((bf16[8,2,16,512]{3,2,1,0:T(8,128)(2,1)}), bf16[8,2,16,512]{3,2,1,0:T(8,128)(2,1)S(1)}, u32[]{:S(2)}, u32[]{:S(2)}) async-start(bf16[8,2,16,512]{3,2,1,0:T(8,128)(2,1)} %pack.1), calls=%async_computation | async-start | bytes 524288 | tf_op jit(solution)/shard_map/all_to_all | solution.py:152
  12.7 1.0 %pieces.1 = (bf16[16,2,8,256]{3,2,1,0:T(8,128)(2,1)S(1)}, bf16[16,2,8,256]{3,2,1,0:T(8,128)(2,1)S(1)}) custom-call(s32[1]{0:T(128)} %bitcast.low_ref, f32[16,8,512]{2,1,0:T(8,128)} %bitcast.13, bf16[3,16,8,512]{3,2,1,0:T(8,128)(2,1)} %w_ref.1), custom_call_target="tpu_custom_call" | custom-call | tf_op jit(solution)/shard_map/pieces/pallas_call | solution.py:167
  13.7 4.2 %collective-permute-start.1 = (bf16[16,2,8,256]{3,2,1,0:T(8,128)(2,1)S(1)}, bf16[16,2,8,256]{3,2,1,0:T(8,128)(2,1)S(1)}, u32[]{:S(2)}, u32[]{:S(2)}) collective-permute-start(bf16[16,2,8,256]{3,2,1,0:T(8,128)(2,1)S(1)} %get-tuple-element.8), channel_id=1, source_target_pairs={{0,4},{4,0},{1,5},{5,1},{2,6},{6,2},{3,7},{7,3},{8,12},{12,8},{9,1... | collective-permute-start | bytes 393224 | tf_op jit(solution)/shard_map/ppermute | solution.py:149
  17.9 5.8 %collective-permute-done.1.refs_1_ = bf16[16,2,8,256]{3,2,1,0:T(8,128)(2,1)S(1)} collective-permute-done((bf16[16,2,8,256]{3,2,1,0:T(8,128)(2,1)S(1)}, bf16[16,2,8,256]{3,2,1,0:T(8,128)(2,1)S(1)}, u32[]{:S(2)}, u32[]{:S(2)}) %collective-permute-start.1) | collective-permute-done | bytes 131104 | tf_op jit(solution)/shard_map/ppermute | solution.py:149
  23.7 0.7 %join.1 = bf16[16,2,2,8,256]{4,3,2,1,0:T(8,128)(2,1)} custom-call(bf16[16,2,8,256]{3,2,1,0:T(8,128)(2,1)S(1)} %get-tuple-element.7.refs_0_, bf16[16,2,8,256]{3,2,1,0:T(8,128)(2,1)S(1)} %collective-permute-done.1.refs_1_), custom_call_target="tpu_custom_call" | custom-call | tf_op jit(solution)/shard_map/join/pallas_call | solution.py:178
  24.4 0.0 all-to-all-done.r_ref
  24.4 6.4 %all-to-all-start.2 = ((bf16[16,2,2,8,256]{4,3,2,1,0:T(8,128)(2,1)}), bf16[16,2,2,8,256]{4,3,2,1,0:T(8,128)(2,1)S(1)}, u32[]{:S(2)}, u32[]{:S(2)}) async-start(bf16[16,2,2,8,256]{4,3,2,1,0:T(8,128)(2,1)} %join.1), calls=%async_computation.2 | async-start | bytes 524288 | tf_op jit(solution)/shard_map/all_to_all | solution.py:152
  30.8 0.0 copy-start.4
  30.9 0.0 copy-start.5
  30.9 7.0 %collective-permute-start = (bf16[2,8,16,512]{3,2,1,0:T(8,128)(2,1)S(1)}, bf16[2,8,16,512]{3,2,1,0:T(8,128)(2,1)S(1)}, u32[]{:S(2)}, u32[]{:S(2)}) collective-permute-start(bf16[2,8,16,512]{3,2,1,0:T(8,128)(2,1)S(1)} %flux.1.own_ref), channel_id=1, source_target_pairs={{0,32},{32,0},{1,33},{33,1},{2,34},{34,2},{3,35},{35,3},{4,36},{36... | collective-permute-start | bytes 786440 | tf_op jit(solution)/shard_map/ppermute | solution.py:149
  37.9 0.1 all-to-all-done.2.r_ref
  38.0 0.0 copy-done.4
  38.0 0.0 copy-done.5
  38.0 1.0 %zmath.1 = bf16[16,2,8,256]{3,2,1,0:T(8,128)(2,1)} custom-call(s32[1]{0:T(128)} %bitcast.low_ref, bf16[16,2,2,8,256]{4,3,2,1,0:T(8,128)(2,1)S(1)} %all-to-all-done.2.r_ref, bf16[256,256]{1,0:T(8,128)(2,1)S(1)} %copy-done.4, bf16[256,256]{1,0:T(8,128)(2,1)S(1)} %copy-done.5), custom_call_target="tpu_custom_call" | custom-call | tf_op jit(solution)/shard_map/zmath/pallas_call | solution.py:209
  39.0 0.0 copy-start.2
  39.0 0.0 copy-start.3
  39.0 6.0 %all-to-all-start.3 = ((bf16[16,2,8,256]{3,2,1,0:T(8,128)(2,1)}), bf16[16,2,8,256]{3,2,1,0:T(8,128)(2,1)S(1)}, u32[]{:S(2)}, u32[]{:S(2)}) async-start(bf16[16,2,8,256]{3,2,1,0:T(8,128)(2,1)} %zmath.1), calls=%async_computation.3 | async-start | bytes 262144 | tf_op jit(solution)/shard_map/all_to_all | solution.py:152
  45.0 0.0 copy-done.2
  45.0 0.0 copy-done.3
  45.1 0.0 copy-start
  45.1 0.0 copy-start.1
  45.1 2.0 %collective-permute-done.other_ref = bf16[2,8,16,512]{3,2,1,0:T(8,128)(2,1)S(1)} collective-permute-done((bf16[2,8,16,512]{3,2,1,0:T(8,128)(2,1)S(1)}, bf16[2,8,16,512]{3,2,1,0:T(8,128)(2,1)S(1)}, u32[]{:S(2)}, u32[]{:S(2)}) %collective-permute-start) | collective-permute-done | bytes 262176 | tf_op jit(solution)/shard_map/ppermute | solution.py:149
  47.1 1.0 %ymath.1 = bf16[8,16,512]{2,1,0:T(8,128)(2,1)} custom-call(s32[1]{0:T(128)} %bitcast.2.high_ref, bf16[8,2,16,512]{3,2,1,0:T(8,128)(2,1)S(1)} %all-to-all-done.r_ref, bf16[2,8,16,512]{3,2,1,0:T(8,128)(2,1)S(1)} %flux.1.own_ref, bf16[2,8,16,512]{3,2,1,0:T(8,128)(2,1)S(1)} %collective-permute-done.other_ref, bf16[2,8,16,256]{3,2,1,0:T(8,128)(2,1)S(1)} %rows.1.rows_ref), custom_call_target="tpu_custom_call" | custom-call | tf_op jit(solution)/shard_map/ymath/pallas_call | solution.py:221
  48.1 7.0 %all-to-all-done.3.own_ref = bf16[16,2,8,256]{3,2,1,0:T(8,128)(2,1)S(1)} async-done(((bf16[16,2,8,256]{3,2,1,0:T(8,128)(2,1)}), bf16[16,2,8,256]{3,2,1,0:T(8,128)(2,1)S(1)}, u32[]{:S(2)}, u32[]{:S(2)}) %all-to-all-start.3) | async-done | bytes 131104 | tf_op jit(solution)/shard_map/all_to_all | solution.py:152
  55.0 6.6 %all-to-all-start.1 = ((bf16[8,16,512]{2,1,0:T(8,128)(2,1)}), bf16[8,16,512]{2,1,0:T(8,128)(2,1)S(1)}, u32[]{:S(2)}, u32[]{:S(2)}) async-start(bf16[8,16,512]{2,1,0:T(8,128)(2,1)} %ymath.1), calls=%async_computation.1 | async-start | bytes 262144 | tf_op jit(solution)/shard_map/all_to_all | solution.py:152
  61.7 2.4 %collective-permute-start.2 = (bf16[16,8,256]{2,1,0:T(8,128)(2,1)S(1)}, bf16[16,8,256]{2,1,0:T(8,128)(2,1)S(1)}, u32[]{:S(2)}, u32[]{:S(2)}) collective-permute-start(bf16[16,8,256]{2,1,0:T(8,128)(2,1)S(1)} %slice_bitcast_fusion), channel_id=1, source_target_pairs={{0,4},{4,0},{1,5},{5,1},{2,6},{6,2},{3,7},{7,3},{8,12},{12,8},{9,1... | collective-permute-start | bytes 196616 | tf_op jit(solution)/shard_map/ppermute | solution.py:149
  64.1 0.0 copy-done
  64.1 0.0 copy-done.1
  64.1 1.6 %xmath.1.base_ref = f32[16,8,512]{2,1,0:T(8,128)S(1)} custom-call(f32[16,8,512]{2,1,0:T(8,128)} %bitcast.14, bf16[3,16,8,512]{3,2,1,0:T(8,128)(2,1)} %w_ref.1, bf16[512,512]{1,0:T(8,128)(2,1)S(1)} %copy-done, bf16[512,512]{1,0:T(8,128)(2,1)S(1)} %copy-done.1), custom_call_target="tpu_custom_call" | custom-call | tf_op jit(solution)/shard_map/xmath/pallas_call | solution.py:194
  65.7 4.0 %collective-permute-done.2.rest_0_ = bf16[16,8,256]{2,1,0:T(8,128)(2,1)S(1)} collective-permute-done((bf16[16,8,256]{2,1,0:T(8,128)(2,1)S(1)}, bf16[16,8,256]{2,1,0:T(8,128)(2,1)S(1)}, u32[]{:S(2)}, u32[]{:S(2)}) %collective-permute-start.2) | collective-permute-done | bytes 65568 | tf_op jit(solution)/shard_map/ppermute | solution.py:149
  69.7 0.0 all-to-all-done.1.y_ref
  69.7 0.8 %last.1 = f32[16,8,512]{2,1,0:T(8,128)} custom-call(s32[1]{0:T(128)} %bitcast.low_ref, f32[16,8,512]{2,1,0:T(8,128)S(1)} %xmath.1.base_ref, bf16[8,16,512]{2,1,0:T(8,128)(2,1)S(1)} %all-to-all-done.1.y_ref, bf16[16,2,8,256]{3,2,1,0:T(8,128)(2,1)S(1)} %all-to-all-done.3.own_ref, bf16[16,8,256]{2,1,0:T(8,128)(2,1)S(1)} %collective-permute-done.2.rest_0_), custom_call_target="tpu_custom_call" | custom-call | tf_op jit(solution)/shard_map/last/pallas_call | solution.py:233
  (3 shorter events, 0.1 us)
Async XLA Ops:
  1.8 22.6 %all-to-all-start = ((bf16[8,2,16,512]{3,2,1,0:T(8,128)(2,1)}), bf16[8,2,16,512]{3,2,1,0:T(8,128)(2,1)S(1)}, u32[]{:S(2)}, u32[]{:S(2)}) async-start(bf16[8,2,16,512]{3,2,1,0:T(8,128)(2,1)} %pack.1), calls=%async_computation | async-start | bytes 524288 | tf_op jit(solution)/shard_map/all_to_all | solution.py:152
  13.7 10.0 %collective-permute-start.1 = (bf16[16,2,8,256]{3,2,1,0:T(8,128)(2,1)S(1)}, bf16[16,2,8,256]{3,2,1,0:T(8,128)(2,1)S(1)}, u32[]{:S(2)}, u32[]{:S(2)}) collective-permute-start(bf16[16,2,8,256]{3,2,1,0:T(8,128)(2,1)S(1)} %get-tuple-element.8), channel_id=1, source_target_pairs={{0,4},{4,0},{1,5},{5,1},{2,6},{6,2},{3,7},{7,3},{8,12},{12,8},{9,1... | collective-permute-start | bytes 393224 | tf_op jit(solution)/shard_map/ppermute | solution.py:149
  24.4 13.6 %all-to-all-start.2 = ((bf16[16,2,2,8,256]{4,3,2,1,0:T(8,128)(2,1)}), bf16[16,2,2,8,256]{4,3,2,1,0:T(8,128)(2,1)S(1)}, u32[]{:S(2)}, u32[]{:S(2)}) async-start(bf16[16,2,2,8,256]{4,3,2,1,0:T(8,128)(2,1)} %join.1), calls=%async_computation.2 | async-start | bytes 524288 | tf_op jit(solution)/shard_map/all_to_all | solution.py:152
  30.8 7.2 %copy-start.4 = (bf16[256,256]{1,0:T(8,128)(2,1)S(1)}, bf16[256,256]{1,0:T(8,128)(2,1)}, u32[]{:S(2)}) copy-start(bf16[256,256]{1,0:T(8,128)(2,1)} %first_ref.3) | copy-start | bytes 393220
  30.9 7.2 %copy-start.5 = (bf16[256,256]{1,0:T(8,128)(2,1)S(1)}, bf16[256,256]{1,0:T(8,128)(2,1)}, u32[]{:S(2)}) copy-start(bf16[256,256]{1,0:T(8,128)(2,1)} %second_ref.3) | copy-start | bytes 393220
  30.9 16.2 %collective-permute-start = (bf16[2,8,16,512]{3,2,1,0:T(8,128)(2,1)S(1)}, bf16[2,8,16,512]{3,2,1,0:T(8,128)(2,1)S(1)}, u32[]{:S(2)}, u32[]{:S(2)}) collective-permute-start(bf16[2,8,16,512]{3,2,1,0:T(8,128)(2,1)S(1)} %flux.1.own_ref), channel_id=1, source_target_pairs={{0,32},{32,0},{1,33},{33,1},{2,34},{34,2},{3,35},{35,3},{4,36},{36... | collective-permute-start | bytes 786440 | tf_op jit(solution)/shard_map/ppermute | solution.py:149
  39.0 6.0 %copy-start.2 = (bf16[256,256]{1,0:T(8,128)(2,1)S(1)}, bf16[256,256]{1,0:T(8,128)(2,1)}, u32[]{:S(2)}) copy-start(bf16[256,256]{1,0:T(8,128)(2,1)} %param.12) | copy-start | bytes 393220
  39.0 6.0 %copy-start.3 = (bf16[256,256]{1,0:T(8,128)(2,1)S(1)}, bf16[256,256]{1,0:T(8,128)(2,1)}, u32[]{:S(2)}) copy-start(bf16[256,256]{1,0:T(8,128)(2,1)} %param.13) | copy-start | bytes 393220
  39.0 16.0 %all-to-all-start.3 = ((bf16[16,2,8,256]{3,2,1,0:T(8,128)(2,1)}), bf16[16,2,8,256]{3,2,1,0:T(8,128)(2,1)S(1)}, u32[]{:S(2)}, u32[]{:S(2)}) async-start(bf16[16,2,8,256]{3,2,1,0:T(8,128)(2,1)} %zmath.1), calls=%async_computation.3 | async-start | bytes 262144 | tf_op jit(solution)/shard_map/all_to_all | solution.py:152
  45.1 19.0 %copy-start = (bf16[512,512]{1,0:T(8,128)(2,1)S(1)}, bf16[512,512]{1,0:T(8,128)(2,1)}, u32[]{:S(2)}) copy-start(bf16[512,512]{1,0:T(8,128)(2,1)} %first_ref.2) | copy-start | bytes 1572868
  45.1 19.0 %copy-start.1 = (bf16[512,512]{1,0:T(8,128)(2,1)S(1)}, bf16[512,512]{1,0:T(8,128)(2,1)}, u32[]{:S(2)}) copy-start(bf16[512,512]{1,0:T(8,128)(2,1)} %second_ref.2) | copy-start | bytes 1572868
  55.0 14.7 %all-to-all-start.1 = ((bf16[8,16,512]{2,1,0:T(8,128)(2,1)}), bf16[8,16,512]{2,1,0:T(8,128)(2,1)S(1)}, u32[]{:S(2)}, u32[]{:S(2)}) async-start(bf16[8,16,512]{2,1,0:T(8,128)(2,1)} %ymath.1), calls=%async_computation.1 | async-start | bytes 262144 | tf_op jit(solution)/shard_map/all_to_all | solution.py:152
  61.7 8.0 %collective-permute-start.2 = (bf16[16,8,256]{2,1,0:T(8,128)(2,1)S(1)}, bf16[16,8,256]{2,1,0:T(8,128)(2,1)S(1)}, u32[]{:S(2)}, u32[]{:S(2)}) collective-permute-start(bf16[16,8,256]{2,1,0:T(8,128)(2,1)S(1)} %slice_bitcast_fusion), channel_id=1, source_target_pairs={{0,4},{4,0},{1,5},{5,1},{2,6},{6,2},{3,7},{7,3},{8,12},{12,8},{9,1... | collective-permute-start | bytes 196616 | tf_op jit(solution)/shard_map/ppermute | solution.py:149

commit v8 on v5

--- a/solution.py
+++ b/solution.py
@@ -10,6 +10,7 @@
 LANES = 128
 VMEM = pl.BlockSpec(memory_space=pltpu.VMEM)
 SMEM = pl.BlockSpec(memory_space=pltpu.SMEM)
+HBM = pl.BlockSpec(memory_space=pltpu.HBM)
 BF16, F32 = jnp.bfloat16, jnp.float32
 
 
@@ -19,6 +20,10 @@
 
 def near(array):
     return pltpu.with_memory_space_constraint(array, pltpu.VMEM)
+
+
+def far(array):
+    return pltpu.with_memory_space_constraint(array, pltpu.HBM)
 
 
 def dot(a, b, side):
@@ -30,12 +35,34 @@
     return -0.5 * (c * product(first, s) + product(first, flux)) + 0.5 * product(second, s)
 
 
-def pack_kernel(low_ref, s_ref, v_ref, w_ref, row_ref, *rest):
-    pieces, (s32, v32) = rest[:-2], rest[-2:]
+def pack_kernel(low_ref, s_any, velocity_any, row_any, *rest):
+    pieces, (s_ref, v_ref, w_ref, row_ref, s32, v32, sems) = rest[:-7], rest[-7:]
     ny, nz, nx = s_ref.shape
     half = nx // 2
     group = ny // len(pieces)
     low = low_ref[0]
+    loads, stores = [], []
+    for h in range(2):
+        lanes = slice(h * half, (h + 1) * half)
+        loads.append(pltpu.make_async_copy(s_any.at[:, :, lanes], s_ref.at[:, :, lanes], sems.at[h]))
+        loads.append(pltpu.make_async_copy(velocity_any.at[1, :, :, lanes], v_ref.at[:, :, lanes], sems.at[2 + h]))
+        stores.append(pltpu.make_async_copy(row_ref.at[:, :, :, lanes], row_any.at[:, :, :, lanes], sems.at[4 + h]))
+    last = pltpu.make_async_copy(velocity_any.at[2], w_ref, sems.at[6])
+    for copy in loads:
+        copy.start()
+    last.start()
+    for h in range(2):
+        loads[2 * h].wait()
+        loads[2 * h + 1].wait()
+        for t in range(h * half // LANES, (h + 1) * half // LANES):
+            lanes = slice(t * LANES, (t + 1) * LANES)
+            s32[t] = s_ref[:, :, lanes].reshape(ny * nz, LANES)
+            v32[t] = v_ref[:, :, lanes].astype(F32).reshape(ny * nz, LANES)
+            for z in range(nz):
+                row_ref[z, 0, :, lanes] = s32[t, pl.ds(z, ny, stride=nz), :].astype(BF16)
+                row_ref[z, 1, :, lanes] = v32[t, pl.ds(z, ny, stride=nz), :].astype(BF16)
+        stores[h].start()
+    last.wait()
     for j, piece in enumerate(pieces):
         for q in range(group):
             y = (low ^ j) * group + q
@@ -43,18 +70,17 @@
                 lanes = slice(h * half, (h + 1) * half)
                 piece[2 * q + h, 0] = s_ref[y, :, lanes].astype(BF16)
                 piece[2 * q + h, 1] = w_ref[y, :, lanes]
-    for t in range(nx // LANES):
-        lanes = slice(t * LANES, (t + 1) * LANES)
-        s32[t] = s_ref[:, :, lanes].reshape(ny * nz, LANES)
-        v32[t] = v_ref[:, :, lanes].astype(F32).reshape(ny * nz, LANES)
-        for z in range(nz):
-            row_ref[z, 0, :, lanes] = s32[t, pl.ds(z, ny, stride=nz), :].astype(BF16)
-            row_ref[z, 1, :, lanes] = v32[t, pl.ds(z, ny, stride=nz), :].astype(BF16)
+    for copy in stores:
+        copy.wait()
 
 
 def join_kernel(*refs):
-    for j, piece in enumerate(refs[:-1]):
-        refs[-1][:, j] = piece[...]
+    pieces, (out_any, sems) = refs[:-2], refs[-2:]
+    copies = [pltpu.make_async_copy(piece, out_any.at[:, j], sems.at[j]) for j, piece in enumerate(pieces)]
+    for copy in copies:
+        copy.start()
+    for copy in copies:
+        copy.wait()
 
 
 def flux_kernel(r_ref, out_ref):
@@ -71,7 +97,15 @@
     out_ref[...] = (s + 0.5 * term).reshape(ny, nz, nx)
 
 
-def y_kernel(high_ref, r_ref, own_ref, other_ref, first_ref, second_ref, out_ref, lines):
+def rows_kernel(high_ref, first_ref, second_ref, first_z_ref, second_z_ref, out_ref, z_ref):
+    high = high_ref[0]
+    out_ref[0] = first_ref[:, high]
+    out_ref[1] = second_ref[:, high]
+    z_ref[0] = first_z_ref[...]
+    z_ref[1] = second_z_ref[...]
+
+
+def y_kernel(high_ref, r_ref, own_ref, other_ref, rows_ref, out_ref, lines):
     _, blocks, depth, lanes = own_ref.shape
     high = high_ref[0]
     length = 2 * blocks * depth
@@ -79,14 +113,14 @@
     lines[:, :, 1 - high] = other_ref[...]
     s = lines[0].reshape(length, lanes)
     flux = lines[1].reshape(length, lanes)
-    first = first_ref[:, high].reshape(blocks * depth, length)
-    second = second_ref[:, high].reshape(blocks * depth, length)
+    first = rows_ref[0].reshape(blocks * depth, length)
+    second = rows_ref[1].reshape(blocks * depth, length)
     c = r_ref[:, 1].reshape(blocks * depth, lanes).astype(F32)
     term = -0.5 * (c * dot(first, s, 0) + dot(first, flux, 0)) + 0.5 * dot(second, s, 0)
     out_ref[...] = term.astype(BF16).reshape(blocks, depth, lanes)
 
 
-def z_kernel(low_ref, r_ref, first_ref, second_ref, out_ref, lines, terms):
+def z_kernel(low_ref, r_ref, operators_ref, out_ref, lines, terms):
     _, nx_blocks, lows, cores, depth, lanes = lines.shape
     low = low_ref[0]
     length = nx_blocks * lows * cores * depth
@@ -97,7 +131,7 @@
                     lines[f, x, low ^ j, c] = r_ref[x * cores + c, j, f]
     s = lines[0].reshape(length, lanes)
     c = lines[1].reshape(length, lanes).astype(F32)
-    term = term_of(s, c, first_ref[...], second_ref[...], lambda m, f: dot(m, f, 0))
+    term = term_of(s, c, operators_ref[0], operators_ref[1], lambda m, f: dot(m, f, 0))
     terms[...] = term.astype(BF16).reshape(terms.shape)
     for x in range(nx_blocks):
         for j in range(lows):
@@ -147,13 +181,20 @@
 
     row_send, keep, *give = pl.pallas_call(
         pack_kernel,
-        grid=(1,),
-        in_specs=[SMEM, whole, component(velocity.shape, 1), component(velocity.shape, 2)],
-        out_specs=[VMEM] * (1 + lows),
-        out_shape=[pltpu.VMEM((blocks, 2, ny, nx), BF16)] + [pltpu.VMEM((peers, 2, nz, half), BF16)] * lows,
-        scratch_shapes=[pltpu.VMEM((nx // LANES, ny * nz, LANES), F32)] * 2,
+        in_specs=[SMEM, HBM, HBM],
+        out_specs=[HBM] + [VMEM] * lows,
+        out_shape=[pltpu.HBM((blocks, 2, ny, nx), BF16)] + [pltpu.VMEM((peers, 2, nz, half), BF16)] * lows,
+        scratch_shapes=[
+            pltpu.VMEM((ny, nz, nx), F32),
+            pltpu.VMEM((ny, nz, nx), BF16),
+            pltpu.VMEM((ny, nz, nx), BF16),
+            pltpu.VMEM((blocks, 2, ny, nx), BF16),
+            pltpu.VMEM((nx // LANES, ny * nz, LANES), F32),
+            pltpu.VMEM((nx // LANES, ny * nz, LANES), F32),
+            pltpu.SemaphoreType.DMA((7,)),
+        ],
         name="pack",
-    )(low, s, velocity, velocity)
+    )(low, far(s), far(velocity))
     row_in = near(exchange(row_send, "z"))
     got = []
     for j, piece in enumerate(give, 1):
@@ -161,11 +202,11 @@
     col_send = pl.pallas_call(
         join_kernel,
         in_specs=[VMEM] * lows,
-        out_specs=VMEM,
-        out_shape=pltpu.VMEM((peers, lows, 2, nz, half), BF16),
+        out_specs=HBM,
+        out_shape=pltpu.HBM((peers, lows, 2, nz, half), BF16),
+        scratch_shapes=[pltpu.SemaphoreType.DMA((lows,))],
         name="join",
     )(near(keep), *got)
-    col_in = exchange(col_send, ("x", "l", "c"))
     own = pl.pallas_call(
         flux_kernel,
         in_specs=[VMEM],
@@ -173,6 +214,8 @@
         out_shape=pltpu.VMEM((2, blocks, ny, nx), BF16),
         name="flux",
     )(row_in)
+    col_send, own = lax.optimization_barrier((col_send, own))
+    col_in = exchange(col_send, ("x", "l", "c"))
     other = swap(own, "h", 1)
     base = pl.pallas_call(
         x_kernel,
@@ -182,9 +225,19 @@
         out_shape=pltpu.VMEM((ny, nz, nx), F32),
         name="xmath",
     )(s, velocity, near(first_x), near(second_x))
+    rows, z_operators = pl.pallas_call(
+        rows_kernel,
+        in_specs=[SMEM] + [VMEM] * 4,
+        out_specs=[VMEM] * 2,
+        out_shape=[
+            pltpu.VMEM((2, blocks, ny, first_y.shape[1]), BF16),
+            pltpu.VMEM((2,) + first_z.shape, BF16),
+        ],
+        name="rows",
+    )(high, rows_split(first_y), rows_split(second_y), near(first_z), near(second_z))
     z_term = pl.pallas_call(
         z_kernel,
-        in_specs=[SMEM] + [VMEM] * 3,
+        in_specs=[SMEM] + [VMEM] * 2,
         out_specs=VMEM,
         out_shape=pltpu.VMEM((peers, lows, nz, half), BF16),
         scratch_shapes=[
@@ -192,16 +245,16 @@
             pltpu.VMEM((peers // cores, lows, cores, nz, half), BF16),
         ],
         name="zmath",
-    )(low, near(col_in), near(first_z), near(second_z))
+    )(low, near(col_in), near(z_operators))
     z_back = exchange(z_term, ("x", "l", "c"))
     y_term = pl.pallas_call(
         y_kernel,
-        in_specs=[SMEM] + [VMEM] * 5,
+        in_specs=[SMEM] + [VMEM] * 4,
         out_specs=VMEM,
         out_shape=pltpu.VMEM((blocks, ny, nx), BF16),
         scratch_shapes=[pltpu.VMEM((2, blocks, 2, ny, nx), BF16)],
         name="ymath",
-    )(high, row_in, near(own), near(other), rows_split(first_y), rows_split(second_y))
+    )(high, row_in, near(own), near(other), near(rows))
     y_back = exchange(y_term, "z")
     returned = []
     for j in range(1, lows):

time: 70.2 us -> 70 us (level)
    all_to_all x4, waiting for transfers between devices: 7.44 us -> 10.7 us  [exchange(): return lax.all_to_all(array, axes, split_axis=0, concat_axis=0, tiled=True)]
    ppermute x3, waiting for transfers between devices: 11.7 us -> 8.55 us  [swap(): lax.ppermute(array, axis, [(i, i ^ j) for i in range(lax.axis_size(axis))])]
    pallas_call x4 -> x5, Pallas kernels: 4.55 us -> 4.5 us  [the longest x1 1.79 us: body(): pl.pallas_call(pack_kernel, in_specs=[SMEM, HBM, HBM], out_specs=[HBM] +...]
  transfers between devices with their start and end apart: 7 -> 7, of which waited for: 5 -> 6; matrix products, arithmetic and copies ran while one was open for 0% -> 0% of each run, Pallas kernels for 6% -> 6%
where the time goes in v8:
time: 70 us; the launch traced here: 69.5 us
  starting transfers between devices  43.1 us (62%)
  waiting for transfers between devices  19.2 us (27%)
  Pallas kernels  6.97 us (10%)
    all_to_all x4, starting transfers between devices, exchange(): return lax.all_to_all(array, axes, split_axis=0, concat_axis=0, tiled=True)  29.8 us
    ppermute x3, starting transfers between devices, swap(): lax.ppermute(array, axis, [(i, i ^ j) for i in range(lax.axis_size(axis))])  13.2 us
    all_to_all x4, waiting for transfers between devices, exchange(): return lax.all_to_all(array, axes, split_axis=0, concat_axis=0, tiled=True)  10.7 us
    ppermute x3, waiting for transfers between devices, swap(): lax.ppermute(array, axis, [(i, i ^ j) for i in range(lax.axis_size(axis))])  8.55 us
    pallas_call x1, Pallas kernels, body(): pl.pallas_call(pack_kernel, in_specs=[SMEM, HBM, HBM], out_specs=[HBM] +...  1.79 us
    pallas_call x1, Pallas kernels, body(): pl.pallas_call(x_kernel, grid=(1,), in_specs=[whole, component(velocity.s...  1.64 us
  transfers between devices with their start and end apart: 7, of which 6 were waited for; matrix products, arithmetic and copies ran while one was open for 0% of the time, Pallas kernels for 6%

profile of v8, /device:TPU:1, one launch (start us, length us, event | category | flops | bytes accessed | tf_op | source)
XLA Modules:
  0.0 69.5 jit_solution(15621447478032845609)
XLA Ops:
  0.0 1.8 %pack.1 = (bf16[8,2,16,512]{3,2,1,0:T(8,128)(2,1)}, bf16[16,2,8,256]{3,2,1,0:T(8,128)(2,1)S(1)}, bf16[16,2,8,256]{3,2,1,0:T(8,128)(2,1)S(1)}) custom-call(s32[1]{0:T(128)} %bitcast.low_ref, f32[16,8,512]{2,1,0:T(8,128)} %bitcast.12, bf16[3,16,8,512]{3,2,1,0:T(8,128)(2,1)} %velocity_any.1), custom_call_target="tpu_custom_call" | custom-call | tf_op jit(solution)/shard_map/pack/pallas_call | solution.py:182
  1.8 10.9 %all-to-all-start = ((bf16[8,2,16,512]{3,2,1,0:T(8,128)(2,1)}), bf16[8,2,16,512]{3,2,1,0:T(8,128)(2,1)S(1)}, u32[]{:S(2)}, u32[]{:S(2)}) async-start(bf16[8,2,16,512]{3,2,1,0:T(8,128)(2,1)} %get-tuple-element.12), calls=%async_computation | async-start | bytes 524288 | tf_op jit(solution)/shard_map/all_to_all | solution.py:177
  12.7 4.2 %collective-permute-start = (bf16[16,2,8,256]{3,2,1,0:T(8,128)(2,1)S(1)}, bf16[16,2,8,256]{3,2,1,0:T(8,128)(2,1)S(1)}, u32[]{:S(2)}, u32[]{:S(2)}) collective-permute-start(bf16[16,2,8,256]{3,2,1,0:T(8,128)(2,1)S(1)} %get-tuple-element.14), channel_id=1, source_target_pairs={{0,4},{4,0},{1,5},{5,1},{2,6},{6,2},{3,7},{7,3},{8,12},{12,8},{9,1... | collective-permute-start | bytes 393224 | tf_op jit(solution)/shard_map/ppermute | solution.py:174
  16.9 5.8 %collective-permute-done.refs_1_ = bf16[16,2,8,256]{3,2,1,0:T(8,128)(2,1)S(1)} collective-permute-done((bf16[16,2,8,256]{3,2,1,0:T(8,128)(2,1)S(1)}, bf16[16,2,8,256]{3,2,1,0:T(8,128)(2,1)S(1)}, u32[]{:S(2)}, u32[]{:S(2)}) %collective-permute-start) | collective-permute-done | bytes 131104 | tf_op jit(solution)/shard_map/ppermute | solution.py:174
  22.7 0.7 %join.1 = bf16[16,2,2,8,256]{4,3,2,1,0:T(8,128)(2,1)} custom-call(bf16[16,2,8,256]{3,2,1,0:T(8,128)(2,1)S(1)} %get-tuple-element.13.refs_0_, bf16[16,2,8,256]{3,2,1,0:T(8,128)(2,1)S(1)} %collective-permute-done.refs_1_), custom_call_target="tpu_custom_call" | custom-call | tf_op jit(solution)/shard_map/join/pallas_call | solution.py:202
  23.4 0.0 all-to-all-done.r_ref
  23.5 0.0 copy-start.2
  23.5 0.0 copy-start.3
  23.5 0.0 copy-start.4
  23.5 0.0 copy-start.5
  23.5 7.5 %all-to-all-start.2 = ((bf16[16,2,2,8,256]{4,3,2,1,0:T(8,128)(2,1)}), bf16[16,2,2,8,256]{4,3,2,1,0:T(8,128)(2,1)S(1)}, u32[]{:S(2)}, u32[]{:S(2)}) async-start(bf16[16,2,2,8,256]{4,3,2,1,0:T(8,128)(2,1)} %join.1), calls=%async_computation.2 | async-start | bytes 524288 | tf_op jit(solution)/shard_map/all_to_all | solution.py:177
  31.1 6.5 %collective-permute-start.1 = (bf16[2,8,16,512]{3,2,1,0:T(8,128)(2,1)S(1)}, bf16[2,8,16,512]{3,2,1,0:T(8,128)(2,1)S(1)}, u32[]{:S(2)}, u32[]{:S(2)}) collective-permute-start(bf16[2,8,16,512]{3,2,1,0:T(8,128)(2,1)S(1)} %flux.1.own_ref), channel_id=1, source_target_pairs={{0,32},{32,0},{1,33},{33,1},{2,34},{34,2},{3,35},{35,3},{4,36},{36... | collective-permute-start | bytes 786440 | tf_op jit(solution)/shard_map/ppermute | solution.py:174
  37.6 0.0 copy-done.2
  37.6 0.0 copy-done.3
  37.6 0.0 copy-done.4
  37.6 0.0 copy-done.5
  37.7 0.6 all-to-all-done.2.r_ref
  38.2 1.0 %zmath.1 = bf16[16,2,8,256]{3,2,1,0:T(8,128)(2,1)} custom-call(s32[1]{0:T(128)} %bitcast.low_ref, bf16[16,2,2,8,256]{4,3,2,1,0:T(8,128)(2,1)S(1)} %all-to-all-done.2.r_ref, bf16[2,256,256]{2,1,0:T(8,128)(2,1)S(1)} %get-tuple-element.18.operators_ref), custom_call_target="tpu_custom_call" | custom-call | tf_op jit(solution)/shard_map/zmath/pallas_call | solution.py:238
  39.2 5.5 %all-to-all-start.3 = ((bf16[16,2,8,256]{3,2,1,0:T(8,128)(2,1)}), bf16[16,2,8,256]{3,2,1,0:T(8,128)(2,1)S(1)}, u32[]{:S(2)}, u32[]{:S(2)}) async-start(bf16[16,2,8,256]{3,2,1,0:T(8,128)(2,1)} %zmath.1), calls=%async_computation.3 | async-start | bytes 262144 | tf_op jit(solution)/shard_map/all_to_all | solution.py:177
  44.7 2.6 %collective-permute-done.1.other_ref = bf16[2,8,16,512]{3,2,1,0:T(8,128)(2,1)S(1)} collective-permute-done((bf16[2,8,16,512]{3,2,1,0:T(8,128)(2,1)S(1)}, bf16[2,8,16,512]{3,2,1,0:T(8,128)(2,1)S(1)}, u32[]{:S(2)}, u32[]{:S(2)}) %collective-permute-start.1) | collective-permute-done | bytes 262176 | tf_op jit(solution)/shard_map/ppermute | solution.py:174
  47.2 0.0 copy-start
  47.2 0.0 copy-start.1
  47.2 1.0 %ymath.1 = bf16[8,16,512]{2,1,0:T(8,128)(2,1)} custom-call(s32[1]{0:T(128)} %bitcast.2.high_ref, bf16[8,2,16,512]{3,2,1,0:T(8,128)(2,1)S(1)} %all-to-all-done.r_ref, bf16[2,8,16,512]{3,2,1,0:T(8,128)(2,1)S(1)} %flux.1.own_ref, bf16[2,8,16,512]{3,2,1,0:T(8,128)(2,1)S(1)} %collective-permute-done.1.other_ref, ...), custom_call_target="tpu_custom_call" | custom-call | tf_op jit(solution)/shard_map/ymath/pallas_call | solution.py:250
  48.2 6.5 %all-to-all-done.3.own_ref = bf16[16,2,8,256]{3,2,1,0:T(8,128)(2,1)S(1)} async-done(((bf16[16,2,8,256]{3,2,1,0:T(8,128)(2,1)}), bf16[16,2,8,256]{3,2,1,0:T(8,128)(2,1)S(1)}, u32[]{:S(2)}, u32[]{:S(2)}) %all-to-all-start.3) | async-done | bytes 131104 | tf_op jit(solution)/shard_map/all_to_all | solution.py:177
  54.7 6.0 %all-to-all-start.1 = ((bf16[8,16,512]{2,1,0:T(8,128)(2,1)}), bf16[8,16,512]{2,1,0:T(8,128)(2,1)S(1)}, u32[]{:S(2)}, u32[]{:S(2)}) async-start(bf16[8,16,512]{2,1,0:T(8,128)(2,1)} %ymath.1), calls=%async_computation.1 | async-start | bytes 262144 | tf_op jit(solution)/shard_map/all_to_all | solution.py:177
  60.7 2.5 %collective-permute-start.2 = (bf16[16,8,256]{2,1,0:T(8,128)(2,1)S(1)}, bf16[16,8,256]{2,1,0:T(8,128)(2,1)S(1)}, u32[]{:S(2)}, u32[]{:S(2)}) collective-permute-start(bf16[16,8,256]{2,1,0:T(8,128)(2,1)S(1)} %slice_bitcast_fusion), channel_id=1, source_target_pairs={{0,4},{4,0},{1,5},{5,1},{2,6},{6,2},{3,7},{7,3},{8,12},{12,8},{9,1... | collective-permute-start | bytes 196616 | tf_op jit(solution)/shard_map/ppermute | solution.py:174
  63.2 0.0 copy-done
  63.2 0.0 copy-done.1
  63.2 1.6 %xmath.1.base_ref = f32[16,8,512]{2,1,0:T(8,128)S(1)} custom-call(f32[16,8,512]{2,1,0:T(8,128)} %bitcast.13, bf16[3,16,8,512]{3,2,1,0:T(8,128)(2,1)} %velocity_any.1, bf16[512,512]{1,0:T(8,128)(2,1)S(1)} %copy-done, bf16[512,512]{1,0:T(8,128)(2,1)S(1)} %copy-done.1), custom_call_target="tpu_custom_call" | custom-call | tf_op jit(solution)/shard_map/xmath/pallas_call | solution.py:220
  64.9 3.6 %all-to-all-done.1.y_ref = bf16[8,16,512]{2,1,0:T(8,128)(2,1)S(1)} async-done(((bf16[8,16,512]{2,1,0:T(8,128)(2,1)}), bf16[8,16,512]{2,1,0:T(8,128)(2,1)S(1)}, u32[]{:S(2)}, u32[]{:S(2)}) %all-to-all-start.1) | async-done | bytes 131104 | tf_op jit(solution)/shard_map/all_to_all | solution.py:177
  68.4 0.2 collective-permute-done.2.rest_0_
  68.7 0.8 %last.1 = f32[16,8,512]{2,1,0:T(8,128)} custom-call(s32[1]{0:T(128)} %bitcast.low_ref, f32[16,8,512]{2,1,0:T(8,128)S(1)} %xmath.1.base_ref, bf16[8,16,512]{2,1,0:T(8,128)(2,1)S(1)} %all-to-all-done.1.y_ref, bf16[16,2,8,256]{3,2,1,0:T(8,128)(2,1)S(1)} %all-to-all-done.3.own_ref, bf16[16,8,256]{2,1,0:T(8,128)(2,1)S(1)} %collective-permute-done.2.rest_0_), custom_call_target="tpu_custom_call" | custom-call | tf_op jit(solution)/shard_map/last/pallas_call | solution.py:262
  (3 shorter events, 0.1 us)
Async XLA Ops:
  1.8 21.6 %all-to-all-start = ((bf16[8,2,16,512]{3,2,1,0:T(8,128)(2,1)}), bf16[8,2,16,512]{3,2,1,0:T(8,128)(2,1)S(1)}, u32[]{:S(2)}, u32[]{:S(2)}) async-start(bf16[8,2,16,512]{3,2,1,0:T(8,128)(2,1)} %get-tuple-element.12), calls=%async_computation | async-start | bytes 524288 | tf_op jit(solution)/shard_map/all_to_all | solution.py:177
  12.7 10.0 %collective-permute-start = (bf16[16,2,8,256]{3,2,1,0:T(8,128)(2,1)S(1)}, bf16[16,2,8,256]{3,2,1,0:T(8,128)(2,1)S(1)}, u32[]{:S(2)}, u32[]{:S(2)}) collective-permute-start(bf16[16,2,8,256]{3,2,1,0:T(8,128)(2,1)S(1)} %get-tuple-element.14), channel_id=1, source_target_pairs={{0,4},{4,0},{1,5},{5,1},{2,6},{6,2},{3,7},{7,3},{8,12},{12,8},{9,1... | collective-permute-start | bytes 393224 | tf_op jit(solution)/shard_map/ppermute | solution.py:174
  23.5 14.1 %copy-start.2 = (bf16[256,256]{1,0:T(8,128)(2,1)S(1)}, bf16[256,256]{1,0:T(8,128)(2,1)}, u32[]{:S(2)}) copy-start(bf16[256,256]{1,0:T(8,128)(2,1)} %param.12) | copy-start | bytes 393220
  23.5 14.1 %copy-start.3 = (bf16[256,256]{1,0:T(8,128)(2,1)S(1)}, bf16[256,256]{1,0:T(8,128)(2,1)}, u32[]{:S(2)}) copy-start(bf16[256,256]{1,0:T(8,128)(2,1)} %param.13) | copy-start | bytes 393220
  23.5 14.1 %copy-start.4 = (bf16[256,256]{1,0:T(8,128)(2,1)S(1)}, bf16[256,256]{1,0:T(8,128)(2,1)}, u32[]{:S(2)}) copy-start(bf16[256,256]{1,0:T(8,128)(2,1)} %first_z_ref.1) | copy-start | bytes 393220
  23.5 14.1 %copy-start.5 = (bf16[256,256]{1,0:T(8,128)(2,1)S(1)}, bf16[256,256]{1,0:T(8,128)(2,1)}, u32[]{:S(2)}) copy-start(bf16[256,256]{1,0:T(8,128)(2,1)} %second_z_ref.1) | copy-start | bytes 393220
  23.5 14.7 %all-to-all-start.2 = ((bf16[16,2,2,8,256]{4,3,2,1,0:T(8,128)(2,1)}), bf16[16,2,2,8,256]{4,3,2,1,0:T(8,128)(2,1)S(1)}, u32[]{:S(2)}, u32[]{:S(2)}) async-start(bf16[16,2,2,8,256]{4,3,2,1,0:T(8,128)(2,1)} %join.1), calls=%async_computation.2 | async-start | bytes 524288 | tf_op jit(solution)/shard_map/all_to_all | solution.py:177
  31.1 16.2 %collective-permute-start.1 = (bf16[2,8,16,512]{3,2,1,0:T(8,128)(2,1)S(1)}, bf16[2,8,16,512]{3,2,1,0:T(8,128)(2,1)S(1)}, u32[]{:S(2)}, u32[]{:S(2)}) collective-permute-start(bf16[2,8,16,512]{3,2,1,0:T(8,128)(2,1)S(1)} %flux.1.own_ref), channel_id=1, source_target_pairs={{0,32},{32,0},{1,33},{33,1},{2,34},{34,2},{3,35},{35,3},{4,36},{36... | collective-permute-start | bytes 786440 | tf_op jit(solution)/shard_map/ppermute | solution.py:174
  39.2 15.5 %all-to-all-start.3 = ((bf16[16,2,8,256]{3,2,1,0:T(8,128)(2,1)}), bf16[16,2,8,256]{3,2,1,0:T(8,128)(2,1)S(1)}, u32[]{:S(2)}, u32[]{:S(2)}) async-start(bf16[16,2,8,256]{3,2,1,0:T(8,128)(2,1)} %zmath.1), calls=%async_computation.3 | async-start | bytes 262144 | tf_op jit(solution)/shard_map/all_to_all | solution.py:177
  47.2 16.0 %copy-start = (bf16[512,512]{1,0:T(8,128)(2,1)S(1)}, bf16[512,512]{1,0:T(8,128)(2,1)}, u32[]{:S(2)}) copy-start(bf16[512,512]{1,0:T(8,128)(2,1)} %first_ref.1) | copy-start | bytes 1572868
  47.2 16.0 %copy-start.1 = (bf16[512,512]{1,0:T(8,128)(2,1)S(1)}, bf16[512,512]{1,0:T(8,128)(2,1)}, u32[]{:S(2)}) copy-start(bf16[512,512]{1,0:T(8,128)(2,1)} %second_ref.1) | copy-start | bytes 1572868
  54.7 13.7 %all-to-all-start.1 = ((bf16[8,16,512]{2,1,0:T(8,128)(2,1)}), bf16[8,16,512]{2,1,0:T(8,128)(2,1)S(1)}, u32[]{:S(2)}, u32[]{:S(2)}) async-start(bf16[8,16,512]{2,1,0:T(8,128)(2,1)} %ymath.1), calls=%async_computation.1 | async-start | bytes 262144 | tf_op jit(solution)/shard_map/all_to_all | solution.py:177
  60.7 8.0 %collective-permute-start.2 = (bf16[16,8,256]{2,1,0:T(8,128)(2,1)S(1)}, bf16[16,8,256]{2,1,0:T(8,128)(2,1)S(1)}, u32[]{:S(2)}, u32[]{:S(2)}) collective-permute-start(bf16[16,8,256]{2,1,0:T(8,128)(2,1)S(1)} %slice_bitcast_fusion), channel_id=1, source_target_pairs={{0,4},{4,0},{1,5},{5,1},{2,6},{6,2},{3,7},{7,3},{8,12},{12,8},{9,1... | collective-permute-start | bytes 196616 | tf_op jit(solution)/shard_map/ppermute | solution.py:174

commit v9 on v8

--- a/solution.py
+++ b/solution.py
@@ -105,19 +105,27 @@
     z_ref[1] = second_z_ref[...]
 
 
-def y_kernel(high_ref, r_ref, own_ref, other_ref, rows_ref, out_ref, lines):
-    _, blocks, depth, lanes = own_ref.shape
+def y_kernel(high_ref, r_ref, own_ref, other_ref, rows_ref, out_any, lines, out_ref, sems):
+    _, blocks, depth, width = own_ref.shape
     high = high_ref[0]
     length = 2 * blocks * depth
-    lines[:, :, high] = own_ref[...]
-    lines[:, :, 1 - high] = other_ref[...]
-    s = lines[0].reshape(length, lanes)
-    flux = lines[1].reshape(length, lanes)
     first = rows_ref[0].reshape(blocks * depth, length)
     second = rows_ref[1].reshape(blocks * depth, length)
-    c = r_ref[:, 1].reshape(blocks * depth, lanes).astype(F32)
-    term = -0.5 * (c * dot(first, s, 0) + dot(first, flux, 0)) + 0.5 * dot(second, s, 0)
-    out_ref[...] = term.astype(BF16).reshape(blocks, depth, lanes)
+    half = width // 2
+    copies = []
+    for part in range(2):
+        lanes = slice(part * half, (part + 1) * half)
+        lines[:, :, high] = own_ref[:, :, :, lanes]
+        lines[:, :, 1 - high] = other_ref[:, :, :, lanes]
+        s = lines[0].reshape(length, half)
+        flux = lines[1].reshape(length, half)
+        c = r_ref[:, 1, :, lanes].reshape(blocks * depth, half).astype(F32)
+        term = -0.5 * (c * dot(first, s, 0) + dot(first, flux, 0)) + 0.5 * dot(second, s, 0)
+        out_ref[:, :, lanes] = term.astype(BF16).reshape(blocks, depth, half)
+        copies.append(pltpu.make_async_copy(out_ref.at[:, :, lanes], out_any.at[:, :, lanes], sems.at[part]))
+        copies[part].start()
+    for copy in copies:
+        copy.wait()
 
 
 def z_kernel(low_ref, r_ref, operators_ref, out_ref, lines, terms):
@@ -250,9 +258,13 @@
     y_term = pl.pallas_call(
         y_kernel,
         in_specs=[SMEM] + [VMEM] * 4,
-        out_specs=VMEM,
-        out_shape=pltpu.VMEM((blocks, ny, nx), BF16),
-        scratch_shapes=[pltpu.VMEM((2, blocks, 2, ny, nx), BF16)],
+        out_specs=HBM,
+        out_shape=pltpu.HBM((blocks, ny, nx), BF16),
+        scratch_shapes=[
+            pltpu.VMEM((2, blocks, 2, ny, half), BF16),
+            pltpu.VMEM((blocks, ny, nx), BF16),
+            pltpu.SemaphoreType.DMA((2,)),
+        ],
         name="ymath",
     )(high, row_in, near(own), near(other), near(rows))
     y_back = exchange(y_term, "z")

time: 70 us -> 70 us (level)
  no operation moved by 1% of the time
where the time goes in v9:
time: 70 us; the launch traced here: 69.5 us
  starting transfers between devices  43.1 us (62%)
  waiting for transfers between devices  19.2 us (27%)
  Pallas kernels  6.96 us (10%)
    all_to_all x4, starting transfers between devices, exchange(): return lax.all_to_all(array, axes, split_axis=0, concat_axis=0, tiled=True)  29.8 us
    ppermute x3, starting transfers between devices, swap(): lax.ppermute(array, axis, [(i, i ^ j) for i in range(lax.axis_size(axis))])  13.2 us
    all_to_all x4, waiting for transfers between devices, exchange(): return lax.all_to_all(array, axes, split_axis=0, concat_axis=0, tiled=True)  10.7 us
    ppermute x3, waiting for transfers between devices, swap(): lax.ppermute(array, axis, [(i, i ^ j) for i in range(lax.axis_size(axis))])  8.55 us
    pallas_call x1, Pallas kernels, body(): pl.pallas_call(pack_kernel, in_specs=[SMEM, HBM, HBM], out_specs=[HBM] +...  1.79 us
    pallas_call x1, Pallas kernels, body(): pl.pallas_call(x_kernel, grid=(1,), in_specs=[whole, component(velocity.s...  1.64 us
  transfers between devices with their start and end apart: 7, of which 6 were waited for; matrix products, arithmetic and copies ran while one was open for 0% of the time, Pallas kernels for 6%

profile of v9, /device:TPU:1, one launch (start us, length us, event | category | flops | bytes accessed | tf_op | source)
XLA Modules:
  0.0 69.5 jit_solution(8116714765615924746)
XLA Ops:
  0.0 1.8 %pack.1 = (bf16[8,2,16,512]{3,2,1,0:T(8,128)(2,1)}, bf16[16,2,8,256]{3,2,1,0:T(8,128)(2,1)S(1)}, bf16[16,2,8,256]{3,2,1,0:T(8,128)(2,1)S(1)}) custom-call(s32[1]{0:T(128)} %bitcast.low_ref, f32[16,8,512]{2,1,0:T(8,128)} %bitcast.12, bf16[3,16,8,512]{3,2,1,0:T(8,128)(2,1)} %velocity_any.1), custom_call_target="tpu_custom_call" | custom-call | tf_op jit(solution)/shard_map/pack/pallas_call | solution.py:190
  1.8 10.9 %all-to-all-start = ((bf16[8,2,16,512]{3,2,1,0:T(8,128)(2,1)}), bf16[8,2,16,512]{3,2,1,0:T(8,128)(2,1)S(1)}, u32[]{:S(2)}, u32[]{:S(2)}) async-start(bf16[8,2,16,512]{3,2,1,0:T(8,128)(2,1)} %get-tuple-element.12), calls=%async_computation | async-start | bytes 524288 | tf_op jit(solution)/shard_map/all_to_all | solution.py:185
  12.7 4.2 %collective-permute-start = (bf16[16,2,8,256]{3,2,1,0:T(8,128)(2,1)S(1)}, bf16[16,2,8,256]{3,2,1,0:T(8,128)(2,1)S(1)}, u32[]{:S(2)}, u32[]{:S(2)}) collective-permute-start(bf16[16,2,8,256]{3,2,1,0:T(8,128)(2,1)S(1)} %get-tuple-element.14), channel_id=1, source_target_pairs={{0,4},{4,0},{1,5},{5,1},{2,6},{6,2},{3,7},{7,3},{8,12},{12,8},{9,1... | collective-permute-start | bytes 393224 | tf_op jit(solution)/shard_map/ppermute | solution.py:182
  16.9 5.8 %collective-permute-done.refs_1_ = bf16[16,2,8,256]{3,2,1,0:T(8,128)(2,1)S(1)} collective-permute-done((bf16[16,2,8,256]{3,2,1,0:T(8,128)(2,1)S(1)}, bf16[16,2,8,256]{3,2,1,0:T(8,128)(2,1)S(1)}, u32[]{:S(2)}, u32[]{:S(2)}) %collective-permute-start) | collective-permute-done | bytes 131104 | tf_op jit(solution)/shard_map/ppermute | solution.py:182
  22.7 0.7 %join.1 = bf16[16,2,2,8,256]{4,3,2,1,0:T(8,128)(2,1)} custom-call(bf16[16,2,8,256]{3,2,1,0:T(8,128)(2,1)S(1)} %get-tuple-element.13.refs_0_, bf16[16,2,8,256]{3,2,1,0:T(8,128)(2,1)S(1)} %collective-permute-done.refs_1_), custom_call_target="tpu_custom_call" | custom-call | tf_op jit(solution)/shard_map/join/pallas_call | solution.py:210
  23.4 0.0 all-to-all-done.r_ref
  23.5 0.0 copy-start.2
  23.5 0.0 copy-start.3
  23.5 0.0 copy-start.4
  23.5 0.0 copy-start.5
  23.5 7.5 %all-to-all-start.2 = ((bf16[16,2,2,8,256]{4,3,2,1,0:T(8,128)(2,1)}), bf16[16,2,2,8,256]{4,3,2,1,0:T(8,128)(2,1)S(1)}, u32[]{:S(2)}, u32[]{:S(2)}) async-start(bf16[16,2,2,8,256]{4,3,2,1,0:T(8,128)(2,1)} %join.1), calls=%async_computation.2 | async-start | bytes 524288 | tf_op jit(solution)/shard_map/all_to_all | solution.py:185
  31.1 6.5 %collective-permute-start.1 = (bf16[2,8,16,512]{3,2,1,0:T(8,128)(2,1)S(1)}, bf16[2,8,16,512]{3,2,1,0:T(8,128)(2,1)S(1)}, u32[]{:S(2)}, u32[]{:S(2)}) collective-permute-start(bf16[2,8,16,512]{3,2,1,0:T(8,128)(2,1)S(1)} %flux.1.own_ref), channel_id=1, source_target_pairs={{0,32},{32,0},{1,33},{33,1},{2,34},{34,2},{3,35},{35,3},{4,36},{36... | collective-permute-start | bytes 786440 | tf_op jit(solution)/shard_map/ppermute | solution.py:182
  37.6 0.0 copy-done.2
  37.6 0.0 copy-done.3
  37.6 0.0 copy-done.4
  37.6 0.0 copy-done.5
  37.7 0.6 all-to-all-done.2.r_ref
  38.2 1.0 %zmath.1 = bf16[16,2,8,256]{3,2,1,0:T(8,128)(2,1)} custom-call(s32[1]{0:T(128)} %bitcast.low_ref, bf16[16,2,2,8,256]{4,3,2,1,0:T(8,128)(2,1)S(1)} %all-to-all-done.2.r_ref, bf16[2,256,256]{2,1,0:T(8,128)(2,1)S(1)} %get-tuple-element.18.operators_ref), custom_call_target="tpu_custom_call" | custom-call | tf_op jit(solution)/shard_map/zmath/pallas_call | solution.py:246
  39.2 5.5 %all-to-all-start.3 = ((bf16[16,2,8,256]{3,2,1,0:T(8,128)(2,1)}), bf16[16,2,8,256]{3,2,1,0:T(8,128)(2,1)S(1)}, u32[]{:S(2)}, u32[]{:S(2)}) async-start(bf16[16,2,8,256]{3,2,1,0:T(8,128)(2,1)} %zmath.1), calls=%async_computation.3 | async-start | bytes 262144 | tf_op jit(solution)/shard_map/all_to_all | solution.py:185
  44.7 2.6 %collective-permute-done.1.other_ref = bf16[2,8,16,512]{3,2,1,0:T(8,128)(2,1)S(1)} collective-permute-done((bf16[2,8,16,512]{3,2,1,0:T(8,128)(2,1)S(1)}, bf16[2,8,16,512]{3,2,1,0:T(8,128)(2,1)S(1)}, u32[]{:S(2)}, u32[]{:S(2)}) %collective-permute-start.1) | collective-permute-done | bytes 262176 | tf_op jit(solution)/shard_map/ppermute | solution.py:182
  47.2 0.0 copy-start
  47.2 0.0 copy-start.1
  47.2 1.0 %ymath.1 = bf16[8,16,512]{2,1,0:T(8,128)(2,1)} custom-call(s32[1]{0:T(128)} %bitcast.2.high_ref, bf16[8,2,16,512]{3,2,1,0:T(8,128)(2,1)S(1)} %all-to-all-done.r_ref, bf16[2,8,16,512]{3,2,1,0:T(8,128)(2,1)S(1)} %flux.1.own_ref, bf16[2,8,16,512]{3,2,1,0:T(8,128)(2,1)S(1)} %collective-permute-done.1.other_ref, ...), custom_call_target="tpu_custom_call" | custom-call | tf_op jit(solution)/shard_map/ymath/pallas_call | solution.py:258
  48.2 6.5 %all-to-all-done.3.own_ref = bf16[16,2,8,256]{3,2,1,0:T(8,128)(2,1)S(1)} async-done(((bf16[16,2,8,256]{3,2,1,0:T(8,128)(2,1)}), bf16[16,2,8,256]{3,2,1,0:T(8,128)(2,1)S(1)}, u32[]{:S(2)}, u32[]{:S(2)}) %all-to-all-start.3) | async-done | bytes 131104 | tf_op jit(solution)/shard_map/all_to_all | solution.py:185
  54.7 6.0 %all-to-all-start.1 = ((bf16[8,16,512]{2,1,0:T(8,128)(2,1)}), bf16[8,16,512]{2,1,0:T(8,128)(2,1)S(1)}, u32[]{:S(2)}, u32[]{:S(2)}) async-start(bf16[8,16,512]{2,1,0:T(8,128)(2,1)} %ymath.1), calls=%async_computation.1 | async-start | bytes 262144 | tf_op jit(solution)/shard_map/all_to_all | solution.py:185
  60.7 2.5 %collective-permute-start.2 = (bf16[16,8,256]{2,1,0:T(8,128)(2,1)S(1)}, bf16[16,8,256]{2,1,0:T(8,128)(2,1)S(1)}, u32[]{:S(2)}, u32[]{:S(2)}) collective-permute-start(bf16[16,8,256]{2,1,0:T(8,128)(2,1)S(1)} %slice_bitcast_fusion), channel_id=1, source_target_pairs={{0,4},{4,0},{1,5},{5,1},{2,6},{6,2},{3,7},{7,3},{8,12},{12,8},{9,1... | collective-permute-start | bytes 196616 | tf_op jit(solution)/shard_map/ppermute | solution.py:182
  63.2 0.0 copy-done
  63.2 0.0 copy-done.1
  63.2 1.6 %xmath.1.base_ref = f32[16,8,512]{2,1,0:T(8,128)S(1)} custom-call(f32[16,8,512]{2,1,0:T(8,128)} %bitcast.13, bf16[3,16,8,512]{3,2,1,0:T(8,128)(2,1)} %velocity_any.1, bf16[512,512]{1,0:T(8,128)(2,1)S(1)} %copy-done, bf16[512,512]{1,0:T(8,128)(2,1)S(1)} %copy-done.1), custom_call_target="tpu_custom_call" | custom-call | tf_op jit(solution)/shard_map/xmath/pallas_call | solution.py:228
  64.9 3.6 %all-to-all-done.1.y_ref = bf16[8,16,512]{2,1,0:T(8,128)(2,1)S(1)} async-done(((bf16[8,16,512]{2,1,0:T(8,128)(2,1)}), bf16[8,16,512]{2,1,0:T(8,128)(2,1)S(1)}, u32[]{:S(2)}, u32[]{:S(2)}) %all-to-all-start.1) | async-done | bytes 131104 | tf_op jit(solution)/shard_map/all_to_all | solution.py:185
  68.4 0.2 collective-permute-done.2.rest_0_
  68.7 0.8 %last.1 = f32[16,8,512]{2,1,0:T(8,128)} custom-call(s32[1]{0:T(128)} %bitcast.low_ref, f32[16,8,512]{2,1,0:T(8,128)S(1)} %xmath.1.base_ref, bf16[8,16,512]{2,1,0:T(8,128)(2,1)S(1)} %all-to-all-done.1.y_ref, bf16[16,2,8,256]{3,2,1,0:T(8,128)(2,1)S(1)} %all-to-all-done.3.own_ref, bf16[16,8,256]{2,1,0:T(8,128)(2,1)S(1)} %collective-permute-done.2.rest_0_), custom_call_target="tpu_custom_call" | custom-call | tf_op jit(solution)/shard_map/last/pallas_call | solution.py:274
  (3 shorter events, 0.1 us)
Async XLA Ops:
  1.8 21.6 %all-to-all-start = ((bf16[8,2,16,512]{3,2,1,0:T(8,128)(2,1)}), bf16[8,2,16,512]{3,2,1,0:T(8,128)(2,1)S(1)}, u32[]{:S(2)}, u32[]{:S(2)}) async-start(bf16[8,2,16,512]{3,2,1,0:T(8,128)(2,1)} %get-tuple-element.12), calls=%async_computation | async-start | bytes 524288 | tf_op jit(solution)/shard_map/all_to_all | solution.py:185
  12.7 10.0 %collective-permute-start = (bf16[16,2,8,256]{3,2,1,0:T(8,128)(2,1)S(1)}, bf16[16,2,8,256]{3,2,1,0:T(8,128)(2,1)S(1)}, u32[]{:S(2)}, u32[]{:S(2)}) collective-permute-start(bf16[16,2,8,256]{3,2,1,0:T(8,128)(2,1)S(1)} %get-tuple-element.14), channel_id=1, source_target_pairs={{0,4},{4,0},{1,5},{5,1},{2,6},{6,2},{3,7},{7,3},{8,12},{12,8},{9,1... | collective-permute-start | bytes 393224 | tf_op jit(solution)/shard_map/ppermute | solution.py:182
  23.5 14.1 %copy-start.2 = (bf16[256,256]{1,0:T(8,128)(2,1)S(1)}, bf16[256,256]{1,0:T(8,128)(2,1)}, u32[]{:S(2)}) copy-start(bf16[256,256]{1,0:T(8,128)(2,1)} %param.12) | copy-start | bytes 393220
  23.5 14.1 %copy-start.3 = (bf16[256,256]{1,0:T(8,128)(2,1)S(1)}, bf16[256,256]{1,0:T(8,128)(2,1)}, u32[]{:S(2)}) copy-start(bf16[256,256]{1,0:T(8,128)(2,1)} %param.13) | copy-start | bytes 393220
  23.5 14.1 %copy-start.4 = (bf16[256,256]{1,0:T(8,128)(2,1)S(1)}, bf16[256,256]{1,0:T(8,128)(2,1)}, u32[]{:S(2)}) copy-start(bf16[256,256]{1,0:T(8,128)(2,1)} %first_z_ref.1) | copy-start | bytes 393220
  23.5 14.1 %copy-start.5 = (bf16[256,256]{1,0:T(8,128)(2,1)S(1)}, bf16[256,256]{1,0:T(8,128)(2,1)}, u32[]{:S(2)}) copy-start(bf16[256,256]{1,0:T(8,128)(2,1)} %second_z_ref.1) | copy-start | bytes 393220
  23.5 14.7 %all-to-all-start.2 = ((bf16[16,2,2,8,256]{4,3,2,1,0:T(8,128)(2,1)}), bf16[16,2,2,8,256]{4,3,2,1,0:T(8,128)(2,1)S(1)}, u32[]{:S(2)}, u32[]{:S(2)}) async-start(bf16[16,2,2,8,256]{4,3,2,1,0:T(8,128)(2,1)} %join.1), calls=%async_computation.2 | async-start | bytes 524288 | tf_op jit(solution)/shard_map/all_to_all | solution.py:185
  31.1 16.2 %collective-permute-start.1 = (bf16[2,8,16,512]{3,2,1,0:T(8,128)(2,1)S(1)}, bf16[2,8,16,512]{3,2,1,0:T(8,128)(2,1)S(1)}, u32[]{:S(2)}, u32[]{:S(2)}) collective-permute-start(bf16[2,8,16,512]{3,2,1,0:T(8,128)(2,1)S(1)} %flux.1.own_ref), channel_id=1, source_target_pairs={{0,32},{32,0},{1,33},{33,1},{2,34},{34,2},{3,35},{35,3},{4,36},{36... | collective-permute-start | bytes 786440 | tf_op jit(solution)/shard_map/ppermute | solution.py:182
  39.2 15.5 %all-to-all-start.3 = ((bf16[16,2,8,256]{3,2,1,0:T(8,128)(2,1)}), bf16[16,2,8,256]{3,2,1,0:T(8,128)(2,1)S(1)}, u32[]{:S(2)}, u32[]{:S(2)}) async-start(bf16[16,2,8,256]{3,2,1,0:T(8,128)(2,1)} %zmath.1), calls=%async_computation.3 | async-start | bytes 262144 | tf_op jit(solution)/shard_map/all_to_all | solution.py:185
  47.2 16.0 %copy-start = (bf16[512,512]{1,0:T(8,128)(2,1)S(1)}, bf16[512,512]{1,0:T(8,128)(2,1)}, u32[]{:S(2)}) copy-start(bf16[512,512]{1,0:T(8,128)(2,1)} %first_ref.1) | copy-start | bytes 1572868
  47.2 16.0 %copy-start.1 = (bf16[512,512]{1,0:T(8,128)(2,1)S(1)}, bf16[512,512]{1,0:T(8,128)(2,1)}, u32[]{:S(2)}) copy-start(bf16[512,512]{1,0:T(8,128)(2,1)} %second_ref.1) | copy-start | bytes 1572868
  54.7 13.7 %all-to-all-start.1 = ((bf16[8,16,512]{2,1,0:T(8,128)(2,1)}), bf16[8,16,512]{2,1,0:T(8,128)(2,1)S(1)}, u32[]{:S(2)}, u32[]{:S(2)}) async-start(bf16[8,16,512]{2,1,0:T(8,128)(2,1)} %ymath.1), calls=%async_computation.1 | async-start | bytes 262144 | tf_op jit(solution)/shard_map/all_to_all | solution.py:185
  60.7 8.0 %collective-permute-start.2 = (bf16[16,8,256]{2,1,0:T(8,128)(2,1)S(1)}, bf16[16,8,256]{2,1,0:T(8,128)(2,1)S(1)}, u32[]{:S(2)}, u32[]{:S(2)}) collective-permute-start(bf16[16,8,256]{2,1,0:T(8,128)(2,1)S(1)} %slice_bitcast_fusion), channel_id=1, source_target_pairs={{0,4},{4,0},{1,5},{5,1},{2,6},{6,2},{3,7},{7,3},{8,12},{12,8},{9,1... | collective-permute-start | bytes 196616 | tf_op jit(solution)/shard_map/ppermute | solution.py:182
